TPU v7x, 32 devices: a whole 2x2x4 slice. The times are simulated.
32 devices in a mesh: dp: 8 (over z, x), mp: 4 (over y, core).
Axes of the slice: x: 2, y: 2, z: 4, core: 2. Of those that a mesh axis runs over, the one named last changes fastest.
Arguments:
- patches: bfloat16 [8192, 1280], P('dp', 'mp'), may hold values from -6 to 6
- cotangent: bfloat16 [8192, 1280], P('dp', 'mp'), may hold values from -0.29882812 to 0.29882812
- encoder_rank: int32 [64], P('dp'), may hold values from 0 to 7, as said below
- block_fill: int32 [64], P('dp'), may hold values from 32 to 128
- w_up: bfloat16 [1280, 5120], P(None, 'mp'), may hold values from -0.15625 to 0.15625
- w_down: bfloat16 [5120, 1280], P('mp'), may hold values from -0.078125 to 0.078125
- q_up: float32 [5120, 64], P('mp'), may hold values from -6 to 6
- q_down: float32 [1280, 64], replicated, may hold values from -6 to 6
Outputs:
- encoded: bfloat16 [14336, 1280], P('dp', 'mp')
- approx_up: float32 [1280, 5120], P(None, 'mp')
- approx_down: float32 [5120, 1280], P('mp')
- qnew_up: float32 [5120, 64], P('mp')
- qnew_down: float32 [1280, 64], replicated
Inputs may be any that keep to these rules, and one draw needn't show every extreme that they name: `encoder_rank`: from the blocks of one data rank at most 2 go to one encoder rank, and one encoder rank receives at most 14 blocks in all; both bounds are reached in every draw. Every encoder rank receives some block.
All inputs are finite; a program needn't handle non-finite values.
Results may differ from a plain program's by a relative error of at most 0.015.
Values may be sent and summed in bfloat16 or wider, within the bound.
No kernel may reach another device: no remote copies, remote signals or barrier semaphores. Data moves between devices by JAX's collectives and lax.ppermute only.
A program may use at most 128 MiB of HBM per device.

v0:
```python
import functools

import jax
import jax.numpy as jnp
from jax import lax
from jax.experimental import pallas as pl
from jax.experimental.pallas import tpu as pltpu
from jax.sharding import PartitionSpec as P

BLOCK = 128
CAP = 2
EXTRA = 6
bf16 = jnp.bfloat16
f32 = jnp.float32


def bits_of(count):
    return [1 << b for b in range(count.bit_length() - 1)]


def swap(x, axis, bit):
    count = lax.axis_size(axis)
    return lax.ppermute(x, axis, [(i, i ^ bit) for i in range(count)])


def gather_xor(own):
    count = lax.axis_size("mp")
    even = {0: own}
    for bit in bits_of(count)[1:]:
        even.update({o | bit: swap(p, "mp", bit) for o, p in even.items()})
    pieces = dict(even)
    pieces.update({o | 1: swap(p, "mp", 1) for o, p in even.items()})
    return [pieces[o] for o in range(count)]


def reorder(pieces, me):
    for bit in bits_of(len(pieces)):
        flip = (me & bit) != 0
        pieces = [jnp.where(flip, pieces[i ^ bit], pieces[i]) for i in range(len(pieces))]
    return pieces


def slices(x, count, axis):
    size = x.shape[axis] // count
    return [lax.slice_in_dim(x, i * size, (i + 1) * size, axis=axis) for i in range(count)]


def reduce_mp(pieces, send_type):
    pieces = dict(enumerate(pieces))
    for bit in bits_of(len(pieces)):
        out = [o for o in pieces if o & bit]
        sent = swap(jnp.concatenate([pieces[o].astype(send_type) for o in out], axis=1), "mp", bit)
        got = slices(sent, len(out), 1)
        pieces = {o ^ bit: pieces[o ^ bit] + g.astype(f32) for o, g in zip(out, got)}
    return pieces[0]


def spread_mp(own):
    have = own
    offsets = [0]
    for bit in reversed(bits_of(lax.axis_size("mp"))):
        got = swap(have, "mp", bit)
        have = jnp.concatenate([have, got], axis=1)
        offsets = offsets + [o | bit for o in offsets]
    parts = slices(have, len(offsets), 1)
    return [parts[offsets.index(o)] for o in range(len(offsets))]


def sum_over(x, axis, send_type):
    for bit in bits_of(lax.axis_size(axis)):
        mine = x.astype(send_type)
        x = mine.astype(f32) + swap(mine, axis, bit).astype(f32)
    return x


def halves(x, axis):
    head = lax.reduce_precision(x, 8, 7)
    tail = (x - head).astype(bf16)
    return jnp.concatenate([head.astype(bf16), tail], axis=axis)


def fold(x, axis):
    a, b = slices(x, 2, axis)
    return a + b


def dot(a, b, dims):
    return lax.dot_general(a, b, ((dims[:1], dims[1:]), ((), ())), preferred_element_type=f32)


def pick_kernel(index_ref, ok_ref, in_ref, out_ref):
    ok = ok_ref[pl.program_id(0)] > 0
    out_ref[...] = jnp.where(ok, in_ref[...], jnp.zeros_like(in_ref))


def pick_blocks(blocks, index, ok):
    width = blocks.shape[1]
    return pl.pallas_call(
        pick_kernel,
        out_shape=jax.ShapeDtypeStruct((index.shape[0] * BLOCK, width), blocks.dtype),
        grid_spec=pltpu.PrefetchScalarGridSpec(
            num_scalar_prefetch=2,
            grid=(index.shape[0],),
            in_specs=[pl.BlockSpec((BLOCK, width), lambda k, index, ok: (index[k], 0))],
            out_specs=pl.BlockSpec((BLOCK, width), lambda k, index, ok: (k, 0)),
        ),
        cost_estimate=pl.CostEstimate(
            flops=0, transcendentals=0, bytes_accessed=4 * index.shape[0] * BLOCK * width
        ),
    )(index, ok, blocks)


def earlier(labels):
    ids = jnp.arange(labels.shape[0], dtype=jnp.int32)
    same = (labels[:, None] == labels[None, :]) & (ids[None, :] < ids[:, None])
    return jnp.sum(same.astype(jnp.int32), axis=1)


def send_plan(ranks, ranks_dp):
    place = ranks * CAP + earlier(ranks)
    chosen = jnp.arange(ranks_dp * CAP, dtype=jnp.int32)[:, None] == place[None, :]
    ids = jnp.arange(ranks.shape[0], dtype=jnp.int32)
    index = jnp.sum(jnp.where(chosen, ids[None, :], 0), axis=1)
    return index.astype(jnp.int32), jnp.any(chosen, axis=1).astype(jnp.int32)


def recv_plan(all_ranks, per_rank, me, most):
    total = all_ranks.shape[0]
    ids = jnp.arange(total, dtype=jnp.int32)
    source = ids // per_rank
    order = earlier(all_ranks)
    within = earlier(all_ranks + source * total)
    place = source * CAP + within
    mine = all_ranks == me
    chosen = mine[None, :] & (order[None, :] == jnp.arange(most, dtype=jnp.int32)[:, None])
    index = jnp.sum(jnp.where(chosen, place[None, :], 0), axis=1)
    return index.astype(jnp.int32), jnp.any(chosen, axis=1).astype(jnp.int32)


def all_ranks_of(ranks, me):
    count = lax.axis_size("dp")
    table = jnp.where(jnp.arange(count, dtype=jnp.int32)[:, None] == me, ranks[None, :], 0)
    for bit in bits_of(count):
        table = table + swap(table, "dp", bit)
    return table.reshape(-1)


def inverse_factor(gram):
    lower = jnp.linalg.cholesky(gram)
    return jax.scipy.linalg.solve_triangular(lower, jnp.eye(gram.shape[0], dtype=f32), lower=True)


def local(patches, cotangent, encoder_rank, block_fill, w_up, w_down, q_up, q_down):
    ranks_dp = lax.axis_size("dp")
    count = lax.axis_size("mp")
    me, me_dp = lax.axis_index("mp"), lax.axis_index("dp")
    blocks = encoder_rank.shape[0]
    features = patches.shape[1]
    high = lax.Precision.HIGHEST

    x = jnp.concatenate(gather_xor(patches), axis=1)
    c = jnp.concatenate(gather_xor(cotangent), axis=1)
    every = all_ranks_of(encoder_rank, me_dp)
    w1 = jnp.concatenate(reorder(slices(w_up, count, 0), me), axis=0)
    w2 = jnp.concatenate(reorder(slices(w_down, count, 1), me), axis=1)
    qd = halves(jnp.concatenate(reorder(slices(q_down, count, 0), me), axis=0), 1)
    qu = halves(q_up, 1)

    within = jnp.arange(BLOCK, dtype=jnp.int32)
    keep = (within[None, :] < block_fill[:, None]).reshape(-1, 1)

    preact = dot(x, w1, (1, 0))
    sig = jax.nn.sigmoid(1.702 * preact)
    hidden = (preact * sig).astype(bf16)
    slope = sig + 1.702 * preact * sig * (1.0 - sig)
    partial = jnp.where(keep, dot(hidden, w2, (1, 0)), 0.0)

    c = jnp.where(keep, c, jnp.zeros((), bf16))
    grad_pre = (dot(c, w2, (1, 1)) * slope).astype(bf16)
    u = fold(dot(grad_pre, qu, (1, 0)), 1)
    t = fold(dot(c, qd, (1, 0)), 1)
    proj_up = fold(dot(halves(u, 1), x, (0, 0)), 0)
    proj_down = fold(dot(halves(t, 1), hidden, (0, 0)), 0)

    proj_down = sum_over(proj_down, "dp", bf16)
    proj_up = sum_over(reduce_mp(slices(proj_up, count, 1), f32), "dp", f32)
    proj_up = jnp.concatenate(spread_mp(proj_up), axis=1)

    v2 = fold(dot(hidden, halves(proj_down, 0), (1, 1)), 1)
    raw_down = fold(dot(halves(v2, 1), c, (0, 0)), 0)
    v = fold(dot(x, halves(proj_up, 0), (1, 1)), 1)
    raw_up = fold(dot(halves(v, 1), grad_pre, (0, 0)), 0)

    gram_up = jnp.dot(proj_up, proj_up.T, precision=high)
    gram_down = sum_over(jnp.dot(proj_down, proj_down.T, precision=high), "mp", f32)
    inv_up = inverse_factor(gram_up)
    inv_down = inverse_factor(gram_down)
    basis_up = jnp.dot(inv_up, proj_up, precision=high)
    basis_up = jnp.concatenate(reorder(slices(basis_up, count, 1), me), axis=1)
    basis_down = jnp.dot(inv_down, proj_down, precision=high)

    raw_up = sum_over(raw_up, "dp", bf16)
    raw_down = sum_over(reduce_mp(slices(raw_down, count, 1), f32), "dp", f32)
    raw_down = jnp.concatenate(reorder(spread_mp(raw_down), me), axis=1)
    fresh_up = jnp.dot(inv_up, raw_up, precision=high)
    fresh_down = jnp.dot(inv_down, raw_down, precision=high)
    approx_up = lax.dot_general(basis_up, fresh_up, (((0,), (0,)), ((), ())), precision=lax.Precision.HIGH)
    approx_down = lax.dot_general(basis_down, fresh_down, (((0,), (0,)), ((), ())), precision=lax.Precision.HIGH)

    own = reduce_mp(slices(partial, count, 1), bf16).astype(bf16)
    sent = pick_blocks(own, *send_plan(encoder_rank, ranks_dp))
    got = lax.all_to_all(sent, "dp", split_axis=0, concat_axis=0, tiled=True)
    encoded = pick_blocks(got, *recv_plan(every, blocks, me_dp, blocks + EXTRA))
    return (encoded, approx_up, approx_down, fresh_up.T, fresh_down.T)


def solution(mesh):
    placed = (
        P("dp", "mp"),
        P("dp", "mp"),
        P("dp"),
        P("dp"),
        P(None, "mp"),
        P("mp", None),
        P("mp", None),
        P(),
    )
    return jax.shard_map(
        local,
        mesh=mesh,
        in_specs=placed,
        out_specs=(P("dp", "mp"), P(None, "mp"), P("mp", None), P("mp", None), P()),
        check_vma=False,
    )
```

profile of v0, /device:TPU:0, one launch (start us, length us, event | category | flops | bytes accessed | tf_op | source)
XLA Modules:
  0.0 255.2 jit_solution(14559785387690790541)
XLA Ops:
  1.2 2.6 %collective-permute-start.4 = (bf16[1024,320]{0,1:T(8,128)(2,1)}, bf16[1024,320]{0,1:T(8,128)(2,1)}, u32[]{:S(2)}, u32[]{:S(2)}) collective-permute-start(bf16[1024,320]{0,1:T(8,128)(2,1)} %param.11), channel_id=1, source_target_pairs={{0,2},{1,3},{2,0},{3,1},{4,6},{5,7},{6,4},{7,5},{8,10},{9,11},{10,... | collective-permute-start | bytes 1966088 | tf_op jit(solution)/shard_map/ppermute | solution.py:23
  4.9 1.7 collective-permute-start
  9.3 1.7 reduce-precision_convert_fusion.3
  11.1 1.9 broadcast_select_fusion.17
  12.9 1.8 concatenate.76
  14.8 1.7 reduce-precision_convert_fusion.1
  16.5 4.2 %broadcast_select_fusion.16 = (bf16[320,1280]{1,0:T(8,128)(2,1)}, bf16[320,1280]{1,0:T(8,128)(2,1)}, bf16[320,1280]{1,0:T(8,128)(2,1)}, bf16[320,1280]{1,0:T(8,128)(2,1)}) fusion(pred[]{:T(512)S(6)} %ne.60, bf16[1280,1280]{1,0:T(8,128)(2,1)} %param.15, pred[]{:T(512)S(6)} %ne.61), kind=kLoop, calls=%fused_computation.34 | loop fusion | flops 3276800 | bytes 6553602 | tf_op jit(solution)/shard_map/jit(_where)/select_n | solution.py:39
  20.7 2.9 %broadcast_select_fusion.5 = (bf16[1280,320]{1,0:T(8,128)(2,1)}, bf16[1280,320]{1,0:T(8,128)(2,1)}, bf16[1280,320]{1,0:T(8,128)(2,1)}, bf16[1280,320]{1,0:T(8,128)(2,1)}) fusion(pred[]{:T(512)S(6)} %ne.60, bf16[1280,1280]{1,0:T(8,128)(2,1)S(1)} %copy-done.4, pred[]{:T(512)S(6)} %ne.61), kind=kLoop, calls=%fused_computation.23 | loop fusion | flops 3276800 | bytes 6553602 | tf_op jit(solution)/shard_map/jit(_where)/select_n | solution.py:39
  23.7 6.8 %concatenate.65 = bf16[1280,1280]{1,0:T(8,128)(2,1)} concatenate(bf16[1280,320]{1,0:T(8,128)(2,1)} %get-tuple-element.25, bf16[1280,320]{1,0:T(8,128)(2,1)} %get-tuple-element.23, bf16[1280,320]{1,0:T(8,128)(2,1)} %get-tuple-element.24, bf16[1280,320]{1,0:T(8,128)(2,1)} %get-tuple-element.22), dimensions={1} | concatenate | bytes 6553600 | tf_op jit(solution)/shard_map/concatenate | solution.py:165
  30.7 1.6 collective-permute-start.1
  32.4 1.9 collective-permute-done.1
  34.3 2.6 %collective-permute-start.2 = (s32[8,8]{1,0:T(8,128)S(1)}, s32[8,8]{1,0:T(8,128)S(1)}, u32[]{:S(2)}, u32[]{:S(2)}) collective-permute-start(s32[8,8]{1,0:T(8,128)S(1)} %add.151), channel_id=1, source_target_pairs={{0,16},{4,20},{8,24},{12,28},{16,0},{20,4},{24,8},{28,12},{1,17},{... | collective-permute-start | bytes 776 | tf_op jit(solution)/shard_map/ppermute | solution.py:23
  40.7 2.2 copy.40
  43.5 2.2 copy.39
  48.0 2.3 copy.41
  50.3 5.8 %concatenate.67 = bf16[1024,1280]{1,0:T(8,128)(2,1)} concatenate(bf16[1024,320]{1,0:T(8,128)(2,1)S(1)} %copy.38, bf16[1024,320]{1,0:T(8,128)(2,1)} %copy.39, bf16[1024,320]{1,0:T(8,128)(2,1)} %copy.40, bf16[1024,320]{1,0:T(8,128)(2,1)} %copy.41), dimensions={1} | concatenate | bytes 5242880 | tf_op jit(solution)/shard_map/concatenate | solution.py:162
  56.1 3.0 %fusion.25 = f32[1024,128]{0,1:T(8,128)S(1)} fusion(bf16[1280,64]{0,1:T(8,128)(2,1)} %get-tuple-element.49, bf16[1280,64]{0,1:T(8,128)(2,1)} %get-tuple-element.48, bf16[1024,1280]{1,0:T(8,128)(2,1)} %concatenate.67, pred[1024]{0:T(1024)(128)(4,1)S(1)} %fusion.77), kind=kOutput, calls=%fused_computation.69 | convolution fusion | flops 337510400 | bytes 3474432 | tf_op jit(solution)/shard_map/dot_general | solution.py:88
  60.4 4.4 %multiply_convert_fusion.1 = (bf16[1024,1280]{1,0:T(8,128)(2,1)S(1)}, f32[1024,1280]{1,0:T(8,128)S(1)}) fusion(bf16[1024,1280]{0,1:T(8,128)(2,1)S(1)} %constant_dynamic-update-slice_fusion, bf16[320,1280]{1,0:T(8,128)(2,1)S(1)} %copy-done.13, bf16[320,1280]{1,0:T(8,128)(2,1)S(1)} %copy-done.12, bf16[320,1280]{1,0:T(8,128)(2,1)S(1)} %copy-done.11, ...), kind=kOutput, calls=%fused_computation.1 | convolution fusion | flops 3376414720 | bytes 13762560 | tf_op jit(solution)/shard_map/dot_general | solution.py:88
  64.8 4.8 %multiply_convert_fusion = bf16[1024,1280]{1,0:T(8,128)(2,1)S(1)} fusion(f32[1024,1280]{1,0:T(8,128)S(1)} %get-tuple-element.69, bf16[1280,1280]{1,0:T(8,128)(2,1)S(1)} %copy-done.5, bf16[1024,1280]{1,0:T(8,128)(2,1)S(1)} %copy-done.6, pred[1024]{0:T(1024)(128)(4,1)S(1)} %fusion.77), kind=kOutput, calls=%fused_computation | convolution fusion | flops 3369861120 | bytes 13763584 | tf_op jit(solution)/shard_map/dot_general | solution.py:88
  72.7 5.3 %fusion.92 = (bf16[1024,1280]{1,0:T(8,128)(2,1)S(1)}, f32[1024,1280]{1,0:T(8,128)}) fusion(bf16[1024,1280]{1,0:T(8,128)(2,1)S(1)} %get-tuple-element.68, bf16[1280,1280]{1,0:T(8,128)(2,1)S(1)} %copy-done.5, pred[1024]{0:T(1024)(128)(4,1)S(1)} %fusion.77), kind=kOutput, calls=%fused_computation.211 | convolution fusion | flops 3358064640 | bytes 13763584 | tf_op jit(solution)/shard_map/dot_general | solution.py:88
  79.0 1.8 collective-permute-start.12
  80.9 4.4 %collective-permute-done.21 = bf16[64,1280]{1,0:T(8,128)(2,1)S(1)} collective-permute-done((bf16[64,1280]{1,0:T(8,128)(2,1)S(1)}, bf16[64,1280]{1,0:T(8,128)(2,1)S(1)}, u32[]{:S(2)}, u32[]{:S(2)}) %collective-permute-start.21) | collective-permute-done | bytes 163872 | tf_op jit(solution)/shard_map/ppermute | solution.py:23
  85.3 1.6 collective-permute-start.22
  87.5 3.5 %collective-permute-done.22 = bf16[64,1280]{1,0:T(8,128)(2,1)S(1)} collective-permute-done((bf16[64,1280]{1,0:T(8,128)(2,1)S(1)}, bf16[64,1280]{1,0:T(8,128)(2,1)S(1)}, u32[]{:S(2)}, u32[]{:S(2)}) %collective-permute-start.22) | collective-permute-done | bytes 163872 | tf_op jit(solution)/shard_map/ppermute | solution.py:23
  91.1 2.7 %collective-permute-start.23 = (bf16[64,1280]{1,0:T(8,128)(2,1)S(1)}, bf16[64,1280]{1,0:T(8,128)(2,1)S(1)}, u32[]{:S(2)}, u32[]{:S(2)}) collective-permute-start(bf16[64,1280]{1,0:T(8,128)(2,1)S(1)} %add_convert_fusion), channel_id=1, source_target_pairs={{0,16},{4,20},{8,24},{12,28},{16,0},{20,4},{24,8},{28,12},{1,17},{... | collective-permute-start | bytes 491528 | tf_op jit(solution)/shard_map/ppermute | solution.py:23
  94.5 1.6 collective-permute-start.14
  97.7 2.9 %collective-permute-done.14 = f32[64,320]{1,0:T(8,128)S(1)} collective-permute-done((f32[64,320]{1,0:T(8,128)S(1)}, f32[64,320]{1,0:T(8,128)S(1)}, u32[]{:S(2)}, u32[]{:S(2)}) %collective-permute-start.14) | collective-permute-done | bytes 81952 | tf_op jit(solution)/shard_map/ppermute | solution.py:23
  108.9 5.8 %cholesky.55 = f32[64,64]{1,0:T(8,128)S(1)} custom-call(f32[64,64]{1,0:T(8,128)S(1)} %fusion.68), custom_call_target="Cholesky" | custom-call | tf_op jit(solution)/shard_map/jit(cholesky)/cholesky | solution.py:149
  116.1 4.9 %custom-call.7 = f32[1,64,64]{1,2,0:T(8,128)S(1)} custom-call(f32[1,64,64]{2,1,0:T(8,128)S(1)} %fusion.66), custom_call_target="InvertDiagBlocksLowerTriangular" | custom-call | tf_op jit(solution)/shard_map/jit(_solve_triangular)/triangular_solve | solution.py:150
  121.9 1.7 slice_add_fusion.10
  133.5 7.2 %cholesky.44 = f32[64,64]{1,0:T(8,128)} custom-call(f32[64,64]{1,0:T(8,128)} %fusion.70), custom_call_target="Cholesky" | custom-call | tf_op jit(solution)/shard_map/jit(cholesky)/cholesky | solution.py:149
  142.2 3.1 %fusion.21 = f32[1024,128]{0,1:T(8,128)} fusion(bf16[1024,1280]{0,1:T(8,128)(2,1)} %copy-done, bf16[64,1280]{1,0:T(8,128)(2,1)} %get-tuple-element.55, bf16[64,1280]{1,0:T(8,128)(2,1)S(1)} %get-tuple-element.54), kind=kOutput, calls=%fused_computation.65 | convolution fusion | flops 336199680 | bytes 3473408 | tf_op jit(solution)/shard_map/dot_general | solution.py:88
  146.0 4.9 %custom-call.6 = f32[1,64,64]{1,2,0:T(8,128)S(1)} custom-call(f32[1,64,64]{2,1,0:T(8,128)S(1)} %fusion.65), custom_call_target="InvertDiagBlocksLowerTriangular" | custom-call | tf_op jit(solution)/shard_map/jit(_solve_triangular)/triangular_solve | solution.py:150
  157.2 2.0 fusion.8
  161.5 3.4 %collective-permute-start.30 = (f32[64,320]{1,0:T(8,128)S(1)}, f32[64,320]{1,0:T(8,128)S(1)}, u32[]{:S(2)}, u32[]{:S(2)}) collective-permute-start(f32[64,320]{1,0:T(8,128)S(1)} %add.187), channel_id=1, source_target_pairs={{0,16},{4,20},{8,24},{12,28},{16,0},{20,4},{24,8},{28,12},{1,17},{... | collective-permute-start | bytes 245768 | tf_op jit(solution)/shard_map/ppermute | solution.py:23
  166.3 2.2 collective-permute-done.30
  168.8 7.6 %collective-permute-done.7 = bf16[1024,320]{0,1:T(8,128)(2,1)} collective-permute-done((bf16[1024,320]{0,1:T(8,128)(2,1)S(1)}, bf16[1024,320]{0,1:T(8,128)(2,1)}, u32[]{:S(2)}, u32[]{:S(2)}) %collective-permute-start.7) | collective-permute-done | bytes 655392 | tf_op jit(solution)/shard_map/ppermute | solution.py:23
  176.3 1.7 copy.35
  178.0 2.7 %fusion.10.in_ref = bf16[1024,320]{1,0:T(8,128)(2,1)} fusion(f32[1024,1280]{1,0:T(8,128)} %get-tuple-element.71, bf16[1024,320]{1,0:T(8,128)(2,1)S(1)} %copy.35, bf16[1024,640]{1,0:T(8,128)(2,1)} %collective-permute-done.6), kind=kLoop, calls=%fused_computation.17 | loop fusion | flops 1638400 | bytes 3276800 | tf_op jit(solution)/shard_map/convert_element_type | solution.py:210
  180.8 9.5 %shard_map.119 = bf16[2048,320]{1,0:T(8,128)(2,1)} custom-call(s32[16]{0:T(128)} %select_reduce_fusion.3.index_ref, s32[16]{0:T(128)} %convert_element_type.150.ok_ref, bf16[1024,320]{1,0:T(8,128)(2,1)} %fusion.10.in_ref), custom_call_target="tpu_custom_call" | custom-call | bytes 2621440 | tf_op jit(solution)/shard_map/pallas_call | solution.py:98
  190.3 2.6 %copy.36 = bf16[8,256,320]{1,2,0:T(8,128)(2,1)} copy(bf16[8,256,320]{2,1,0:T(8,128)(2,1)} %bitcast.46) | data formatting | bytes 2621440 | tf_op jit(solution)/shard_map/all_to_all | solution.py:212
  192.9 5.0 %all-to-all-start = ((bf16[8,256,320]{1,2,0:T(8,128)(2,1)}), bf16[8,256,320]{1,2,0:T(8,128)(2,1)S(1)}, u32[]{:S(2)}, u32[]{:S(2)}) async-start(bf16[8,256,320]{1,2,0:T(8,128)(2,1)} %copy.36), calls=%async_computation | async-start | bytes 2621440 | tf_op jit(solution)/shard_map/all_to_all | solution.py:212
  198.4 3.0 %collective-permute-start.20 = (bf16[64,1280]{1,0:T(8,128)(2,1)S(1)}, bf16[64,1280]{1,0:T(8,128)(2,1)S(1)}, u32[]{:S(2)}, u32[]{:S(2)}) collective-permute-start(bf16[64,1280]{1,0:T(8,128)(2,1)S(1)} %add_convert_fusion.2), channel_id=1, source_target_pairs={{0,16},{4,20},{8,24},{12,28},{16,0},{20,4},{24,8},{28,12},{1,17},{... | collective-permute-start | bytes 491528 | tf_op jit(solution)/shard_map/ppermute | solution.py:23
  202.1 31.9 %collective-permute-done.20 = bf16[64,1280]{1,0:T(8,128)(2,1)S(1)} collective-permute-done((bf16[64,1280]{1,0:T(8,128)(2,1)S(1)}, bf16[64,1280]{1,0:T(8,128)(2,1)S(1)}, u32[]{:S(2)}, u32[]{:S(2)}) %collective-permute-start.20) | collective-permute-done | bytes 163872 | tf_op jit(solution)/shard_map/ppermute | solution.py:23
  234.4 4.7 %fusion.95 = f32[1280,1280]{1,0:T(8,128)} fusion(f32[64,1280]{1,0:T(8,128)S(1)} %concatenate.73, f32[64,1280]{1,0:T(8,128)S(1)} %fusion.33), kind=kOutput, calls=%fused_computation.214 | convolution fusion | flops 629145600 | bytes 7208960 | tf_op jit(solution)/shard_map/dot_general | solution.py:207
  239.1 4.7 %fusion.97 = f32[1280,1280]{1,0:T(8,128)} fusion(f32[64,1280]{1,0:T(8,128)S(1)} %fusion.37, f32[64,1280]{1,0:T(8,128)S(1)} %fusion.96), kind=kOutput, calls=%fused_computation.216 | convolution fusion | flops 629145600 | bytes 7208960 | tf_op jit(solution)/shard_map/dot_general | solution.py:208
  245.4 7.4 %shard_map.120 = bf16[1792,320]{1,0:T(8,128)(2,1)} custom-call(s32[14]{0:T(128)} %select_reduce_fusion.2.index_ref, s32[14]{0:T(128)} %convert_element_type.148.ok_ref, bf16[2048,320]{1,0:T(8,128)(2,1)} %bitcast.47), custom_call_target="tpu_custom_call" | custom-call | bytes 2293760 | tf_op jit(solution)/shard_map/pallas_call | solution.py:98
  252.8 2.4 copy.46
  (181 shorter events, 55.1 us)
Async XLA Ops:
  0.6 8.6 %copy-start.20 = (s32[8]{0:T(128)S(1)}, s32[8]{0:T(128)}, u32[]{:S(2)}) copy-start(s32[8]{0:T(128)} %param.14) | copy-start | bytes 100
  0.6 45.1 %collective-permute-start.3 = (bf16[1024,320]{0,1:T(8,128)(2,1)}, bf16[1024,320]{0,1:T(8,128)(2,1)}, u32[]{:S(2)}, u32[]{:S(2)}) collective-permute-start(bf16[1024,320]{0,1:T(8,128)(2,1)} %param.11), channel_id=1, source_target_pairs={{0,1},{1,0},{2,3},{3,2},{4,5},{5,4},{6,7},{7,6},{8,9},{9,8},{10,11... | collective-permute-start | bytes 1966088 | tf_op jit(solution)/shard_map/ppermute | solution.py:23
  1.2 41.8 %collective-permute-start.4 = (bf16[1024,320]{0,1:T(8,128)(2,1)}, bf16[1024,320]{0,1:T(8,128)(2,1)}, u32[]{:S(2)}, u32[]{:S(2)}) collective-permute-start(bf16[1024,320]{0,1:T(8,128)(2,1)} %param.11), channel_id=1, source_target_pairs={{0,2},{1,3},{2,0},{3,1},{4,6},{5,7},{6,4},{7,5},{8,10},{9,11},{10,... | collective-permute-start | bytes 1966088 | tf_op jit(solution)/shard_map/ppermute | solution.py:23
  3.8 39.7 %collective-permute-start.8 = (bf16[1024,320]{0,1:T(8,128)(2,1)}, bf16[1024,320]{0,1:T(8,128)(2,1)}, u32[]{:S(2)}, u32[]{:S(2)}) collective-permute-start(bf16[1024,320]{0,1:T(8,128)(2,1)} %param.12), channel_id=1, source_target_pairs={{0,1},{1,0},{2,3},{3,2},{4,5},{5,4},{6,7},{7,6},{8,9},{9,8},{10,11... | collective-permute-start | bytes 1966088 | tf_op jit(solution)/shard_map/ppermute | solution.py:23
  3.9 35.9 %collective-permute-start.9 = (bf16[1024,320]{0,1:T(8,128)(2,1)}, bf16[1024,320]{0,1:T(8,128)(2,1)}, u32[]{:S(2)}, u32[]{:S(2)}) collective-permute-start(bf16[1024,320]{0,1:T(8,128)(2,1)} %param.12), channel_id=1, source_target_pairs={{0,2},{1,3},{2,0},{3,1},{4,6},{5,7},{6,4},{7,5},{8,10},{9,11},{10,... | collective-permute-start | bytes 1966088 | tf_op jit(solution)/shard_map/ppermute | solution.py:23
  4.9 25.5 %collective-permute-start = (s32[8,8]{1,0:T(8,128)S(1)}, s32[8,8]{1,0:T(8,128)S(1)}, u32[]{:S(2)}, u32[]{:S(2)}) collective-permute-start(s32[8,8]{1,0:T(8,128)S(1)} %broadcast_select_fusion.29), channel_id=1, source_target_pairs={{0,4},{4,0},{8,12},{12,8},{16,20},{20,16},{24,28},{28,24},{1,5},{5... | collective-permute-start | bytes 776 | tf_op jit(solution)/shard_map/ppermute | solution.py:23
  23.7 6.8 %copy-start.19 = (s32[8]{0:T(128)S(1)}, s32[8]{0:T(128)}, u32[]{:S(2)}) copy-start(s32[8]{0:T(128)} %param.13) | copy-start | bytes 100
  30.7 3.7 %collective-permute-start.1 = (s32[8,8]{1,0:T(8,128)S(1)}, s32[8,8]{1,0:T(8,128)S(1)}, u32[]{:S(2)}, u32[]{:S(2)}) collective-permute-start(s32[8,8]{1,0:T(8,128)S(1)} %get-tuple-element.67), channel_id=1, source_target_pairs={{0,8},{4,12},{8,0},{12,4},{16,24},{20,28},{24,16},{28,20},{1,9},{5... | collective-permute-start | bytes 776 | tf_op jit(solution)/shard_map/ppermute | solution.py:23
  34.3 4.5 %collective-permute-start.2 = (s32[8,8]{1,0:T(8,128)S(1)}, s32[8,8]{1,0:T(8,128)S(1)}, u32[]{:S(2)}, u32[]{:S(2)}) collective-permute-start(s32[8,8]{1,0:T(8,128)S(1)} %add.151), channel_id=1, source_target_pairs={{0,16},{4,20},{8,24},{12,28},{16,0},{20,4},{24,8},{28,12},{1,17},{... | collective-permute-start | bytes 776 | tf_op jit(solution)/shard_map/ppermute | solution.py:23
  39.8 8.2 %collective-permute-start.10 = (bf16[1024,320]{0,1:T(8,128)(2,1)}, bf16[1024,320]{0,1:T(8,128)(2,1)}, u32[]{:S(2)}, u32[]{:S(2)}) collective-permute-start(bf16[1024,320]{0,1:T(8,128)(2,1)} %collective-permute-done.9), channel_id=1, source_target_pairs={{0,1},{1,0},{2,3},{3,2},{4,5},{5,4},{6,7},{7,6},{8,9},{9,8},{10,11... | collective-permute-start | bytes 1966088 | tf_op jit(solution)/shard_map/ppermute | solution.py:23
  43.0 16.2 %collective-permute-start.5 = (bf16[1024,320]{0,1:T(8,128)(2,1)}, bf16[1024,320]{0,1:T(8,128)(2,1)}, u32[]{:S(2)}, u32[]{:S(2)}) collective-permute-start(bf16[1024,320]{0,1:T(8,128)(2,1)} %collective-permute-done.4), channel_id=1, source_target_pairs={{0,1},{1,0},{2,3},{3,2},{4,5},{5,4},{6,7},{7,6},{8,9},{9,8},{10,11... | collective-permute-start | bytes 1966088 | tf_op jit(solution)/shard_map/ppermute | solution.py:23
  56.1 4.2 %copy-start.12 = (bf16[320,1280]{1,0:T(8,128)(2,1)S(1)}, bf16[320,1280]{1,0:T(8,128)(2,1)}, u32[]{:S(2)}) copy-start(bf16[320,1280]{1,0:T(8,128)(2,1)} %get-tuple-element.28) | copy-start | bytes 2457604
  56.1 4.2 %copy-start.13 = (bf16[320,1280]{1,0:T(8,128)(2,1)S(1)}, bf16[320,1280]{1,0:T(8,128)(2,1)}, u32[]{:S(2)}) copy-start(bf16[320,1280]{1,0:T(8,128)(2,1)} %get-tuple-element.29) | copy-start | bytes 2457604
  60.3 4.5 %copy-start = (bf16[1024,1280]{0,1:T(8,128)(2,1)}, bf16[1024,1280]{0,1:T(8,128)(2,1)S(1)}, u32[]{:S(2)}) copy-start(bf16[1024,1280]{0,1:T(8,128)(2,1)S(1)} %constant_dynamic-update-slice_fusion) | copy-start | bytes 7864324
  60.3 4.4 %copy-start.5 = (bf16[1280,1280]{1,0:T(8,128)(2,1)S(1)}, bf16[1280,1280]{1,0:T(8,128)(2,1)}, u32[]{:S(2)}) copy-start(bf16[1280,1280]{1,0:T(8,128)(2,1)} %concatenate.65) | copy-start | bytes 9830404
  60.4 4.4 %copy-start.6 = (bf16[1024,1280]{1,0:T(8,128)(2,1)S(1)}, bf16[1024,1280]{1,0:T(8,128)(2,1)}, u32[]{:S(2)}) copy-start(bf16[1024,1280]{1,0:T(8,128)(2,1)} %concatenate.67) | copy-start | bytes 7864324
  64.8 4.8 %copy-start.14 = (bf16[1280,64]{0,1:T(8,128)(2,1)S(1)}, bf16[1280,64]{0,1:T(8,128)(2,1)}, u32[]{:S(2)}) copy-start(bf16[1280,64]{0,1:T(8,128)(2,1)} %get-tuple-element.62) | copy-start | bytes 491524
  64.8 4.8 %copy-start.15 = (bf16[1280,64]{0,1:T(8,128)(2,1)S(1)}, bf16[1280,64]{0,1:T(8,128)(2,1)}, u32[]{:S(2)}) copy-start(bf16[1280,64]{0,1:T(8,128)(2,1)} %get-tuple-element.63) | copy-start | bytes 491524
  72.6 6.3 %collective-permute-start.11 = (f32[64,640]{1,0:T(8,128)S(1)}, f32[64,640]{1,0:T(8,128)S(1)}, u32[]{:S(2)}, u32[]{:S(2)}) collective-permute-start(f32[64,640]{1,0:T(8,128)S(1)} %pad_maximum_fusion.1), channel_id=1, source_target_pairs={{0,1},{1,0},{2,3},{3,2},{4,5},{5,4},{6,7},{7,6},{8,9},{9,8},{10,11... | collective-permute-start | bytes 491528 | tf_op jit(solution)/shard_map/ppermute | solution.py:23
  78.6 6.6 %collective-permute-start.21 = (bf16[64,1280]{1,0:T(8,128)(2,1)S(1)}, bf16[64,1280]{1,0:T(8,128)(2,1)S(1)}, u32[]{:S(2)}, u32[]{:S(2)}) collective-permute-start(bf16[64,1280]{1,0:T(8,128)(2,1)S(1)} %fusion.15), channel_id=1, source_target_pairs={{0,4},{4,0},{8,12},{12,8},{16,20},{20,16},{24,28},{28,24},{1,5},{5... | collective-permute-start | bytes 491528 | tf_op jit(solution)/shard_map/ppermute | solution.py:23
  79.0 7.9 %collective-permute-start.12 = (f32[64,320]{1,0:T(8,128)S(1)}, f32[64,320]{1,0:T(8,128)S(1)}, u32[]{:S(2)}, u32[]{:S(2)}) collective-permute-start(f32[64,320]{1,0:T(8,128)S(1)} %slice_add_fusion.12), channel_id=1, source_target_pairs={{0,2},{1,3},{2,0},{3,1},{4,6},{5,7},{6,4},{7,5},{8,10},{9,11},{10,... | collective-permute-start | bytes 245768 | tf_op jit(solution)/shard_map/ppermute | solution.py:23
  85.3 5.8 %collective-permute-start.22 = (bf16[64,1280]{1,0:T(8,128)(2,1)S(1)}, bf16[64,1280]{1,0:T(8,128)(2,1)S(1)}, u32[]{:S(2)}, u32[]{:S(2)}) collective-permute-start(bf16[64,1280]{1,0:T(8,128)(2,1)S(1)} %add_convert_fusion.1), channel_id=1, source_target_pairs={{0,8},{4,12},{8,0},{12,4},{16,24},{20,28},{24,16},{28,20},{1,9},{5... | collective-permute-start | bytes 491528 | tf_op jit(solution)/shard_map/ppermute | solution.py:23
  86.9 7.5 %collective-permute-start.13 = (f32[64,320]{1,0:T(8,128)S(1)}, f32[64,320]{1,0:T(8,128)S(1)}, u32[]{:S(2)}, u32[]{:S(2)}) collective-permute-start(f32[64,320]{1,0:T(8,128)S(1)} %fusion.60), channel_id=1, source_target_pairs={{0,4},{4,0},{8,12},{12,8},{16,20},{20,16},{24,28},{28,24},{1,5},{5... | collective-permute-start | bytes 245768 | tf_op jit(solution)/shard_map/ppermute | solution.py:23
  91.1 9.6 %collective-permute-start.23 = (bf16[64,1280]{1,0:T(8,128)(2,1)S(1)}, bf16[64,1280]{1,0:T(8,128)(2,1)S(1)}, u32[]{:S(2)}, u32[]{:S(2)}) collective-permute-start(bf16[64,1280]{1,0:T(8,128)(2,1)S(1)} %add_convert_fusion), channel_id=1, source_target_pairs={{0,16},{4,20},{8,24},{12,28},{16,0},{20,4},{24,8},{28,12},{1,17},{... | collective-permute-start | bytes 491528 | tf_op jit(solution)/shard_map/ppermute | solution.py:23
  94.5 6.1 %collective-permute-start.14 = (f32[64,320]{1,0:T(8,128)S(1)}, f32[64,320]{1,0:T(8,128)S(1)}, u32[]{:S(2)}, u32[]{:S(2)}) collective-permute-start(f32[64,320]{1,0:T(8,128)S(1)} %add.166), channel_id=1, source_target_pairs={{0,8},{4,12},{8,0},{12,4},{16,24},{20,28},{24,16},{28,20},{1,9},{5... | collective-permute-start | bytes 245768 | tf_op jit(solution)/shard_map/ppermute | solution.py:23
  97.7 59.6 %collective-permute-start.6 = (bf16[1024,640]{1,0:T(8,128)(2,1)}, bf16[1024,640]{1,0:T(8,128)(2,1)}, u32[]{:S(2)}, u32[]{:S(2)}) collective-permute-start(bf16[1024,640]{1,0:T(8,128)(2,1)} %pad_maximum_fusion), channel_id=1, source_target_pairs={{0,1},{1,0},{2,3},{3,2},{4,5},{5,4},{6,7},{7,6},{8,9},{9,8},{10,11... | collective-permute-start | bytes 3932168 | tf_op jit(solution)/shard_map/ppermute | solution.py:23
  100.6 6.6 %collective-permute-start.15 = (f32[64,320]{1,0:T(8,128)S(1)}, f32[64,320]{1,0:T(8,128)S(1)}, u32[]{:S(2)}, u32[]{:S(2)}) collective-permute-start(f32[64,320]{1,0:T(8,128)S(1)} %add.167), channel_id=1, source_target_pairs={{0,16},{4,20},{8,24},{12,28},{16,0},{20,4},{24,8},{28,12},{1,17},{... | collective-permute-start | bytes 245768 | tf_op jit(solution)/shard_map/ppermute | solution.py:23
  101.2 2.7 %collective-permute-start.24 = (f32[64,64]{0,1:T(8,128)S(1)}, f32[64,64]{0,1:T(8,128)S(1)}, u32[]{:S(2)}, u32[]{:S(2)}) collective-permute-start(f32[64,64]{0,1:T(8,128)S(1)} %fusion.38), channel_id=1, source_target_pairs={{0,1},{1,0},{2,3},{3,2},{4,5},{5,4},{6,7},{7,6},{8,9},{9,8},{10,11... | collective-permute-start | bytes 49160 | tf_op jit(solution)/shard_map/ppermute | solution.py:23
  103.9 4.9 %collective-permute-start.25 = (f32[64,64]{0,1:T(8,128)S(1)}, f32[64,64]{0,1:T(8,128)S(1)}, u32[]{:S(2)}, u32[]{:S(2)}) collective-permute-start(f32[64,64]{0,1:T(8,128)S(1)} %add.179), channel_id=1, source_target_pairs={{0,2},{1,3},{2,0},{3,1},{4,6},{5,7},{6,4},{7,5},{8,10},{9,11},{10,... | collective-permute-start | bytes 49160 | tf_op jit(solution)/shard_map/ppermute | solution.py:23
  106.3 15.6 %collective-permute-start.26 = (f32[64,640]{1,0:T(8,128)}, f32[64,640]{1,0:T(8,128)}, u32[]{:S(2)}, u32[]{:S(2)}) collective-permute-start(f32[64,640]{1,0:T(8,128)} %pad_maximum_fusion.3), channel_id=1, source_target_pairs={{0,1},{1,0},{2,3},{3,2},{4,5},{5,4},{6,7},{7,6},{8,9},{9,8},{10,11... | collective-permute-start | bytes 491528 | tf_op jit(solution)/shard_map/ppermute | solution.py:23
  107.2 14.5 %collective-permute-start.16 = (f32[64,320]{1,0:T(8,128)S(1)}, f32[64,320]{1,0:T(8,128)S(1)}, u32[]{:S(2)}, u32[]{:S(2)}) collective-permute-start(f32[64,320]{1,0:T(8,128)S(1)} %add.168), channel_id=1, source_target_pairs={{0,2},{1,3},{2,0},{3,1},{4,6},{5,7},{6,4},{7,5},{8,10},{9,11},{10,... | collective-permute-start | bytes 245768 | tf_op jit(solution)/shard_map/ppermute | solution.py:23
  121.8 2.4 collective-permute-start.17
  123.5 5.5 %collective-permute-start.27 = (f32[64,320]{1,0:T(8,128)}, f32[64,320]{1,0:T(8,128)}, u32[]{:S(2)}, u32[]{:S(2)}) collective-permute-start(f32[64,320]{1,0:T(8,128)} %slice_add_fusion.10), channel_id=1, source_target_pairs={{0,2},{1,3},{2,0},{3,1},{4,6},{5,7},{6,4},{7,5},{8,10},{9,11},{10,... | collective-permute-start | bytes 245768 | tf_op jit(solution)/shard_map/ppermute | solution.py:23
  130.0 25.2 %collective-permute-start.28 = (f32[64,320]{1,0:T(8,128)S(1)}, f32[64,320]{1,0:T(8,128)}, u32[]{:S(2)}, u32[]{:S(2)}) collective-permute-start(f32[64,320]{1,0:T(8,128)S(1)} %fusion.59), channel_id=1, source_target_pairs={{0,4},{4,0},{8,12},{12,8},{16,20},{20,16},{24,28},{28,24},{1,5},{5... | collective-permute-start | bytes 245768 | tf_op jit(solution)/shard_map/ppermute | solution.py:23
  140.7 4.7 %copy-start.18 = (f32[64,64]{1,0:T(8,128)S(1)}, f32[64,64]{1,0:T(8,128)}, u32[]{:S(2)}) copy-start(f32[64,64]{1,0:T(8,128)} %cholesky.44) | copy-start | bytes 49156
  153.6 11.4 %collective-permute-start.18 = (bf16[64,1280]{1,0:T(8,128)(2,1)S(1)}, bf16[64,1280]{1,0:T(8,128)(2,1)}, u32[]{:S(2)}, u32[]{:S(2)}) collective-permute-start(bf16[64,1280]{1,0:T(8,128)(2,1)S(1)} %fusion.16), channel_id=1, source_target_pairs={{0,4},{4,0},{8,12},{12,8},{16,20},{20,16},{24,28},{28,24},{1,5},{5... | collective-permute-start | bytes 491528 | tf_op jit(solution)/shard_map/ppermute | solution.py:23
  156.1 5.4 %collective-permute-start.29 = (f32[64,320]{1,0:T(8,128)S(1)}, f32[64,320]{1,0:T(8,128)S(1)}, u32[]{:S(2)}, u32[]{:S(2)}) collective-permute-start(f32[64,320]{1,0:T(8,128)S(1)} %add.186), channel_id=1, source_target_pairs={{0,8},{4,12},{8,0},{12,4},{16,24},{20,28},{24,16},{28,20},{1,9},{5... | collective-permute-start | bytes 245768 | tf_op jit(solution)/shard_map/ppermute | solution.py:23
  157.2 7.8 %copy-start.3 = (f32[128,1280]{1,0:T(8,128)S(1)}, f32[128,1280]{1,0:T(8,128)}, u32[]{:S(2)}) copy-start(f32[128,1280]{1,0:T(8,128)} %copy-done.2) | copy-start | bytes 1966084
  159.5 16.8 %collective-permute-start.7 = (bf16[1024,320]{0,1:T(8,128)(2,1)S(1)}, bf16[1024,320]{0,1:T(8,128)(2,1)}, u32[]{:S(2)}, u32[]{:S(2)}) collective-permute-start(bf16[1024,320]{0,1:T(8,128)(2,1)S(1)} %copy.34), channel_id=1, source_target_pairs={{0,2},{1,3},{2,0},{3,1},{4,6},{5,7},{6,4},{7,5},{8,10},{9,11},{10,... | collective-permute-start | bytes 1966088 | tf_op jit(solution)/shard_map/ppermute | solution.py:23
  161.5 7.0 %collective-permute-start.30 = (f32[64,320]{1,0:T(8,128)S(1)}, f32[64,320]{1,0:T(8,128)S(1)}, u32[]{:S(2)}, u32[]{:S(2)}) collective-permute-start(f32[64,320]{1,0:T(8,128)S(1)} %add.187), channel_id=1, source_target_pairs={{0,16},{4,20},{8,24},{12,28},{16,0},{20,4},{24,8},{28,12},{1,17},{... | collective-permute-start | bytes 245768 | tf_op jit(solution)/shard_map/ppermute | solution.py:23
  166.0 32.4 %collective-permute-start.19 = (bf16[64,1280]{1,0:T(8,128)(2,1)S(1)}, bf16[64,1280]{1,0:T(8,128)(2,1)S(1)}, u32[]{:S(2)}, u32[]{:S(2)}) collective-permute-start(bf16[64,1280]{1,0:T(8,128)(2,1)S(1)} %add_convert_fusion.3), channel_id=1, source_target_pairs={{0,8},{4,12},{8,0},{12,4},{16,24},{20,28},{24,16},{28,20},{1,9},{5... | collective-permute-start | bytes 491528 | tf_op jit(solution)/shard_map/ppermute | solution.py:23
  168.5 29.6 %collective-permute-start.31 = (f32[64,320]{1,0:T(8,128)S(1)}, f32[64,320]{1,0:T(8,128)S(1)}, u32[]{:S(2)}, u32[]{:S(2)}) collective-permute-start(f32[64,320]{1,0:T(8,128)S(1)} %add.188), channel_id=1, source_target_pairs={{0,2},{1,3},{2,0},{3,1},{4,6},{5,7},{6,4},{7,5},{8,10},{9,11},{10,... | collective-permute-start | bytes 245768 | tf_op jit(solution)/shard_map/ppermute | solution.py:23
  192.9 8.8 %copy-start.17 = (f32[64,64]{1,0:T(8,128)S(1)}, f32[64,64]{1,0:T(8,128)}, u32[]{:S(2)}) copy-start(f32[64,64]{1,0:T(8,128)} %copy-done.16) | copy-start | bytes 49156
  192.9 51.0 %all-to-all-start = ((bf16[8,256,320]{1,2,0:T(8,128)(2,1)}), bf16[8,256,320]{1,2,0:T(8,128)(2,1)S(1)}, u32[]{:S(2)}, u32[]{:S(2)}) async-start(bf16[8,256,320]{1,2,0:T(8,128)(2,1)} %copy.36), calls=%async_computation | async-start | bytes 2621440 | tf_op jit(solution)/shard_map/all_to_all | solution.py:212
  198.2 3.1 %collective-permute-start.32 = (f32[64,640]{1,0:T(8,128)S(1)}, f32[64,640]{1,0:T(8,128)S(1)}, u32[]{:S(2)}, u32[]{:S(2)}) collective-permute-start(f32[64,640]{1,0:T(8,128)S(1)} %pad_maximum_fusion.4), channel_id=1, source_target_pairs={{0,1},{1,0},{2,3},{3,2},{4,5},{5,4},{6,7},{7,6},{8,9},{9,8},{10,11... | collective-permute-start | bytes 491528 | tf_op jit(solution)/shard_map/ppermute | solution.py:23
  198.4 35.6 %collective-permute-start.20 = (bf16[64,1280]{1,0:T(8,128)(2,1)S(1)}, bf16[64,1280]{1,0:T(8,128)(2,1)S(1)}, u32[]{:S(2)}, u32[]{:S(2)}) collective-permute-start(bf16[64,1280]{1,0:T(8,128)(2,1)S(1)} %add_convert_fusion.2), channel_id=1, source_target_pairs={{0,16},{4,20},{8,24},{12,28},{16,0},{20,4},{24,8},{28,12},{1,17},{... | collective-permute-start | bytes 491528 | tf_op jit(solution)/shard_map/ppermute | solution.py:23
  202.0 37.1 %copy-start.8 = (f32[64,1280]{1,0:T(8,128)}, f32[64,1280]{1,0:T(8,128)S(1)}, u32[]{:S(2)}) copy-start(f32[64,1280]{1,0:T(8,128)S(1)} %fusion.96) | copy-start | bytes 983044
  234.4 4.7 %copy-start.9 = (f32[64,1280]{1,0:T(8,128)}, f32[64,1280]{1,0:T(8,128)S(1)}, u32[]{:S(2)}) copy-start(f32[64,1280]{1,0:T(8,128)S(1)} %fusion.33) | copy-start | bytes 983044
  (7 other events, 19.6 us)
where the time goes:
time: 258 us; the launch traced here: 255 us
  other arithmetic  58.7 us (23%)
  waiting for transfers between devices  57.1 us (22%)
  local copies, waits for them, and re-layouts  42.7 us (17%)
  starting transfers between devices  40.2 us (16%)
  matrix products  38.2 us (15%)
  Pallas kernels  16.9 us (7%)
    ppermute x33, waiting for transfers between devices, swap(): return lax.ppermute(x, axis, [(i, i ^ bit) for i in range(count)])  57.1 us
    ppermute x33, starting transfers between devices, swap(): return lax.ppermute(x, axis, [(i, i ^ bit) for i in range(count)])  35.2 us
    dot_general x11, matrix products, dot(): lax.dot_general(a, b, ((dims[:1], dims[1:]), ((), ())), preferred_element...  25.2 us
    pallas_call x2, Pallas kernels, pick_blocks(): pl.pallas_call(pick_kernel, out_shape=jax.ShapeDtypeStruct((index.shape[0...  16.9 us
    another operation x6, other arithmetic, inverse_factor(): lower = jnp.linalg.cholesky(gram)  15.3 us
    another operation x4, other arithmetic, inverse_factor(): jax.scipy.linalg.solve_triangular(lower, jnp.eye(gram.shape[0], dtype=f32...  11.1 us
    unnamed x47, local copies, waits for them, and re-layouts  9.61 us
    select_n x5, other arithmetic, reorder(): jnp.where(flip, pieces[i ^ bit], pieces[i])  9.24 us
  transfers between devices with their start and end apart: 34, of which 10 were waited for; matrix products, arithmetic and copies ran while one was open for 47% of the time, Pallas kernels for 4%

commit v1 on v0

v1 whole, which is shorter than its diff:
```python
import functools

import jax
import jax.numpy as jnp
from jax import lax
from jax.experimental import pallas as pl
from jax.experimental.pallas import tpu as pltpu
from jax.sharding import PartitionSpec as P

BLOCK = 128
TILE = 256
CAP = 2
EXTRA = 6
bf16 = jnp.bfloat16
f32 = jnp.float32
HIGHEST = lax.Precision.HIGHEST


def bits_of(count):
    return [1 << b for b in range(count.bit_length() - 1)]


def swap(x, axis, bit):
    count = lax.axis_size(axis)
    return lax.ppermute(x, axis, [(i, i ^ bit) for i in range(count)])


def gather_xor(own):
    count = lax.axis_size("mp")
    pieces = {0: own}
    for bit in bits_of(count)[1:]:
        pieces.update({o | bit: swap(p, "mp", bit) for o, p in list(pieces.items())})
    pieces.update({o | 1: swap(p, "mp", 1) for o, p in list(pieces.items())})
    return [pieces[o] for o in range(count)]


def reorder(pieces, me):
    for bit in bits_of(len(pieces)):
        flip = (me & bit) != 0
        pieces = [jnp.where(flip, pieces[i ^ bit], pieces[i]) for i in range(len(pieces))]
    return pieces


def slices(x, count, axis):
    size = x.shape[axis] // count
    return [lax.slice_in_dim(x, i * size, (i + 1) * size, axis=axis) for i in range(count)]


def reduce_mp(even, odd):
    have = even + swap(odd, "mp", 1)
    for bit in bits_of(lax.axis_size("mp"))[1:]:
        have = have.reshape(have.shape[0] // 2, 2, *have.shape[1:])
        have = have[:, 0] + swap(have[:, 1], "mp", bit)
    return have[0]


def spread_mp(own):
    have = {0: own}
    for bit in reversed(bits_of(lax.axis_size("mp"))):
        offsets = sorted(have)
        if len(offsets) == 1:
            got = [swap(have[0], "mp", bit)]
        else:
            sent = swap(jnp.stack([have[o] for o in offsets]), "mp", bit)
            got = [sent[i] for i in range(len(offsets))]
        have.update({o | bit: g for o, g in zip(offsets, got)})
    return [have[o] for o in range(len(have))]


def sum_over(x, axis, send_type):
    for bit in bits_of(lax.axis_size(axis)):
        mine = x.astype(send_type)
        x = mine.astype(f32) + swap(mine, axis, bit).astype(f32)
    return x


def dot(a, b, contract=(1, 0), precision=None):
    dims = (((contract[0],), (contract[1],)), ((), ()))
    return lax.dot_general(a, b, dims, preferred_element_type=f32, precision=precision)


def head_tail(x):
    head = x.astype(bf16)
    return head, (x - head.astype(f32)).astype(bf16)


def stacked(x):
    return jnp.concatenate(head_tail(x), axis=0)


def fold(x):
    rows = x.shape[0] // 2
    return x[:rows] + x[rows:]


def call(body, out_shape, args, scalars=(), grid=(1,), in_specs=None, out_specs=None, scratch=(), flops=0):
    moved = sum(a.size * a.dtype.itemsize for a in args)
    moved += sum(o.size * o.dtype.itemsize for o in jax.tree.leaves(out_shape))
    return pl.pallas_call(
        body,
        out_shape=out_shape,
        grid_spec=pltpu.PrefetchScalarGridSpec(
            num_scalar_prefetch=len(scalars),
            grid=grid,
            in_specs=in_specs,
            out_specs=out_specs,
            scratch_shapes=list(scratch),
        ),
        cost_estimate=pl.CostEstimate(flops=flops, transcendentals=0, bytes_accessed=moved),
        compiler_params=pltpu.CompilerParams(vmem_limit_bytes=48 << 20),
    )(*scalars, *args)


def whole(x):
    return pl.BlockSpec(x.shape, lambda *_: (0,) * len(x.shape), pipeline_mode=pl.Buffered(1))


def tokens_of(x):
    return pl.BlockSpec((x.shape[0], TILE), lambda i, *_: (0, i))


def struct(shape, dtype):
    return jax.ShapeDtypeStruct(shape, dtype)


def prepare_kernel(count, me_ref, up_ref, down_ref, up_t_ref, down_t_ref, down_x_ref, held):
    me = me_ref[0]
    features, hidden = up_ref.shape
    piece = features // count
    strip = TILE
    for o in range(count):
        rows = pl.ds(pl.multiple_of((me ^ o) * piece, piece), piece)
        held[o * piece : (o + 1) * piece, :] = up_ref[rows, :]

    for k in range(0, hidden, strip):
        up_t_ref[k : k + strip, :] = held[:, k : k + strip].T
    for k in range(0, down_ref.shape[0], strip):
        held[:, k : k + strip] = down_ref[k : k + strip, :].T
    for o in range(count):
        rows = pl.ds(pl.multiple_of((me ^ o) * piece, piece), piece)
        down_t_ref[o * piece : (o + 1) * piece, :] = held[rows, :]
    for k in range(0, down_ref.shape[0], strip):
        down_x_ref[k : k + strip, :] = down_t_ref[:, k : k + strip].T


def prepare(w_up, w_down, me, count):
    features, hidden = w_up.shape
    outs = (struct((hidden, features), bf16), struct((features, hidden), bf16), struct((hidden, features), bf16))
    return call(
        functools.partial(prepare_kernel, count),
        outs,
        (w_up, w_down),
        (me.reshape(1),),
        in_specs=[whole(w_up), whole(w_down)],
        out_specs=[whole(o) for o in outs],
        scratch=[pltpu.VMEM((features, hidden), bf16)],
    )


def assemble(refs, held):
    at = 0
    for ref in refs:
        held[at : at + ref.shape[0], :] = ref[...]
        at += ref.shape[0]


def lanes_kept(fill_ref, block):
    return lax.broadcasted_iota(jnp.int32, (1, BLOCK), 1) < fill_ref[block]


def mask_tokens(x, fill_ref):
    per = TILE // BLOCK
    parts = []
    for b in range(per):
        keep = lanes_kept(fill_ref, pl.program_id(0) * per + b)
        part = x[:, b * BLOCK : (b + 1) * BLOCK]
        parts.append(jnp.where(keep, part, jnp.zeros_like(part)))
    return jnp.concatenate(parts, axis=1)


def forward_kernel(count, fill_ref, *refs):
    x_refs, (up_t_ref, down_t_ref), refs = refs[:count], refs[count : count + 2], refs[count + 2 :]
    hidden_ref, slope_ref, out_refs, held = refs[0], refs[1], refs[2:-1], refs[-1]
    assemble(x_refs, held)
    preact = dot(up_t_ref[...], held[...])
    sig = jax.nn.sigmoid(1.702 * preact)
    active = preact * sig
    hidden_ref[...] = active.astype(bf16)
    slope_ref[...] = (sig + 1.702 * active * (1.0 - sig)).astype(bf16)
    out = mask_tokens(dot(down_t_ref[...], hidden_ref[...]), fill_ref).astype(bf16)
    piece = out.shape[0] // count
    for o, ref in enumerate(out_refs):
        ref[...] = out[o * piece : (o + 1) * piece]


def forward(xs, up_t, down_t, fill):
    count = len(xs)
    piece, total = xs[0].shape
    hidden, features = up_t.shape
    outs = [struct((hidden, total), bf16)] * 2 + [struct((piece, total), bf16)] * count
    got = call(
        functools.partial(forward_kernel, count),
        outs,
        (*xs, up_t, down_t),
        (fill,),
        grid=(total // TILE,),
        in_specs=[tokens_of(x) for x in xs] + [whole(up_t), whole(down_t)],
        out_specs=[tokens_of(o) for o in outs],
        scratch=[pltpu.VMEM((features, TILE), bf16)],
        flops=4 * features * hidden * total,
    )
    return got[0], got[1], got[2:]


def write_pieces(value, even_ref, odd_ref):
    half, _, piece = even_ref.shape
    for o in range(2 * half):
        part = value[:, o * piece : (o + 1) * piece]
        (odd_ref if o & 1 else even_ref)[o // 2] = part


def backward_kernel(count, fill_ref, *refs):
    c_refs, x_refs, refs = refs[:count], refs[count : 2 * count], refs[2 * count :]
    slope_ref, hidden_ref, down_x_ref, qu_ref, qd_ref = refs[:5]
    grad_ref, even_ref, odd_ref, down_ref, held_c, held_x, acc_up, acc_down = refs[5:]
    step = pl.program_id(0)

    @pl.when(step == 0)
    def _():
        acc_up[...] = jnp.zeros_like(acc_up)
        acc_down[...] = jnp.zeros_like(acc_down)

    assemble(c_refs, held_c)
    assemble(x_refs, held_x)
    held_c[...] = mask_tokens(held_c[...], fill_ref)
    grad = dot(down_x_ref[...], held_c[...])
    grad_ref[...] = (grad * slope_ref[...].astype(f32)).astype(bf16)
    t = fold(dot(qd_ref[...], held_c[...]))
    acc_down[...] += fold(dot(stacked(t), hidden_ref[...], (1, 1)))
    u = fold(dot(qu_ref[...], grad_ref[...]))
    acc_up[...] += fold(dot(stacked(u), held_x[...], (1, 1)))

    @pl.when(step == pl.num_programs(0) - 1)
    def _():
        down_ref[...] = acc_down[...]
        write_pieces(acc_up[...], even_ref, odd_ref)


def backward(cs, xs, slope, hidden, down_x, qu, qd, fill):
    count = len(xs)
    piece, total = xs[0].shape
    units, features = down_x.shape
    rank = qu.shape[0] // 2
    pieces = struct((count // 2, rank, piece), f32)
    outs = [struct((units, total), bf16), pieces, pieces, struct((rank, units), f32)]
    return call(
        functools.partial(backward_kernel, count),
        outs,
        (*cs, *xs, slope, hidden, down_x, qu, qd),
        (fill,),
        grid=(total // TILE,),
        in_specs=[tokens_of(x) for x in (*cs, *xs, slope, hidden)] + [whole(x) for x in (down_x, qu, qd)],
        out_specs=[tokens_of(outs[0])] + [whole(o) for o in outs[1:]],
        scratch=[
            pltpu.VMEM((features, TILE), bf16),
            pltpu.VMEM((features, TILE), bf16),
            pltpu.VMEM((rank, features), f32),
            pltpu.VMEM((rank, units), f32),
        ],
        flops=2 * features * units * total,
    )


def two_sided_kernel(n_left, n_first, n_second, masked, fill_ref, *refs):
    left_refs, refs = refs[:n_left], refs[n_left:]
    first_refs, refs = refs[:n_first], refs[n_first:]
    second_refs, refs = refs[:n_second], refs[n_second:]
    out_refs, (left, first, second, acc) = refs[:-4], refs[-4:]
    rank = left_refs[0].shape[0]

    @pl.when(pl.program_id(0) == 0)
    def _():
        acc[...] = jnp.zeros_like(acc)
        joined = jnp.concatenate([r[...] for r in left_refs], axis=1)
        left[...] = stacked(joined)

    assemble(first_refs, first)
    assemble(second_refs, second)
    v = fold(dot(left[...], first[...]))
    if masked:
        v = mask_tokens(v, fill_ref)
    acc[...] += fold(dot(stacked(v), second[...], (1, 1)))

    @pl.when(pl.program_id(0) == pl.num_programs(0) - 1)
    def _():
        if masked:
            write_pieces(acc[...], *out_refs)
        else:
            out_refs[0][...] = acc[...]


def two_sided(lefts, firsts, seconds, fill, masked):
    rank = lefts[0].shape[0]
    total = firsts[0].shape[1]
    inner = sum(x.shape[0] for x in firsts)
    outer = sum(x.shape[0] for x in seconds)
    if masked:
        pieces = struct((len(seconds) // 2, rank, seconds[0].shape[0]), f32)
        outs = [pieces, pieces]
    else:
        outs = [struct((rank, outer), f32)]
    return call(
        functools.partial(two_sided_kernel, len(lefts), len(firsts), len(seconds), masked),
        outs,
        (*lefts, *firsts, *seconds),
        (fill,),
        grid=(total // TILE,),
        in_specs=[whole(x) for x in lefts] + [tokens_of(x) for x in (*firsts, *seconds)],
        out_specs=[whole(o) for o in outs],
        scratch=[
            pltpu.VMEM((2 * rank, inner), bf16),
            pltpu.VMEM((inner, TILE), bf16),
            pltpu.VMEM((outer, TILE), bf16),
            pltpu.VMEM((rank, outer), f32),
        ],
        flops=4 * rank * (inner + outer) * total,
    )


def outer_kernel(n_raw, me_ref, inv_ref, basis_ref, *refs):
    raw_refs, (fresh_ref, approx_ref, right) = refs[:n_raw], refs[n_raw:]

    @pl.when(pl.program_id(0) == 0)
    def _():
        raw = jnp.concatenate(reorder([r[...] for r in raw_refs], me_ref[0]), axis=1)
        fresh = dot(inv_ref[...], raw, precision=HIGHEST)
        fresh_ref[...] = fresh
        head, tail = head_tail(fresh)
        right[...] = jnp.concatenate([head, tail, head], axis=0)

    head, tail = head_tail(basis_ref[...])
    approx_ref[...] = dot(jnp.concatenate([head, head, tail], axis=0), right[...], (0, 0))


def outer(inv, basis, raws, me):
    rank, rows = basis.shape
    columns = sum(r.shape[1] for r in raws)
    outs = [struct((rank, columns), f32), struct((rows, columns), f32)]
    return call(
        functools.partial(outer_kernel, len(raws)),
        outs,
        (inv, basis, *raws),
        (me.reshape(1),),
        grid=(rows // BLOCK // 2 if rows % (2 * BLOCK) == 0 else rows // BLOCK,),
        in_specs=[whole(inv), pl.BlockSpec((rank, 2 * BLOCK if rows % (2 * BLOCK) == 0 else BLOCK), lambda i, *_: (0, i))]
        + [whole(r) for r in raws],
        out_specs=[
            whole(outs[0]),
            pl.BlockSpec((2 * BLOCK if rows % (2 * BLOCK) == 0 else BLOCK, columns), lambda i, *_: (i, 0)),
        ],
        scratch=[pltpu.VMEM((3 * rank, columns), bf16)],
        flops=6 * rank * rows * columns,
    )


def pack_kernel(index_ref, a_ref, b_ref, out_ref):
    for s in range(out_ref.shape[0]):
        lanes = pl.ds(pl.multiple_of(index_ref[s] * BLOCK, BLOCK), BLOCK)
        total = a_ref[:, lanes].astype(f32) + b_ref[:, lanes].astype(f32)
        out_ref[s] = total.astype(bf16)


def pack(a, b, index):
    out = struct((index.shape[0], a.shape[0], BLOCK), bf16)
    return call(pack_kernel, out, (a, b), (index,), in_specs=[whole(a), whole(b)], out_specs=whole(out))


def unpack_kernel(index_ref, ok_ref, in_ref, out_ref):
    for k in range(out_ref.shape[1] // BLOCK):
        part = in_ref[index_ref[k]]
        out_ref[:, k * BLOCK : (k + 1) * BLOCK] = jnp.where(ok_ref[k] > 0, part, jnp.zeros_like(part))


def unpack(got, index, ok):
    out = struct((got.shape[1], index.shape[0] * BLOCK), bf16)
    return call(unpack_kernel, out, (got,), (index, ok), in_specs=[whole(got)], out_specs=whole(out))


def earlier(labels):
    ids = jnp.arange(labels.shape[0], dtype=jnp.int32)
    same = (labels[:, None] == labels[None, :]) & (ids[None, :] < ids[:, None])
    return jnp.sum(same.astype(jnp.int32), axis=1)


def send_plan(ranks, ranks_dp):
    place = ranks * CAP + earlier(ranks)
    chosen = jnp.arange(ranks_dp * CAP, dtype=jnp.int32)[:, None] == place[None, :]
    ids = jnp.arange(ranks.shape[0], dtype=jnp.int32)
    return jnp.sum(jnp.where(chosen, ids[None, :], 0), axis=1).astype(jnp.int32)


def recv_plan(all_ranks, per_rank, me, most):
    total = all_ranks.shape[0]
    ids = jnp.arange(total, dtype=jnp.int32)
    source = ids // per_rank
    order = earlier(all_ranks)
    within = earlier(all_ranks + source * total)
    place = source * CAP + within
    mine = all_ranks == me
    chosen = mine[None, :] & (order[None, :] == jnp.arange(most, dtype=jnp.int32)[:, None])
    index = jnp.sum(jnp.where(chosen, place[None, :], 0), axis=1)
    return index.astype(jnp.int32), jnp.any(chosen, axis=1).astype(jnp.int32)


def all_ranks_of(ranks, me):
    count = lax.axis_size("dp")
    table = jnp.where(jnp.arange(count, dtype=jnp.int32)[:, None] == me, ranks[None, :], 0)
    for bit in bits_of(count):
        table = table + swap(table, "dp", bit)
    return table.reshape(-1)


def inverse_factor(gram):
    lower = jnp.linalg.cholesky(gram)
    return jax.scipy.linalg.solve_triangular(lower, jnp.eye(gram.shape[0], dtype=f32), lower=True)


def split_rows(x):
    head = lax.reduce_precision(x, 8, 7)
    return jnp.concatenate([head.astype(bf16), (x - head).astype(bf16)], axis=0)


def local(patches, cotangent, encoder_rank, block_fill, w_up, w_down, q_up, q_down):
    ranks_dp = lax.axis_size("dp")
    count = lax.axis_size("mp")
    me, me_dp = lax.axis_index("mp"), lax.axis_index("dp")
    blocks = encoder_rank.shape[0]

    xs = gather_xor(patches.T)
    cs = gather_xor(cotangent.T)
    every = all_ranks_of(encoder_rank, me_dp)
    up_t, down_t, down_x = prepare(w_up, w_down, me, count)
    qd = split_rows(jnp.concatenate(reorder(slices(q_down.T, count, 1), me), axis=1))
    qu = split_rows(q_up.T)

    hidden, slope, outs = forward(xs, up_t, down_t, block_fill)
    grad_pre, even, odd, proj_down = backward(cs, xs, slope, hidden, down_x, qu, qd, block_fill)

    proj_down = sum_over(proj_down, "dp", bf16)
    proj_up = spread_mp(sum_over(reduce_mp(even, odd), "dp", f32))

    even, odd = two_sided([proj_down], [hidden], cs, block_fill, True)
    (raw_up,) = two_sided(proj_up, xs, [grad_pre], block_fill, False)
    proj_up = jnp.concatenate(reorder(proj_up, me), axis=1)

    gram_up = jnp.dot(proj_up, proj_up.T, precision=HIGHEST)
    gram_down = sum_over(jnp.dot(proj_down, proj_down.T, precision=HIGHEST), "mp", f32)
    inv_up = inverse_factor(gram_up)
    inv_down = inverse_factor(gram_down)
    basis_up = jnp.dot(inv_up, proj_up, precision=HIGHEST)
    basis_down = jnp.dot(inv_down, proj_down, precision=HIGHEST)

    raw_up = sum_over(raw_up, "dp", bf16)
    raw_down = spread_mp(sum_over(reduce_mp(even, odd), "dp", f32))
    fresh_up, approx_up = outer(inv_up, basis_up, [raw_up], me)
    fresh_down, approx_down = outer(inv_down, basis_down, raw_down, me)

    have = dict(enumerate(outs))
    have = {o - 1: (have[o - 1].astype(f32) + swap(have[o], "mp", 1).astype(f32)).astype(bf16) for o in have if o & 1}
    for bit in bits_of(count)[1:]:
        got = {o ^ bit: swap(have[o], "mp", bit) for o in have if o & bit}
        if len(got) == 1:
            break
        have = {o: (have[o].astype(f32) + got[o].astype(f32)).astype(bf16) for o in got}
    sent = pack(have[0], got[0], send_plan(encoder_rank, ranks_dp))
    received = lax.all_to_all(sent, "dp", split_axis=0, concat_axis=0, tiled=True)
    encoded = unpack(received, *recv_plan(every, blocks, me_dp, blocks + EXTRA))
    return (encoded.T, approx_up, approx_down, fresh_up.T, fresh_down.T)


def solution(mesh):
    placed = (
        P("dp", "mp"),
        P("dp", "mp"),
        P("dp"),
        P("dp"),
        P(None, "mp"),
        P("mp", None),
        P("mp", None),
        P(),
    )
    return jax.shard_map(
        local,
        mesh=mesh,
        in_specs=placed,
        out_specs=(P("dp", "mp"), P(None, "mp"), P("mp", None), P("mp", None), P()),
        check_vma=False,
    )
```

time: 258 us -> 223 us (0.86)
  Pallas kernels: 16.9 us -> 64.8 us
  matrix products: 38.2 us -> 4.65 us
  local copies, waits for them, and re-layouts: 42.7 us -> 10.6 us
  other arithmetic: 58.7 us -> 37.4 us
  starting transfers between devices: 40.2 us -> 43.5 us
  waiting for transfers between devices: 57.1 us -> 59.7 us
    pallas_call x2 -> x9, Pallas kernels: 16.9 us -> 64.8 us  [call(): pl.pallas_call(body, out_shape=out_shape, grid_spec=pltpu.PrefetchScalarG...]
    dot_general x19 -> x4, matrix products: 37.7 us -> 3.38 us  [the longest x1 2.14 us: local(): basis_down = jnp.dot(inv_down, proj_down, precision=HIGHEST)]
    concatenate x7 -> x2, local copies, waits for them, and re-layouts: 16.9 us -> 1.17 us  [the longest x1 1.03 us: local(): proj_up = jnp.concatenate(reorder(proj_up, me), axis=1)]
    ppermute x4 -> x0, local copies, waits for them, and re-layouts: 8.46 us -> none  [swap(): return lax.ppermute(x, axis, [(i, i ^ bit) for i in range(count)])]
    select_n x5 -> x2, other arithmetic: 9.24 us -> 1.88 us  [reorder(): jnp.where(flip, pieces[i ^ bit], pieces[i])]
    convert_element_type x11 -> x4, other arithmetic: 10.8 us -> 5.38 us  [the longest x2 4.33 us: local(): (have[o - 1].astype(f32) + swap(have[o], 'mp', 1).astype(f32)).astype(bf16)]
    all_to_all x2 -> x0, local copies, waits for them, and re-layouts: 4.12 us -> none  [local(): got = lax.all_to_all(sent, 'dp', split_axis=0, concat_axis=0, tiled=True)]
    add x6 -> x0, other arithmetic: 2.85 us -> none  [the longest x4 2.78 us: reduce_mp(): pieces[o ^ bit] + g.astype(f32)]
  transfers between devices with their start and end apart: 34 -> 35, of which waited for: 10 -> 11; matrix products, arithmetic and copies ran while one was open for 47% -> 20% of each run, Pallas kernels for 4% -> 23%
where the time goes in v1:
time: 223 us; the launch traced here: 222 us
  Pallas kernels  64.8 us (29%)
  waiting for transfers between devices  59.7 us (27%)
  starting transfers between devices  43.5 us (20%)
  other arithmetic  37.4 us (17%)
  local copies, waits for them, and re-layouts  10.6 us (5%)
  matrix products  4.65 us (2%)
    pallas_call x9, Pallas kernels, call(): pl.pallas_call(body, out_shape=out_shape, grid_spec=pltpu.PrefetchScalarG...  64.8 us
    ppermute x34, waiting for transfers between devices, swap(): return lax.ppermute(x, axis, [(i, i ^ bit) for i in range(count)])  59.7 us
    ppermute x34, starting transfers between devices, swap(): return lax.ppermute(x, axis, [(i, i ^ bit) for i in range(count)])  37.8 us
    another operation x6, other arithmetic, inverse_factor(): lower = jnp.linalg.cholesky(gram)  13.8 us
    another operation x4, other arithmetic, inverse_factor(): jax.scipy.linalg.solve_triangular(lower, jnp.eye(gram.shape[0], dtype=f32...  11.7 us
    unnamed x48, local copies, waits for them, and re-layouts  7.58 us
    all_to_all x1, starting transfers between devices, local(): lax.all_to_all(sent, 'dp', split_axis=0, concat_axis=0, tiled=True)  5.72 us
  transfers between devices with their start and end apart: 35, of which 11 were waited for; matrix products, arithmetic and copies ran while one was open for 20% of the time, Pallas kernels for 23%

profile of v1, /device:TPU:0, one launch (start us, length us, event | category | flops | bytes accessed | tf_op | source)
XLA Modules:
  0.0 221.8 jit_solution(1778104349658463682)
XLA Ops:
  1.2 2.6 %collective-permute-start.4 = (bf16[320,1024]{1,0:T(8,128)(2,1)}, bf16[320,1024]{1,0:T(8,128)(2,1)S(1)}, u32[]{:S(2)}, u32[]{:S(2)}) collective-permute-start(bf16[320,1024]{1,0:T(8,128)(2,1)} %bitcast.86), channel_id=1, source_target_pairs={{0,2},{1,3},{2,0},{3,1},{4,6},{5,7},{6,4},{7,5},{8,10},{9,11},{10,... | collective-permute-start | bytes 1966088 | tf_op jit(solution)/shard_map/ppermute | solution.py:25
  4.9 1.7 collective-permute-start
  7.7 1.2 broadcast_select_fusion.8
  9.1 7.9 %shard_map.119 = (bf16[1280,1280]{1,0:T(8,128)(2,1)S(1)}, bf16[1280,1280]{1,0:T(8,128)(2,1)}, bf16[1280,1280]{1,0:T(8,128)(2,1)}) custom-call(s32[1]{0:T(128)} %bitcast.1.me_ref, bf16[1280,1280]{1,0:T(8,128)(2,1)} %up_ref.1, bf16[1280,1280]{1,0:T(8,128)(2,1)} %down_ref.1), custom_call_target="tpu_custom_call" | custom-call | bytes 16384000 | tf_op jit(solution)/shard_map/pallas_call | solution.py:99
  17.0 1.7 copy-done.15
  18.9 1.6 collective-permute-start.1
  20.5 2.0 collective-permute-done.1
  22.6 2.6 %collective-permute-start.2 = (s32[8,8]{1,0:T(8,128)S(1)}, s32[8,8]{1,0:T(8,128)S(1)}, u32[]{:S(2)}, u32[]{:S(2)}) collective-permute-start(s32[8,8]{1,0:T(8,128)S(1)} %add.112), channel_id=1, source_target_pairs={{0,16},{4,20},{8,24},{12,28},{16,0},{20,4},{24,8},{28,12},{1,17},{... | collective-permute-start | bytes 776 | tf_op jit(solution)/shard_map/ppermute | solution.py:25
  25.2 1.8 collective-permute-done.2
  27.2 6.3 %collective-permute-done.10.refs_2_.refs_4_ = bf16[320,1024]{1,0:T(8,128)(2,1)} collective-permute-done((bf16[320,1024]{1,0:T(8,128)(2,1)}, bf16[320,1024]{1,0:T(8,128)(2,1)}, u32[]{:S(2)}, u32[]{:S(2)}) %collective-permute-start.10) | collective-permute-done | bytes 655392 | tf_op jit(solution)/shard_map/ppermute | solution.py:25
  33.7 18.8 %shard_map.120 = (bf16[1280,1024]{1,0:T(8,128)(2,1)}, bf16[1280,1024]{1,0:T(8,128)(2,1)}, bf16[320,1024]{1,0:T(8,128)(2,1)S(1)}, bf16[320,1024]{1,0:T(8,128)(2,1...) custom-call(s32[8]{0:T(128)S(1)} %copy-done.14, bf16[320,1024]{1,0:T(8,128)(2,1)S(1)} %bitcast.87, ...), custom_call_target="tpu_custom_call" | custom-call | flops 6710886400 | bytes 17039360 | tf_op jit(solution)/shard_map/pallas_call | solution.py:99
  54.2 13.1 %shard_map.123 = (bf16[1280,1024]{1,0:T(8,128)(2,1)}, f32[2,64,320]{2,1,0:T(8,128)S(1)}, f32[2,64,320]{2,1,0:T(8,128)S(1)}, f32[64,1280]{1,0:T(8,128)S(1)}) custom-call(s32[8]{0:T(128)S(1)} %copy-done.14, bf16[320,1024]{1,0:T(8,128)(2,1)S(1)} %bitcast.92, bf16[320,1024]{1,0:T(8,128)(2,1)} %collective-permute-done.9.refs_1_.refs_3_, ...), custom_call_target="tpu_custom_call" | custom-call | flops 3355443200 | bytes 17694720 | tf_op jit(solution)/shard_map/pallas_call | solution.py:99
  67.8 1.8 collective-permute-start.22
  69.6 1.6 collective-permute-start.13
  71.2 2.8 %collective-permute-done.22 = bf16[64,1280]{1,0:T(8,128)(2,1)S(1)} collective-permute-done((bf16[64,1280]{1,0:T(8,128)(2,1)S(1)}, bf16[64,1280]{1,0:T(8,128)(2,1)S(1)}, u32[]{:S(2)}, u32[]{:S(2)}) %collective-permute-start.22) | collective-permute-done | bytes 163872 | tf_op jit(solution)/shard_map/ppermute | solution.py:25
  74.0 1.9 collective-permute-start.23
  75.9 1.6 collective-permute-start.14
  77.6 3.0 %collective-permute-done.14 = f32[64,320]{1,0:T(8,128)S(1)} collective-permute-done((f32[64,320]{1,0:T(8,128)S(1)}, f32[64,320]{1,0:T(8,128)S(1)}, u32[]{:S(2)}, u32[]{:S(2)}) %collective-permute-start.14) | collective-permute-done | bytes 81952 | tf_op jit(solution)/shard_map/ppermute | solution.py:25
  80.9 2.9 %collective-permute-start.24 = (bf16[64,1280]{1,0:T(8,128)(2,1)S(1)}, bf16[64,1280]{1,0:T(8,128)(2,1)S(1)}, u32[]{:S(2)}, u32[]{:S(2)}) collective-permute-start(bf16[64,1280]{1,0:T(8,128)(2,1)S(1)} %add_convert_fusion.2), channel_id=1, source_target_pairs={{0,16},{4,20},{8,24},{12,28},{16,0},{20,4},{24,8},{28,12},{1,17},{... | collective-permute-start | bytes 491528 | tf_op jit(solution)/shard_map/ppermute | solution.py:25
  83.9 1.3 collective-permute-done.15
  85.3 3.6 %collective-permute-start.16 = (f32[64,320]{1,0:T(8,128)S(1)}, f32[64,320]{1,0:T(8,128)S(1)}, u32[]{:S(2)}, u32[]{:S(2)}) collective-permute-start(f32[64,320]{1,0:T(8,128)S(1)} %add.122), channel_id=1, source_target_pairs={{0,16},{4,20},{8,24},{12,28},{16,0},{20,4},{24,8},{28,12},{1,17},{... | collective-permute-start | bytes 245768 | tf_op jit(solution)/shard_map/ppermute | solution.py:25
  89.5 4.3 %collective-permute-done.16 = f32[64,320]{1,0:T(8,128)S(1)} collective-permute-done((f32[64,320]{1,0:T(8,128)S(1)}, f32[64,320]{1,0:T(8,128)S(1)}, u32[]{:S(2)}, u32[]{:S(2)}) %collective-permute-start.16) | collective-permute-done | bytes 81952 | tf_op jit(solution)/shard_map/ppermute | solution.py:25
  93.8 1.6 collective-permute-start.17
  96.0 1.1 collective-permute-done.25
  97.7 5.9 %shard_map.126 = (f32[2,64,320]{2,1,0:T(8,128)S(1)}, f32[2,64,320]{2,1,0:T(8,128)}) custom-call(s32[8]{0:T(128)S(1)} %copy-done.14, f32[64,1280]{1,0:T(8,128)S(1)} %convert_add_fusion.refs_0_, bf16[1280,1024]{1,0:T(8,128)(2,1)S(1)} %copy-done, bf16[320,1024]{1,0:T(8,128)(2,1)S(1)} %bitcast.93, bf16[320,1024]{1,0:T(8,128)(2,1)} %collective-permute-done.9.refs_1_.refs_3_, ...), custom_call_target="tpu_custom_call" | custom-call | flops 671088640 | bytes 5898240 | tf_op jit(solution)/shard_map/pallas_call | solution.py:99
  105.0 6.6 %cholesky.55 = f32[64,64]{1,0:T(8,128)S(1)} custom-call(f32[64,64]{1,0:T(8,128)} %fusion.13), custom_call_target="Cholesky" | custom-call | tf_op jit(solution)/shard_map/jit(cholesky)/cholesky | solution.py:424
  113.0 5.5 %custom-call.7 = f32[1,64,64]{1,2,0:T(8,128)} custom-call(f32[1,64,64]{2,1,0:T(8,128)S(1)} %fusion.11), custom_call_target="InvertDiagBlocksLowerTriangular" | custom-call | tf_op jit(solution)/shard_map/jit(_solve_triangular)/triangular_solve | solution.py:425
  119.5 2.1 fusion.22.basis_ref
  122.3 2.2 add_convert_fusion
  124.4 1.5 collective-permute-start.8
  128.8 2.2 add_convert_fusion.1.a_ref
  134.2 5.8 %cholesky.44 = f32[64,64]{1,0:T(8,128)S(1)} custom-call(f32[64,64]{1,0:T(8,128)S(1)} %fusion.15), custom_call_target="Cholesky" | custom-call | tf_op jit(solution)/shard_map/jit(cholesky)/cholesky | solution.py:424
  140.1 1.7 copy-done.5
  141.8 4.4 %shard_map.124 = f32[64,1280]{1,0:T(8,128)S(1)} custom-call(s32[8]{0:T(128)S(1)} %copy-done.14, f32[64,320]{1,0:T(8,128)S(1)} %add.123.refs_0_, f32[64,320]{1,0:T(8,128)S(1)} %get-tuple-element.60.refs_1_, f32[64,320]{1,0:T(8,128)S(1)} %collective-permute-done.17.refs_2_, f32[64,320]{1,0:T(8,128)S(1)} %get-tuple-element.59.refs_3_, ...), custom_call_target="tpu_custom_call" | custom-call | flops 671088640 | bytes 5898240 | tf_op jit(solution)/shard_map/pallas_call | solution.py:99
  146.3 1.6 collective-permute-start.19
  150.7 4.9 %custom-call.6 = f32[1,64,64]{1,2,0:T(8,128)S(1)} custom-call(f32[1,64,64]{2,1,0:T(8,128)S(1)} %fusion.10), custom_call_target="InvertDiagBlocksLowerTriangular" | custom-call | tf_op jit(solution)/shard_map/jit(_solve_triangular)/triangular_solve | solution.py:425
  156.1 1.1 copy-done.6
  157.2 3.4 %shard_map.121 = bf16[16,320,128]{2,1,0:T(8,128)(2,1)} custom-call(s32[16]{0:T(128)S(1)} %select_reduce_fusion.3.index_ref, bf16[320,1024]{1,0:T(8,128)(2,1)S(1)} %copy-done.6, bf16[320,1024]{1,0:T(8,128)(2,1)} %collective-permute-done.8.b_ref), custom_call_target="tpu_custom_call" | custom-call | bytes 2621440 | tf_op jit(solution)/shard_map/pallas_call | solution.py:99
  160.6 5.7 %all-to-all-start = ((bf16[16,320,128]{2,1,0:T(8,128)(2,1)}), bf16[16,320,128]{2,1,0:T(8,128)(2,1)S(1)}, u32[]{:S(2)}, u32[]{:S(2)}) async-start(bf16[16,320,128]{2,1,0:T(8,128)(2,1)} %shard_map.121), calls=%async_computation | async-start | bytes 2621440 | tf_op jit(solution)/shard_map/all_to_all | solution.py:476
  166.3 2.1 collective-permute-start.20
  168.4 2.4 %collective-permute-start.31 = (f32[64,320]{1,0:T(8,128)S(1)}, f32[64,320]{1,0:T(8,128)S(1)}, u32[]{:S(2)}, u32[]{:S(2)}) collective-permute-start(f32[64,320]{1,0:T(8,128)S(1)} %add.135), channel_id=1, source_target_pairs={{0,16},{4,20},{8,24},{12,28},{16,0},{20,4},{24,8},{28,12},{1,17},{... | collective-permute-start | bytes 245768 | tf_op jit(solution)/shard_map/ppermute | solution.py:25
  171.1 29.8 %collective-permute-done.31 = f32[64,320]{1,0:T(8,128)S(1)} collective-permute-done((f32[64,320]{1,0:T(8,128)S(1)}, f32[64,320]{1,0:T(8,128)S(1)}, u32[]{:S(2)}, u32[]{:S(2)}) %collective-permute-start.31) | collective-permute-done | bytes 81952 | tf_op jit(solution)/shard_map/ppermute | solution.py:25
  200.9 1.6 collective-permute-start.32
  203.0 2.5 %collective-permute-done.32.refs_2_ = f32[64,320]{1,0:T(8,128)S(1)} collective-permute-done((f32[64,320]{1,0:T(8,128)S(1)}, f32[64,320]{1,0:T(8,128)S(1)}, u32[]{:S(2)}, u32[]{:S(2)}) %collective-permute-start.32) | collective-permute-done | bytes 81952 | tf_op jit(solution)/shard_map/ppermute | solution.py:25
  205.7 4.7 %collective-permute-done.21 = bf16[64,1280]{1,0:T(8,128)(2,1)S(1)} collective-permute-done((bf16[64,1280]{1,0:T(8,128)(2,1)S(1)}, bf16[64,1280]{1,0:T(8,128)(2,1)S(1)}, u32[]{:S(2)}, u32[]{:S(2)}) %collective-permute-start.21) | collective-permute-done | bytes 163872 | tf_op jit(solution)/shard_map/ppermute | solution.py:25
  210.4 4.8 %shard_map.125 = (f32[64,1280]{1,0:T(8,128)}, f32[1280,1280]{1,0:T(8,128)}) custom-call(s32[1]{0:T(128)} %bitcast.1.me_ref, f32[64,64]{1,0:T(8,128)S(1)} %fusion.8.inv_ref, f32[64,1280]{1,0:T(8,128)S(1)} %fusion.25.basis_ref, f32[64,1280]{1,0:T(8,128)S(1)} %convert_add_fusion.1.refs_0_), custom_call_target="tpu_custom_call" | custom-call | flops 629145600 | bytes 7553024 | tf_op jit(solution)/shard_map/pallas_call | solution.py:99
  215.2 4.8 %shard_map.127 = (f32[64,1280]{1,0:T(8,128)}, f32[1280,1280]{1,0:T(8,128)}) custom-call(s32[1]{0:T(128)} %bitcast.1.me_ref, f32[64,64]{1,0:T(8,128)S(1)} %fusion.6.inv_ref, f32[64,1280]{1,0:T(8,128)S(1)} %copy-done.11, f32[64,320]{1,0:T(8,128)S(1)} %add.136.refs_0_, f32[64,320]{1,0:T(8,128)S(1)} %get-tuple-element.58.refs_1_, ...), custom_call_target="tpu_custom_call" | custom-call | flops 629145600 | bytes 7553024 | tf_op jit(solution)/shard_map/pallas_call | solution.py:99
  220.0 1.8 shard_map.122
  (150 shorter events, 23.0 us)
Async XLA Ops:
  0.6 33.0 %collective-permute-start.3 = (bf16[320,1024]{1,0:T(8,128)(2,1)}, bf16[320,1024]{1,0:T(8,128)(2,1)S(1)}, u32[]{:S(2)}, u32[]{:S(2)}) collective-permute-start(bf16[320,1024]{1,0:T(8,128)(2,1)} %bitcast.85), channel_id=1, source_target_pairs={{0,1},{1,0},{2,3},{3,2},{4,5},{5,4},{6,7},{7,6},{8,9},{9,8},{10,11... | collective-permute-start | bytes 1966088 | tf_op jit(solution)/shard_map/ppermute | solution.py:25
  1.2 24.0 %collective-permute-start.4 = (bf16[320,1024]{1,0:T(8,128)(2,1)}, bf16[320,1024]{1,0:T(8,128)(2,1)S(1)}, u32[]{:S(2)}, u32[]{:S(2)}) collective-permute-start(bf16[320,1024]{1,0:T(8,128)(2,1)} %bitcast.86), channel_id=1, source_target_pairs={{0,2},{1,3},{2,0},{3,1},{4,6},{5,7},{6,4},{7,5},{8,10},{9,11},{10,... | collective-permute-start | bytes 1966088 | tf_op jit(solution)/shard_map/ppermute | solution.py:25
  3.8 50.4 %collective-permute-start.9 = (bf16[320,1024]{1,0:T(8,128)(2,1)}, bf16[320,1024]{1,0:T(8,128)(2,1)}, u32[]{:S(2)}, u32[]{:S(2)}) collective-permute-start(bf16[320,1024]{1,0:T(8,128)(2,1)} %bitcast.90), channel_id=1, source_target_pairs={{0,1},{1,0},{2,3},{3,2},{4,5},{5,4},{6,7},{7,6},{8,9},{9,8},{10,11... | collective-permute-start | bytes 1966088 | tf_op jit(solution)/shard_map/ppermute | solution.py:25
  3.9 29.5 %collective-permute-start.10 = (bf16[320,1024]{1,0:T(8,128)(2,1)}, bf16[320,1024]{1,0:T(8,128)(2,1)}, u32[]{:S(2)}, u32[]{:S(2)}) collective-permute-start(bf16[320,1024]{1,0:T(8,128)(2,1)} %bitcast.91), channel_id=1, source_target_pairs={{0,2},{1,3},{2,0},{3,1},{4,6},{5,7},{6,4},{7,5},{8,10},{9,11},{10,... | collective-permute-start | bytes 1966088 | tf_op jit(solution)/shard_map/ppermute | solution.py:25
  4.9 13.8 %collective-permute-start = (s32[8,8]{1,0:T(8,128)S(1)}, s32[8,8]{1,0:T(8,128)S(1)}, u32[]{:S(2)}, u32[]{:S(2)}) collective-permute-start(s32[8,8]{1,0:T(8,128)S(1)} %broadcast_select_fusion.12), channel_id=1, source_target_pairs={{0,4},{4,0},{8,12},{12,8},{16,20},{20,16},{24,28},{28,24},{1,5},{5... | collective-permute-start | bytes 776 | tf_op jit(solution)/shard_map/ppermute | solution.py:25
  9.1 9.6 %copy-start.23 = (s32[8]{0:T(128)S(1)}, s32[8]{0:T(128)}, u32[]{:S(2)}) copy-start(s32[8]{0:T(128)} %param.13) | copy-start | bytes 100
  9.1 24.6 %copy-start.1 = (bf16[1024,320]{0,1:T(8,128)(2,1)S(1)}, bf16[1024,320]{0,1:T(8,128)(2,1)}, u32[]{:S(2)}) copy-start(bf16[1024,320]{0,1:T(8,128)(2,1)} %param.11) | copy-start | bytes 1966084
  9.1 24.6 %copy-start.14 = (s32[8]{0:T(128)S(1)}, s32[8]{0:T(128)}, u32[]{:S(2)}) copy-start(s32[8]{0:T(128)} %fill_ref.7) | copy-start | bytes 100
  18.9 3.7 %collective-permute-start.1 = (s32[8,8]{1,0:T(8,128)S(1)}, s32[8,8]{1,0:T(8,128)S(1)}, u32[]{:S(2)}, u32[]{:S(2)}) collective-permute-start(s32[8,8]{1,0:T(8,128)S(1)} %get-tuple-element.62), channel_id=1, source_target_pairs={{0,8},{4,12},{8,0},{12,4},{16,24},{20,28},{24,16},{28,20},{1,9},{5... | collective-permute-start | bytes 776 | tf_op jit(solution)/shard_map/ppermute | solution.py:25
  22.6 4.5 %collective-permute-start.2 = (s32[8,8]{1,0:T(8,128)S(1)}, s32[8,8]{1,0:T(8,128)S(1)}, u32[]{:S(2)}, u32[]{:S(2)}) collective-permute-start(s32[8,8]{1,0:T(8,128)S(1)} %add.112), channel_id=1, source_target_pairs={{0,16},{4,20},{8,24},{12,28},{16,0},{20,4},{24,8},{28,12},{1,17},{... | collective-permute-start | bytes 776 | tf_op jit(solution)/shard_map/ppermute | solution.py:25
  25.2 8.5 %collective-permute-start.5 = (bf16[320,1024]{1,0:T(8,128)(2,1)S(1)}, bf16[320,1024]{1,0:T(8,128)(2,1)S(1)}, u32[]{:S(2)}, u32[]{:S(2)}) collective-permute-start(bf16[320,1024]{1,0:T(8,128)(2,1)S(1)} %collective-permute-done.4.refs_2_.refs_6_), channel_id=1, source_target_pairs={{0,1},{1,0},{2,3},{3,2},{4,5},{5,4},{6,7},{7,6},{8,9},{9,8},{10,11... | collective-permute-start | bytes 1966088 | tf_op jit(solution)/shard_map/ppermute | solution.py:25
  33.5 20.7 %collective-permute-start.11 = (bf16[320,1024]{1,0:T(8,128)(2,1)}, bf16[320,1024]{1,0:T(8,128)(2,1)S(1)}, u32[]{:S(2)}, u32[]{:S(2)}) collective-permute-start(bf16[320,1024]{1,0:T(8,128)(2,1)} %collective-permute-done.10.refs_2_.refs_4_), channel_id=1, source_target_pairs={{0,1},{1,0},{2,3},{3,2},{4,5},{5,4},{6,7},{7,6},{8,9},{9,8},{10,11... | collective-permute-start | bytes 1966088 | tf_op jit(solution)/shard_map/ppermute | solution.py:25
  33.7 18.8 %copy-start.2 = (bf16[320,1024]{1,0:T(8,128)(2,1)}, bf16[320,1024]{1,0:T(8,128)(2,1)S(1)}, u32[]{:S(2)}) copy-start(bf16[320,1024]{1,0:T(8,128)(2,1)S(1)} %collective-permute-done.5.refs_3_.refs_7_) | copy-start | bytes 1966084
  33.7 20.5 %copy-start.4 = (bf16[1024,320]{0,1:T(8,128)(2,1)S(1)}, bf16[1024,320]{0,1:T(8,128)(2,1)}, u32[]{:S(2)}) copy-start(bf16[1024,320]{0,1:T(8,128)(2,1)} %param.12) | copy-start | bytes 1966084
  67.2 30.5 %copy-start = (bf16[1280,1024]{1,0:T(8,128)(2,1)S(1)}, bf16[1280,1024]{1,0:T(8,128)(2,1)}, u32[]{:S(2)}) copy-start(bf16[1280,1024]{1,0:T(8,128)(2,1)} %get-tuple-element.33.refs_9_.refs_1_) | copy-start | bytes 7864324
  67.2 2.3 %collective-permute-start.12 = (f32[2,64,320]{2,1,0:T(8,128)S(1)}, f32[2,64,320]{2,1,0:T(8,128)S(1)}, u32[]{:S(2)}, u32[]{:S(2)}) collective-permute-start(f32[2,64,320]{2,1,0:T(8,128)S(1)} %get-tuple-element.36), channel_id=1, source_target_pairs={{0,1},{1,0},{2,3},{3,2},{4,5},{5,4},{6,7},{7,6},{8,9},{9,8},{10,11... | collective-permute-start | bytes 491528 | tf_op jit(solution)/shard_map/ppermute | solution.py:25
  67.8 6.2 %collective-permute-start.22 = (bf16[64,1280]{1,0:T(8,128)(2,1)S(1)}, bf16[64,1280]{1,0:T(8,128)(2,1)S(1)}, u32[]{:S(2)}, u32[]{:S(2)}) collective-permute-start(bf16[64,1280]{1,0:T(8,128)(2,1)S(1)} %convert_element_type.126), channel_id=1, source_target_pairs={{0,4},{4,0},{8,12},{12,8},{16,20},{20,16},{24,28},{28,24},{1,5},{5... | collective-permute-start | bytes 491528 | tf_op jit(solution)/shard_map/ppermute | solution.py:25
  69.6 6.3 %collective-permute-start.13 = (f32[1,64,320]{2,1,0:T(8,128)S(1)}, f32[1,64,320]{2,1,0:T(8,128)S(1)}, u32[]{:S(2)}, u32[]{:S(2)}) collective-permute-start(f32[1,64,320]{2,1,0:T(8,128)S(1)} %slice_bitcast_fusion.6), channel_id=1, source_target_pairs={{0,2},{1,3},{2,0},{3,1},{4,6},{5,7},{6,4},{7,5},{8,10},{9,11},{10,... | collective-permute-start | bytes 245768 | tf_op jit(solution)/shard_map/ppermute | solution.py:25
  74.0 6.9 %collective-permute-start.23 = (bf16[64,1280]{1,0:T(8,128)(2,1)S(1)}, bf16[64,1280]{1,0:T(8,128)(2,1)S(1)}, u32[]{:S(2)}, u32[]{:S(2)}) collective-permute-start(bf16[64,1280]{1,0:T(8,128)(2,1)S(1)} %add_convert_fusion.3), channel_id=1, source_target_pairs={{0,8},{4,12},{8,0},{12,4},{16,24},{20,28},{24,16},{28,20},{1,9},{5... | collective-permute-start | bytes 491528 | tf_op jit(solution)/shard_map/ppermute | solution.py:25
  75.9 4.7 %collective-permute-start.14 = (f32[64,320]{1,0:T(8,128)S(1)}, f32[64,320]{1,0:T(8,128)S(1)}, u32[]{:S(2)}, u32[]{:S(2)}) collective-permute-start(f32[64,320]{1,0:T(8,128)S(1)} %fusion.5), channel_id=1, source_target_pairs={{0,4},{4,0},{8,12},{12,8},{16,20},{20,16},{24,28},{28,24},{1,5},{5... | collective-permute-start | bytes 245768 | tf_op jit(solution)/shard_map/ppermute | solution.py:25
  80.6 4.7 %collective-permute-start.15 = (f32[64,320]{1,0:T(8,128)S(1)}, f32[64,320]{1,0:T(8,128)S(1)}, u32[]{:S(2)}, u32[]{:S(2)}) collective-permute-start(f32[64,320]{1,0:T(8,128)S(1)} %add.121), channel_id=1, source_target_pairs={{0,8},{4,12},{8,0},{12,4},{16,24},{20,28},{24,16},{28,20},{1,9},{5... | collective-permute-start | bytes 245768 | tf_op jit(solution)/shard_map/ppermute | solution.py:25
  80.9 16.2 %copy-start.18 = (bf16[64,1280]{1,0:T(8,128)(2,1)}, bf16[64,1280]{1,0:T(8,128)(2,1)S(1)}, u32[]{:S(2)}) copy-start(bf16[64,1280]{1,0:T(8,128)(2,1)S(1)} %add_convert_fusion.2) | copy-start | bytes 491524
  80.9 14.5 %collective-permute-start.24 = (bf16[64,1280]{1,0:T(8,128)(2,1)S(1)}, bf16[64,1280]{1,0:T(8,128)(2,1)S(1)}, u32[]{:S(2)}, u32[]{:S(2)}) collective-permute-start(bf16[64,1280]{1,0:T(8,128)(2,1)S(1)} %add_convert_fusion.2), channel_id=1, source_target_pairs={{0,16},{4,20},{8,24},{12,28},{16,0},{20,4},{24,8},{28,12},{1,17},{... | collective-permute-start | bytes 491528 | tf_op jit(solution)/shard_map/ppermute | solution.py:25
  85.3 8.5 %collective-permute-start.16 = (f32[64,320]{1,0:T(8,128)S(1)}, f32[64,320]{1,0:T(8,128)S(1)}, u32[]{:S(2)}, u32[]{:S(2)}) collective-permute-start(f32[64,320]{1,0:T(8,128)S(1)} %add.122), channel_id=1, source_target_pairs={{0,16},{4,20},{8,24},{12,28},{16,0},{20,4},{24,8},{28,12},{1,17},{... | collective-permute-start | bytes 245768 | tf_op jit(solution)/shard_map/ppermute | solution.py:25
  89.0 39.9 %collective-permute-start.6 = (bf16[320,1024]{1,0:T(8,128)(2,1)}, bf16[320,1024]{1,0:T(8,128)(2,1)}, u32[]{:S(2)}, u32[]{:S(2)}) collective-permute-start(bf16[320,1024]{1,0:T(8,128)(2,1)} %get-tuple-element.29), channel_id=1, source_target_pairs={{0,1},{1,0},{2,3},{3,2},{4,5},{5,4},{6,7},{7,6},{8,9},{9,8},{10,11... | collective-permute-start | bytes 1966088 | tf_op jit(solution)/shard_map/ppermute | solution.py:25
  89.0 33.2 %collective-permute-start.7 = (bf16[320,1024]{1,0:T(8,128)(2,1)}, bf16[320,1024]{1,0:T(8,128)(2,1)}, u32[]{:S(2)}, u32[]{:S(2)}) collective-permute-start(bf16[320,1024]{1,0:T(8,128)(2,1)} %get-tuple-element.31), channel_id=1, source_target_pairs={{0,1},{1,0},{2,3},{3,2},{4,5},{5,4},{6,7},{7,6},{8,9},{9,8},{10,11... | collective-permute-start | bytes 1966088 | tf_op jit(solution)/shard_map/ppermute | solution.py:25
  93.8 27.8 %collective-permute-start.17 = (f32[64,320]{1,0:T(8,128)S(1)}, f32[64,320]{1,0:T(8,128)S(1)}, u32[]{:S(2)}, u32[]{:S(2)}) collective-permute-start(f32[64,320]{1,0:T(8,128)S(1)} %add.123.refs_0_), channel_id=1, source_target_pairs={{0,2},{1,3},{2,0},{3,1},{4,6},{5,7},{6,4},{7,5},{8,10},{9,11},{10,... | collective-permute-start | bytes 245768 | tf_op jit(solution)/shard_map/ppermute | solution.py:25
  95.8 1.3 collective-permute-start.25
  97.1 25.1 %copy-start.10 = (bf16[320,1024]{1,0:T(8,128)(2,1)S(1)}, bf16[320,1024]{1,0:T(8,128)(2,1)}, u32[]{:S(2)}) copy-start(bf16[320,1024]{1,0:T(8,128)(2,1)} %copy-done.9) | copy-start | bytes 1966084
  97.2 7.1 %collective-permute-start.26 = (f32[64,64]{0,1:T(8,128)S(1)}, f32[64,64]{0,1:T(8,128)S(1)}, u32[]{:S(2)}, u32[]{:S(2)}) collective-permute-start(f32[64,64]{0,1:T(8,128)S(1)} %add.130), channel_id=1, source_target_pairs={{0,2},{1,3},{2,0},{3,1},{4,6},{5,7},{6,4},{7,5},{8,10},{9,11},{10,... | collective-permute-start | bytes 49160 | tf_op jit(solution)/shard_map/ppermute | solution.py:25
  104.3 24.5 %copy-start.8 = (bf16[320,1024]{1,0:T(8,128)(2,1)S(1)}, bf16[320,1024]{1,0:T(8,128)(2,1)}, u32[]{:S(2)}) copy-start(bf16[320,1024]{1,0:T(8,128)(2,1)} %copy-done.7) | copy-start | bytes 1966084
  104.3 21.7 %collective-permute-start.27 = (f32[2,64,320]{2,1,0:T(8,128)}, f32[2,64,320]{2,1,0:T(8,128)}, u32[]{:S(2)}, u32[]{:S(2)}) collective-permute-start(f32[2,64,320]{2,1,0:T(8,128)} %get-tuple-element.41), channel_id=1, source_target_pairs={{0,1},{1,0},{2,3},{3,2},{4,5},{5,4},{6,7},{7,6},{8,9},{9,8},{10,11... | collective-permute-start | bytes 491528 | tf_op jit(solution)/shard_map/ppermute | solution.py:25
  118.5 7.5 %copy-start.13 = (f32[2,64,320]{2,1,0:T(8,128)S(1)}, f32[2,64,320]{2,1,0:T(8,128)}, u32[]{:S(2)}) copy-start(f32[2,64,320]{2,1,0:T(8,128)} %copy-done.12) | copy-start | bytes 491524
  121.7 9.3 %collective-permute-start.18 = (f32[2,64,320]{2,1,0:T(8,128)S(1)}, f32[2,64,320]{2,1,0:T(8,128)S(1)}, u32[]{:S(2)}, u32[]{:S(2)}) collective-permute-start(f32[2,64,320]{2,1,0:T(8,128)S(1)} %pad_maximum_fusion.2), channel_id=1, source_target_pairs={{0,1},{1,0},{2,3},{3,2},{4,5},{5,4},{6,7},{7,6},{8,9},{9,8},{10,11... | collective-permute-start | bytes 491528 | tf_op jit(solution)/shard_map/ppermute | solution.py:25
  124.4 31.6 %collective-permute-start.8 = (bf16[320,1024]{1,0:T(8,128)(2,1)}, bf16[320,1024]{1,0:T(8,128)(2,1)}, u32[]{:S(2)}, u32[]{:S(2)}) collective-permute-start(bf16[320,1024]{1,0:T(8,128)(2,1)} %add_convert_fusion), channel_id=1, source_target_pairs={{0,2},{1,3},{2,0},{3,1},{4,6},{5,7},{6,4},{7,5},{8,10},{9,11},{10,... | collective-permute-start | bytes 1966088 | tf_op jit(solution)/shard_map/ppermute | solution.py:25
  125.9 14.1 %copy-start.3 = (bf16[320,1024]{1,0:T(8,128)(2,1)S(1)}, bf16[320,1024]{1,0:T(8,128)(2,1)}, u32[]{:S(2)}) copy-start(bf16[320,1024]{1,0:T(8,128)(2,1)} %copy-done.2) | copy-start | bytes 1966084
  128.3 19.5 %collective-permute-start.28 = (f32[1,64,320]{2,1,0:T(8,128)}, f32[1,64,320]{2,1,0:T(8,128)}, u32[]{:S(2)}, u32[]{:S(2)}) collective-permute-start(f32[1,64,320]{2,1,0:T(8,128)} %slice_bitcast_fusion.2), channel_id=1, source_target_pairs={{0,2},{1,3},{2,0},{3,1},{4,6},{5,7},{6,4},{7,5},{8,10},{9,11},{10,... | collective-permute-start | bytes 245768 | tf_op jit(solution)/shard_map/ppermute | solution.py:25
  146.3 20.0 %collective-permute-start.19 = (bf16[64,1280]{1,0:T(8,128)(2,1)S(1)}, bf16[64,1280]{1,0:T(8,128)(2,1)S(1)}, u32[]{:S(2)}, u32[]{:S(2)}) collective-permute-start(bf16[64,1280]{1,0:T(8,128)(2,1)S(1)} %convert_element_type.117), channel_id=1, source_target_pairs={{0,4},{4,0},{8,12},{12,8},{16,20},{20,16},{24,28},{28,24},{1,5},{5... | collective-permute-start | bytes 491528 | tf_op jit(solution)/shard_map/ppermute | solution.py:25
  148.7 6.8 %collective-permute-start.29 = (f32[64,320]{1,0:T(8,128)S(1)}, f32[64,320]{1,0:T(8,128)S(1)}, u32[]{:S(2)}, u32[]{:S(2)}) collective-permute-start(f32[64,320]{1,0:T(8,128)S(1)} %fusion.3), channel_id=1, source_target_pairs={{0,4},{4,0},{8,12},{12,8},{16,20},{20,16},{24,28},{28,24},{1,5},{5... | collective-permute-start | bytes 245768 | tf_op jit(solution)/shard_map/ppermute | solution.py:25
  155.6 12.8 %collective-permute-start.30 = (f32[64,320]{1,0:T(8,128)S(1)}, f32[64,320]{1,0:T(8,128)S(1)}, u32[]{:S(2)}, u32[]{:S(2)}) collective-permute-start(f32[64,320]{1,0:T(8,128)S(1)} %add.134), channel_id=1, source_target_pairs={{0,8},{4,12},{8,0},{12,4},{16,24},{20,28},{24,16},{28,20},{1,9},{5... | collective-permute-start | bytes 245768 | tf_op jit(solution)/shard_map/ppermute | solution.py:25
  160.6 42.1 %copy-start.17 = (f32[64,1280]{1,0:T(8,128)S(1)}, f32[64,1280]{1,0:T(8,128)}, u32[]{:S(2)}) copy-start(f32[64,1280]{1,0:T(8,128)} %copy-done.16) | copy-start | bytes 983044
  160.6 59.4 %all-to-all-start = ((bf16[16,320,128]{2,1,0:T(8,128)(2,1)}), bf16[16,320,128]{2,1,0:T(8,128)(2,1)S(1)}, u32[]{:S(2)}, u32[]{:S(2)}) async-start(bf16[16,320,128]{2,1,0:T(8,128)(2,1)} %shard_map.121), calls=%async_computation | async-start | bytes 2621440 | tf_op jit(solution)/shard_map/all_to_all | solution.py:476
  166.3 36.2 %collective-permute-start.20 = (bf16[64,1280]{1,0:T(8,128)(2,1)S(1)}, bf16[64,1280]{1,0:T(8,128)(2,1)S(1)}, u32[]{:S(2)}, u32[]{:S(2)}) collective-permute-start(bf16[64,1280]{1,0:T(8,128)(2,1)S(1)} %add_convert_fusion.5), channel_id=1, source_target_pairs={{0,8},{4,12},{8,0},{12,4},{16,24},{20,28},{24,16},{28,20},{1,9},{5... | collective-permute-start | bytes 491528 | tf_op jit(solution)/shard_map/ppermute | solution.py:25
  168.4 32.5 %collective-permute-start.31 = (f32[64,320]{1,0:T(8,128)S(1)}, f32[64,320]{1,0:T(8,128)S(1)}, u32[]{:S(2)}, u32[]{:S(2)}) collective-permute-start(f32[64,320]{1,0:T(8,128)S(1)} %add.135), channel_id=1, source_target_pairs={{0,16},{4,20},{8,24},{12,28},{16,0},{20,4},{24,8},{28,12},{1,17},{... | collective-permute-start | bytes 245768 | tf_op jit(solution)/shard_map/ppermute | solution.py:25
  171.1 44.1 %copy-start.11 = (f32[64,1280]{1,0:T(8,128)S(1)}, f32[64,1280]{1,0:T(8,128)}, u32[]{:S(2)}) copy-start(f32[64,1280]{1,0:T(8,128)} %fusion.22.basis_ref) | copy-start | bytes 983044
  200.9 4.7 %collective-permute-start.32 = (f32[64,320]{1,0:T(8,128)S(1)}, f32[64,320]{1,0:T(8,128)S(1)}, u32[]{:S(2)}, u32[]{:S(2)}) collective-permute-start(f32[64,320]{1,0:T(8,128)S(1)} %add.136.refs_0_), channel_id=1, source_target_pairs={{0,2},{1,3},{2,0},{3,1},{4,6},{5,7},{6,4},{7,5},{8,10},{9,11},{10,... | collective-permute-start | bytes 245768 | tf_op jit(solution)/shard_map/ppermute | solution.py:25
  202.5 7.8 %collective-permute-start.21 = (bf16[64,1280]{1,0:T(8,128)(2,1)S(1)}, bf16[64,1280]{1,0:T(8,128)(2,1)S(1)}, u32[]{:S(2)}, u32[]{:S(2)}) collective-permute-start(bf16[64,1280]{1,0:T(8,128)(2,1)S(1)} %add_convert_fusion.4), channel_id=1, source_target_pairs={{0,16},{4,20},{8,24},{12,28},{16,0},{20,4},{24,8},{28,12},{1,17},{... | collective-permute-start | bytes 491528 | tf_op jit(solution)/shard_map/ppermute | solution.py:25
  205.6 9.5 %collective-permute-start.33 = (f32[2,64,320]{2,1,0:T(8,128)S(1)}, f32[2,64,320]{2,1,0:T(8,128)S(1)}, u32[]{:S(2)}, u32[]{:S(2)}) collective-permute-start(f32[2,64,320]{2,1,0:T(8,128)S(1)} %pad_maximum_fusion.3), channel_id=1, source_target_pairs={{0,1},{1,0},{2,3},{3,2},{4,5},{5,4},{6,7},{7,6},{8,9},{9,8},{10,11... | collective-permute-start | bytes 491528 | tf_op jit(solution)/shard_map/ppermute | solution.py:25
  (11 other events, 23.3 us)

commit v2 on v1

--- a/solution.py
+++ b/solution.py
@@ -7,8 +7,10 @@
 from jax.experimental.pallas import tpu as pltpu
 from jax.sharding import PartitionSpec as P
 
+
 BLOCK = 128
-TILE = 256
+TILE = 512
+STRIP = 128
 CAP = 2
 EXTRA = 6
 bf16 = jnp.bfloat16
@@ -30,7 +32,8 @@
     pieces = {0: own}
     for bit in bits_of(count)[1:]:
         pieces.update({o | bit: swap(p, "mp", bit) for o, p in list(pieces.items())})
-    pieces.update({o | 1: swap(p, "mp", 1) for o, p in list(pieces.items())})
+    near = {o | 1: swap(p, "mp", 1) for o, p in pieces.items()}
+    pieces.update(near)
     return [pieces[o] for o in range(count)]
 
 
@@ -96,6 +99,10 @@
 def call(body, out_shape, args, scalars=(), grid=(1,), in_specs=None, out_specs=None, scratch=(), flops=0):
     moved = sum(a.size * a.dtype.itemsize for a in args)
     moved += sum(o.size * o.dtype.itemsize for o in jax.tree.leaves(out_shape))
+    return kernel_call(body, out_shape, args, scalars, grid, in_specs, out_specs, scratch, flops, moved)
+
+
+def kernel_call(body, out_shape, args, scalars, grid, in_specs, out_specs, scratch, flops, moved):
     return pl.pallas_call(
         body,
         out_shape=out_shape,
@@ -182,15 +189,16 @@
     x_refs, (up_t_ref, down_t_ref), refs = refs[:count], refs[count : count + 2], refs[count + 2 :]
     hidden_ref, slope_ref, out_refs, held = refs[0], refs[1], refs[2:-1], refs[-1]
     assemble(x_refs, held)
-    preact = dot(up_t_ref[...], held[...])
-    sig = jax.nn.sigmoid(1.702 * preact)
-    active = preact * sig
-    hidden_ref[...] = active.astype(bf16)
-    slope_ref[...] = (sig + 1.702 * active * (1.0 - sig)).astype(bf16)
-    out = mask_tokens(dot(down_t_ref[...], hidden_ref[...]), fill_ref).astype(bf16)
-    piece = out.shape[0] // count
+    for k in range(0, up_t_ref.shape[0], STRIP):
+        preact = dot(up_t_ref[k : k + STRIP, :], held[...])
+        sig = jax.nn.sigmoid(1.702 * preact)
+        active = preact * sig
+        hidden_ref[k : k + STRIP, :] = active.astype(bf16)
+        slope_ref[k : k + STRIP, :] = (sig + 1.702 * active * (1.0 - sig)).astype(bf16)
+    piece = down_t_ref.shape[0] // count
     for o, ref in enumerate(out_refs):
-        ref[...] = out[o * piece : (o + 1) * piece]
+        out = dot(down_t_ref[o * piece : (o + 1) * piece, :], hidden_ref[...])
+        ref[...] = mask_tokens(out.astype(bf16), fill_ref)
 
 
 def forward(xs, up_t, down_t, fill):
@@ -233,8 +241,9 @@
     assemble(c_refs, held_c)
     assemble(x_refs, held_x)
     held_c[...] = mask_tokens(held_c[...], fill_ref)
-    grad = dot(down_x_ref[...], held_c[...])
-    grad_ref[...] = (grad * slope_ref[...].astype(f32)).astype(bf16)
+    for k in range(0, down_x_ref.shape[0], STRIP):
+        grad = dot(down_x_ref[k : k + STRIP, :], held_c[...])
+        grad_ref[k : k + STRIP, :] = (grad * slope_ref[k : k + STRIP, :].astype(f32)).astype(bf16)
     t = fold(dot(qd_ref[...], held_c[...]))
     acc_down[...] += fold(dot(stacked(t), hidden_ref[...], (1, 1)))
     u = fold(dot(qu_ref[...], grad_ref[...]))
@@ -276,7 +285,6 @@
     first_refs, refs = refs[:n_first], refs[n_first:]
     second_refs, refs = refs[:n_second], refs[n_second:]
     out_refs, (left, first, second, acc) = refs[:-4], refs[-4:]
-    rank = left_refs[0].shape[0]
 
     @pl.when(pl.program_id(0) == 0)
     def _():
@@ -327,7 +335,61 @@
     )
 
 
-def outer_kernel(n_raw, me_ref, inv_ref, basis_ref, *refs):
+def eliminate(grams):
+    rank = grams[0].shape[0]
+    group = 4
+    wide = 2 * rank
+    row = lax.broadcasted_iota(jnp.int32, (rank, wide), 0)
+    column = lax.broadcasted_iota(jnp.int32, (rank, rank), 1)
+    one = (lax.broadcasted_iota(jnp.int32, (rank, rank), 0) == column).astype(f32)
+    state = [jnp.concatenate([g, one], axis=1) for g in grams]
+    scale = [jnp.ones((rank, wide), f32) for _ in grams]
+    for first in range(0, rank, group):
+        columns = [
+            [jnp.broadcast_to(m[:, first + k : first + k + 1], (rank, wide)) for k in range(group)]
+            for m in state
+        ]
+        for k in range(group):
+            j = first + k
+            for t in range(len(grams)):
+                pivot = columns[t][k][j : j + 1, :]
+                factor = jnp.where(row > j, columns[t][k] * (1.0 / pivot), 0.0)
+                state[t] = state[t] - factor * state[t][j : j + 1, :]
+                for q in range(k + 1, group):
+                    columns[t][q] = columns[t][q] - factor * columns[t][q][j : j + 1, :]
+                scale[t] = jnp.where(row == j, lax.rsqrt(pivot), scale[t])
+    return [(m * c)[:, rank:] for m, c in zip(state, scale)]
+
+
+def factor_kernel(count, me_ref, gram_ref, down_ref, *refs):
+    up_refs, outs = refs[:count], refs[count:]
+    up = jnp.concatenate([r[...] for r in up_refs], axis=1)
+    gram_up = dot(up, up, (1, 1), HIGHEST)
+    inverses = eliminate([gram_up, gram_ref[...]])
+    natural = jnp.concatenate(reorder([r[...] for r in up_refs], me_ref[0]), axis=1)
+    for t, proj in enumerate((natural, down_ref[...])):
+        outs[t][...] = inverses[t]
+        head, tail = head_tail(dot(inverses[t], proj, precision=HIGHEST))
+        outs[2 + t][...] = jnp.concatenate([head, head, tail], axis=0).T
+
+
+def factor(proj_up, proj_down, gram_down, me):
+    rank, units = proj_down.shape
+    features = sum(p.shape[1] for p in proj_up)
+    outs = [struct((rank, rank), f32)] * 2 + [struct((features, 3 * rank), bf16), struct((units, 3 * rank), bf16)]
+    args = (gram_down, proj_down, *proj_up)
+    return call(
+        functools.partial(factor_kernel, len(proj_up)),
+        outs,
+        args,
+        (me.reshape(1),),
+        in_specs=[whole(a) for a in args],
+        out_specs=[whole(o) for o in outs],
+        flops=1 << 28,
+    )
+
+
+def outer_kernel(n_raw, me_ref, inv_ref, left_ref, *refs):
     raw_refs, (fresh_ref, approx_ref, right) = refs[:n_raw], refs[n_raw:]
 
     @pl.when(pl.program_id(0) == 0)
@@ -338,28 +400,24 @@
         head, tail = head_tail(fresh)
         right[...] = jnp.concatenate([head, tail, head], axis=0)
 
-    head, tail = head_tail(basis_ref[...])
-    approx_ref[...] = dot(jnp.concatenate([head, head, tail], axis=0), right[...], (0, 0))
-
-
-def outer(inv, basis, raws, me):
-    rank, rows = basis.shape
+    approx_ref[...] = dot(left_ref[...], right[...])
+
+
+def outer(inv, left, raws, me):
+    rows, triple = left.shape
     columns = sum(r.shape[1] for r in raws)
-    outs = [struct((rank, columns), f32), struct((rows, columns), f32)]
+    strip = 2 * BLOCK if rows % (2 * BLOCK) == 0 else BLOCK
+    outs = [struct((triple // 3, columns), f32), struct((rows, columns), f32)]
     return call(
         functools.partial(outer_kernel, len(raws)),
         outs,
-        (inv, basis, *raws),
+        (inv, left, *raws),
         (me.reshape(1),),
-        grid=(rows // BLOCK // 2 if rows % (2 * BLOCK) == 0 else rows // BLOCK,),
-        in_specs=[whole(inv), pl.BlockSpec((rank, 2 * BLOCK if rows % (2 * BLOCK) == 0 else BLOCK), lambda i, *_: (0, i))]
-        + [whole(r) for r in raws],
-        out_specs=[
-            whole(outs[0]),
-            pl.BlockSpec((2 * BLOCK if rows % (2 * BLOCK) == 0 else BLOCK, columns), lambda i, *_: (i, 0)),
-        ],
-        scratch=[pltpu.VMEM((3 * rank, columns), bf16)],
-        flops=6 * rank * rows * columns,
+        grid=(rows // strip,),
+        in_specs=[whole(inv), pl.BlockSpec((strip, triple), lambda i, *_: (i, 0))] + [whole(r) for r in raws],
+        out_specs=[whole(outs[0]), pl.BlockSpec((strip, columns), lambda i, *_: (i, 0))],
+        scratch=[pltpu.VMEM((triple, columns), bf16)],
+        flops=2 * triple * rows * columns,
     )
 
 
@@ -420,11 +478,6 @@
     return table.reshape(-1)
 
 
-def inverse_factor(gram):
-    lower = jnp.linalg.cholesky(gram)
-    return jax.scipy.linalg.solve_triangular(lower, jnp.eye(gram.shape[0], dtype=f32), lower=True)
-
-
 def split_rows(x):
     head = lax.reduce_precision(x, 8, 7)
     return jnp.concatenate([head.astype(bf16), (x - head).astype(bf16)], axis=0)
@@ -446,27 +499,8 @@
     hidden, slope, outs = forward(xs, up_t, down_t, block_fill)
     grad_pre, even, odd, proj_down = backward(cs, xs, slope, hidden, down_x, qu, qd, block_fill)
 
-    proj_down = sum_over(proj_down, "dp", bf16)
-    proj_up = spread_mp(sum_over(reduce_mp(even, odd), "dp", f32))
-
-    even, odd = two_sided([proj_down], [hidden], cs, block_fill, True)
-    (raw_up,) = two_sided(proj_up, xs, [grad_pre], block_fill, False)
-    proj_up = jnp.concatenate(reorder(proj_up, me), axis=1)
-
-    gram_up = jnp.dot(proj_up, proj_up.T, precision=HIGHEST)
-    gram_down = sum_over(jnp.dot(proj_down, proj_down.T, precision=HIGHEST), "mp", f32)
-    inv_up = inverse_factor(gram_up)
-    inv_down = inverse_factor(gram_down)
-    basis_up = jnp.dot(inv_up, proj_up, precision=HIGHEST)
-    basis_down = jnp.dot(inv_down, proj_down, precision=HIGHEST)
-
-    raw_up = sum_over(raw_up, "dp", bf16)
-    raw_down = spread_mp(sum_over(reduce_mp(even, odd), "dp", f32))
-    fresh_up, approx_up = outer(inv_up, basis_up, [raw_up], me)
-    fresh_down, approx_down = outer(inv_down, basis_down, raw_down, me)
-
-    have = dict(enumerate(outs))
-    have = {o - 1: (have[o - 1].astype(f32) + swap(have[o], "mp", 1).astype(f32)).astype(bf16) for o in have if o & 1}
+    have = {o: outs[o].astype(f32) for o in range(0, count, 2)}
+    have = {o: (h + swap(outs[o | 1], "mp", 1).astype(f32)).astype(bf16) for o, h in have.items()}
     for bit in bits_of(count)[1:]:
         got = {o ^ bit: swap(have[o], "mp", bit) for o in have if o & bit}
         if len(got) == 1:
@@ -475,6 +509,22 @@
     sent = pack(have[0], got[0], send_plan(encoder_rank, ranks_dp))
     received = lax.all_to_all(sent, "dp", split_axis=0, concat_axis=0, tiled=True)
     encoded = unpack(received, *recv_plan(every, blocks, me_dp, blocks + EXTRA))
+
+    proj_down = sum_over(proj_down, "dp", bf16)
+    proj_up = sum_over(reduce_mp(even, odd), "dp", f32)
+    proj_up = spread_mp(proj_up)
+
+    even, odd = two_sided([proj_down], [hidden], cs, block_fill, True)
+    (raw_up,) = two_sided(proj_up, xs, [grad_pre], block_fill, False)
+
+    gram_down = sum_over(dot(proj_down, proj_down, (1, 1), HIGHEST), "mp", f32)
+    inv_up, inv_down, left_up, left_down = factor(proj_up, proj_down, gram_down, me)
+
+    raw_down = sum_over(reduce_mp(even, odd), "dp", f32)
+    raw_up = sum_over(raw_up, "dp", bf16)
+    raw_down = spread_mp(raw_down)
+    fresh_up, approx_up = outer(inv_up, left_up, [raw_up], me)
+    fresh_down, approx_down = outer(inv_down, left_down, raw_down, me)
     return (encoded.T, approx_up, approx_down, fresh_up.T, fresh_down.T)
 
 

time: 223 us -> 175 us (0.78)
  other arithmetic: 37.4 us -> 4.82 us
  local copies, waits for them, and re-layouts: 10.6 us -> 1.98 us
  Pallas kernels: 64.8 us -> 56.3 us
  waiting for transfers between devices: 59.7 us -> 65.9 us
  matrix products: 4.65 us -> 0.41 us
    another operation x10 -> x0, other arithmetic: 25.5 us -> none  [the longest x6 13.8 us: inverse_factor(): lower = jnp.linalg.cholesky(gram)]
    pallas_call x9 -> x10, Pallas kernels: 64.8 us -> 56.3 us  [kernel_call(): pl.pallas_call(body, out_shape=out_shape, grid_spec=pltpu.PrefetchScalarG...]
    ppermute x34, waiting for transfers between devices: 59.7 us -> 65.9 us  [swap(): return lax.ppermute(x, axis, [(i, i ^ bit) for i in range(count)])]
    unnamed x48 -> x18, local copies, waits for them, and re-layouts: 7.58 us -> 1.72 us
    convert_element_type x2, other arithmetic: 4.33 us -> 0.48 us  [local(): (h + swap(outs[o | 1], 'mp', 1).astype(f32)).astype(bf16)]
    dot_general x4 -> x1, matrix products: 3.38 us -> 0.41 us  [dot(): lax.dot_general(a, b, dims, preferred_element_type=f32, precision=precision)]
    ppermute x34, starting transfers between devices: 37.8 us -> 40.5 us  [swap(): return lax.ppermute(x, axis, [(i, i ^ bit) for i in range(count)])]
  transfers between devices with their start and end apart: 35 -> 35, of which waited for: 11 -> 12; matrix products, arithmetic and copies ran while one was open for 20% -> 3% of each run, Pallas kernels for 23% -> 25%
where the time goes in v2:
time: 175 us
  waiting for transfers between devices  65.9 us (38%)
  Pallas kernels  56.3 us (32%)
  starting transfers between devices  44.3 us (25%)
  other arithmetic  4.82 us (3%)
  local copies, waits for them, and re-layouts  1.98 us (1%)
    ppermute x34, waiting for transfers between devices, swap(): return lax.ppermute(x, axis, [(i, i ^ bit) for i in range(count)])  65.9 us
    pallas_call x10, Pallas kernels, kernel_call(): pl.pallas_call(body, out_shape=out_shape, grid_spec=pltpu.PrefetchScalarG...  56.3 us
    ppermute x34, starting transfers between devices, swap(): return lax.ppermute(x, axis, [(i, i ^ bit) for i in range(count)])  40.5 us
    all_to_all x1, starting transfers between devices, local(): lax.all_to_all(sent, 'dp', split_axis=0, concat_axis=0, tiled=True)  3.82 us
  transfers between devices with their start and end apart: 35, of which 12 were waited for; matrix products, arithmetic and copies ran while one was open for 3% of the time, Pallas kernels for 25%

profile of v2, /device:TPU:0, one launch (start us, length us, event | category | flops | bytes accessed | tf_op | source)
XLA Modules:
  0.0 174.8 jit_solution(1009116951715677379)
XLA Ops:
  1.2 2.6 %collective-permute-start.4 = (bf16[320,1024]{1,0:T(8,128)(2,1)}, bf16[320,1024]{1,0:T(8,128)(2,1)S(1)}, u32[]{:S(2)}, u32[]{:S(2)}) collective-permute-start(bf16[320,1024]{1,0:T(8,128)(2,1)} %bitcast.47), channel_id=1, source_target_pairs={{0,2},{1,3},{2,0},{3,1},{4,6},{5,7},{6,4},{7,5},{8,10},{9,11},{10,... | collective-permute-start | bytes 1966088 | tf_op jit(solution)/shard_map/ppermute | solution.py:27
  4.2 0.7 broadcast_select_fusion.4
  4.9 1.7 collective-permute-start
  6.7 1.0 reduce-precision_convert_fusion.1
  7.7 1.2 broadcast_select_fusion
  9.1 7.9 %shard_map.119 = (bf16[1280,1280]{1,0:T(8,128)(2,1)S(1)}, bf16[1280,1280]{1,0:T(8,128)(2,1)}, bf16[1280,1280]{1,0:T(8,128)(2,1)}) custom-call(s32[1]{0:T(128)} %bitcast.1.me_ref, bf16[1280,1280]{1,0:T(8,128)(2,1)} %up_ref.1, bf16[1280,1280]{1,0:T(8,128)(2,1)} %down_ref.1), custom_call_target="tpu_custom_call" | custom-call | bytes 16384000 | tf_op jit(solution)/shard_map/pallas_call | solution.py:106
  17.0 1.7 copy-done.7
  18.7 0.9 collective-permute-done.4.refs_2_.refs_6_
  19.8 2.1 %collective-permute-start.1 = (s32[8,8]{1,0:T(8,128)S(1)}, s32[8,8]{1,0:T(8,128)S(1)}, u32[]{:S(2)}, u32[]{:S(2)}) collective-permute-start(s32[8,8]{1,0:T(8,128)S(1)} %get-tuple-element.64), channel_id=1, source_target_pairs={{0,8},{4,12},{8,0},{12,4},{16,24},{20,28},{24,16},{28,20},{1,9},{5... | collective-permute-start | bytes 776 | tf_op jit(solution)/shard_map/ppermute | solution.py:27
  21.9 1.6 collective-permute-done.1
  23.5 3.0 %collective-permute-start.2 = (s32[8,8]{1,0:T(8,128)S(1)}, s32[8,8]{1,0:T(8,128)S(1)}, u32[]{:S(2)}, u32[]{:S(2)}) collective-permute-start(s32[8,8]{1,0:T(8,128)S(1)} %add.103), channel_id=1, source_target_pairs={{0,16},{4,20},{8,24},{12,28},{16,0},{20,4},{24,8},{28,12},{1,17},{... | collective-permute-start | bytes 776 | tf_op jit(solution)/shard_map/ppermute | solution.py:27
  26.6 1.5 collective-permute-done.2
  28.2 5.3 %collective-permute-done.10.refs_2_.refs_4_ = bf16[320,1024]{1,0:T(8,128)(2,1)} collective-permute-done((bf16[320,1024]{1,0:T(8,128)(2,1)}, bf16[320,1024]{1,0:T(8,128)(2,1)}, u32[]{:S(2)}, u32[]{:S(2)}) %collective-permute-start.10) | collective-permute-done | bytes 655392 | tf_op jit(solution)/shard_map/ppermute | solution.py:27
  33.5 12.5 %shard_map.120 = (bf16[1280,1024]{1,0:T(8,128)(2,1)}, bf16[1280,1024]{1,0:T(8,128)(2,1)}, bf16[320,1024]{1,0:T(8,128)(2,1)S(1)}, bf16[320,1024]{1,0:T(8,128)(2,1...) custom-call(s32[8]{0:T(128)S(1)} %copy-done.6, bf16[320,1024]{1,0:T(8,128)(2,1)S(1)} %bitcast.48, ...), custom_call_target="tpu_custom_call" | custom-call | flops 6710886400 | bytes 17039360 | tf_op jit(solution)/shard_map/pallas_call | solution.py:106
  46.1 11.4 %shard_map.123 = (bf16[1280,1024]{1,0:T(8,128)(2,1)}, f32[2,64,320]{2,1,0:T(8,128)S(1)}, f32[2,64,320]{2,1,0:T(8,128)S(1)}, f32[64,1280]{1,0:T(8,128)S(1)}) custom-call(s32[8]{0:T(128)S(1)} %copy-done.6, bf16[320,1024]{1,0:T(8,128)(2,1)S(1)} %bitcast.53, bf16[320,1024]{1,0:T(8,128)(2,1)} %collective-permute-done.9.refs_1_.refs_3_, ...), custom_call_target="tpu_custom_call" | custom-call | flops 3355443200 | bytes 17694720 | tf_op jit(solution)/shard_map/pallas_call | solution.py:106
  58.2 1.8 %collective-permute-start.12 = (bf16[64,1280]{1,0:T(8,128)(2,1)S(1)}, bf16[64,1280]{1,0:T(8,128)(2,1)S(1)}, u32[]{:S(2)}, u32[]{:S(2)}) collective-permute-start(bf16[64,1280]{1,0:T(8,128)(2,1)S(1)} %convert_element_type.110), channel_id=1, source_target_pairs={{0,4},{4,0},{8,12},{12,8},{16,20},{20,16},{24,28},{28,24},{1,5},{5... | collective-permute-start | bytes 491528 | tf_op jit(solution)/shard_map/ppermute | solution.py:27
  60.0 1.6 collective-permute-start.18
  61.6 2.8 %collective-permute-done.12 = bf16[64,1280]{1,0:T(8,128)(2,1)S(1)} collective-permute-done((bf16[64,1280]{1,0:T(8,128)(2,1)S(1)}, bf16[64,1280]{1,0:T(8,128)(2,1)S(1)}, u32[]{:S(2)}, u32[]{:S(2)}) %collective-permute-start.12) | collective-permute-done | bytes 163872 | tf_op jit(solution)/shard_map/ppermute | solution.py:27
  64.4 1.9 %collective-permute-start.13 = (bf16[64,1280]{1,0:T(8,128)(2,1)S(1)}, bf16[64,1280]{1,0:T(8,128)(2,1)S(1)}, u32[]{:S(2)}, u32[]{:S(2)}) collective-permute-start(bf16[64,1280]{1,0:T(8,128)(2,1)S(1)} %add_convert_fusion.5), channel_id=1, source_target_pairs={{0,8},{4,12},{8,0},{12,4},{16,24},{20,28},{24,16},{28,20},{1,9},{5... | collective-permute-start | bytes 491528 | tf_op jit(solution)/shard_map/ppermute | solution.py:27
  66.3 1.5 collective-permute-start.19
  67.8 2.0 %collective-permute-done.13 = bf16[64,1280]{1,0:T(8,128)(2,1)S(1)} collective-permute-done((bf16[64,1280]{1,0:T(8,128)(2,1)S(1)}, bf16[64,1280]{1,0:T(8,128)(2,1)S(1)}, u32[]{:S(2)}, u32[]{:S(2)}) %collective-permute-start.13) | collective-permute-done | bytes 163872 | tf_op jit(solution)/shard_map/ppermute | solution.py:27
  69.8 2.9 %collective-permute-start.14 = (bf16[64,1280]{1,0:T(8,128)(2,1)S(1)}, bf16[64,1280]{1,0:T(8,128)(2,1)S(1)}, u32[]{:S(2)}, u32[]{:S(2)}) collective-permute-start(bf16[64,1280]{1,0:T(8,128)(2,1)S(1)} %add_convert_fusion.4), channel_id=1, source_target_pairs={{0,16},{4,20},{8,24},{12,28},{16,0},{20,4},{24,8},{28,12},{1,17},{... | collective-permute-start | bytes 491528 | tf_op jit(solution)/shard_map/ppermute | solution.py:27
  72.7 1.6 collective-permute-start.20
  74.4 3.0 %collective-permute-done.20 = f32[64,320]{1,0:T(8,128)S(1)} collective-permute-done((f32[64,320]{1,0:T(8,128)S(1)}, f32[64,320]{1,0:T(8,128)S(1)}, u32[]{:S(2)}, u32[]{:S(2)}) %collective-permute-start.20) | collective-permute-done | bytes 81952 | tf_op jit(solution)/shard_map/ppermute | solution.py:27
  77.4 1.7 collective-permute-start.21
  79.3 3.7 %collective-permute-done.21 = f32[64,320]{1,0:T(8,128)S(1)} collective-permute-done((f32[64,320]{1,0:T(8,128)S(1)}, f32[64,320]{1,0:T(8,128)S(1)}, u32[]{:S(2)}, u32[]{:S(2)}) %collective-permute-start.21) | collective-permute-done | bytes 81952 | tf_op jit(solution)/shard_map/ppermute | solution.py:27
  83.0 1.6 collective-permute-start.22
  84.7 3.6 %shard_map.127 = (f32[2,64,320]{2,1,0:T(8,128)S(1)}, f32[2,64,320]{2,1,0:T(8,128)S(1)}) custom-call(s32[8]{0:T(128)S(1)} %copy-done.6, f32[64,1280]{1,0:T(8,128)S(1)} %convert_add_fusion.1.down_ref.refs_0_, bf16[1280,1024]{1,0:T(8,128)(2,1)S(1)} %copy-done, bf16[320,1024]{1,0:T(8,128)(2,1)S(1)} %bitcast.54, ...), custom_call_target="tpu_custom_call" | custom-call | flops 671088640 | bytes 5898240 | tf_op jit(solution)/shard_map/pallas_call | solution.py:106
  89.2 0.6 collective-permute-start.8
  89.9 1.6 collective-permute-start.28
  91.5 2.7 %shard_map.125 = f32[64,1280]{1,0:T(8,128)S(1)} custom-call(s32[8]{0:T(128)S(1)} %copy-done.6, f32[64,320]{1,0:T(8,128)S(1)} %add.119.refs_0_, f32[64,320]{1,0:T(8,128)S(1)} %get-tuple-element.62.refs_1_, f32[64,320]{1,0:T(8,128)S(1)} %collective-permute-done.22.refs_2_, f32[64,320]{1,0:T(8,128)S(1)} %get-tuple-element.61.refs_3_, ...), custom_call_target="tpu_custom_call" | custom-call | flops 671088640 | bytes 5898240 | tf_op jit(solution)/shard_map/pallas_call | solution.py:106
  94.3 1.5 collective-permute-start.24
  95.8 12.3 %collective-permute-done.28 = f32[1,64,320]{2,1,0:T(8,128)S(1)} collective-permute-done((f32[1,64,320]{2,1,0:T(8,128)S(1)}, f32[1,64,320]{2,1,0:T(8,128)S(1)}, u32[]{:S(2)}, u32[]{:S(2)}) %collective-permute-start.28) | collective-permute-done | bytes 81952 | tf_op jit(solution)/shard_map/ppermute | solution.py:27
  108.1 1.5 collective-permute-start.29
  109.9 2.9 %collective-permute-done.29 = f32[64,320]{1,0:T(8,128)S(1)} collective-permute-done((f32[64,320]{1,0:T(8,128)S(1)}, f32[64,320]{1,0:T(8,128)S(1)}, u32[]{:S(2)}, u32[]{:S(2)}) %collective-permute-start.29) | collective-permute-done | bytes 81952 | tf_op jit(solution)/shard_map/ppermute | solution.py:27
  112.8 2.3 %collective-permute-start.30 = (f32[64,320]{1,0:T(8,128)S(1)}, f32[64,320]{1,0:T(8,128)S(1)}, u32[]{:S(2)}, u32[]{:S(2)}) collective-permute-start(f32[64,320]{1,0:T(8,128)S(1)} %add.125), channel_id=1, source_target_pairs={{0,8},{4,12},{8,0},{12,4},{16,24},{20,28},{24,16},{28,20},{1,9},{5... | collective-permute-start | bytes 245768 | tf_op jit(solution)/shard_map/ppermute | solution.py:27
  115.1 2.3 %shard_map.121 = bf16[16,320,128]{2,1,0:T(8,128)(2,1)} custom-call(s32[16]{0:T(128)S(1)} %select_reduce_fusion.1.index_ref, bf16[320,1024]{1,0:T(8,128)(2,1)S(1)} %add_convert_fusion.1.a_ref, bf16[320,1024]{1,0:T(8,128)(2,1)S(1)} %collective-permute-done.8.b_ref), custom_call_target="tpu_custom_call" | custom-call | bytes 2621440 | tf_op jit(solution)/shard_map/pallas_call | solution.py:106
  117.4 3.8 %all-to-all-start = ((bf16[16,320,128]{2,1,0:T(8,128)(2,1)}), bf16[16,320,128]{2,1,0:T(8,128)(2,1)S(1)}, u32[]{:S(2)}, u32[]{:S(2)}) async-start(bf16[16,320,128]{2,1,0:T(8,128)(2,1)} %shard_map.121), calls=%async_computation | async-start | bytes 2621440 | tf_op jit(solution)/shard_map/all_to_all | solution.py:510
  121.3 2.1 %collective-permute-start.25 = (bf16[64,1280]{1,0:T(8,128)(2,1)S(1)}, bf16[64,1280]{1,0:T(8,128)(2,1)S(1)}, u32[]{:S(2)}, u32[]{:S(2)}) collective-permute-start(bf16[64,1280]{1,0:T(8,128)(2,1)S(1)} %add_convert_fusion.3), channel_id=1, source_target_pairs={{0,8},{4,12},{8,0},{12,4},{16,24},{20,28},{24,16},{28,20},{1,9},{5... | collective-permute-start | bytes 491528 | tf_op jit(solution)/shard_map/ppermute | solution.py:27
  123.9 2.4 %collective-permute-start.31 = (f32[64,320]{1,0:T(8,128)S(1)}, f32[64,320]{1,0:T(8,128)S(1)}, u32[]{:S(2)}, u32[]{:S(2)}) collective-permute-start(f32[64,320]{1,0:T(8,128)S(1)} %add.126), channel_id=1, source_target_pairs={{0,16},{4,20},{8,24},{12,28},{16,0},{20,4},{24,8},{28,12},{1,17},{... | collective-permute-start | bytes 245768 | tf_op jit(solution)/shard_map/ppermute | solution.py:27
  126.5 0.9 collective-permute-start.16
  127.4 27.4 %collective-permute-done.31 = f32[64,320]{1,0:T(8,128)S(1)} collective-permute-done((f32[64,320]{1,0:T(8,128)S(1)}, f32[64,320]{1,0:T(8,128)S(1)}, u32[]{:S(2)}, u32[]{:S(2)}) %collective-permute-start.31) | collective-permute-done | bytes 81952 | tf_op jit(solution)/shard_map/ppermute | solution.py:27
  154.8 1.2 collective-permute-start.32
  156.2 4.7 %shard_map.124 = (f32[64,64]{1,0:T(8,128)S(1)}, f32[64,64]{1,0:T(8,128)S(1)}, bf16[1280,192]{1,0:T(8,128)(2,1)S(1)}, bf16[1280,192]{1,0:T(8,128)(2,1)S(1)}) custom-call(s32[1]{0:T(128)} %bitcast.1.me_ref, f32[64,64]{1,0:T(8,128)S(1)} %add.114.gram_ref, f32[64,1280]{1,0:T(8,128)S(1)} %convert_add_fusion.1.down_ref.refs_0_, f32[64,320]{1,0:T(8,128)S(1)} %add.119.refs_0_, ...), custom_call_target="tpu_custom_call" | custom-call | flops 268435456 | bytes 1687552 | tf_op jit(solution)/shard_map/pallas_call | solution.py:106
  161.1 2.6 %collective-permute-done.26 = bf16[64,1280]{1,0:T(8,128)(2,1)S(1)} collective-permute-done((bf16[64,1280]{1,0:T(8,128)(2,1)S(1)}, bf16[64,1280]{1,0:T(8,128)(2,1)S(1)}, u32[]{:S(2)}, u32[]{:S(2)}) %collective-permute-start.26) | collective-permute-done | bytes 163872 | tf_op jit(solution)/shard_map/ppermute | solution.py:27
  163.7 4.6 %shard_map.126 = (f32[64,1280]{1,0:T(8,128)}, f32[1280,1280]{1,0:T(8,128)}) custom-call(s32[1]{0:T(128)} %bitcast.1.me_ref, f32[64,64]{1,0:T(8,128)S(1)} %get-tuple-element.40.inv_ref, bf16[1280,192]{1,0:T(8,128)(2,1)S(1)} %get-tuple-element.41.left_ref, f32[64,1280]{1,0:T(8,128)S(1)} %convert_add_fusion.refs_0_), custom_call_target="tpu_custom_call" | custom-call | flops 629145600 | bytes 7716864 | tf_op jit(solution)/shard_map/pallas_call | solution.py:106
  168.3 4.7 %shard_map.128 = (f32[64,1280]{1,0:T(8,128)}, f32[1280,1280]{1,0:T(8,128)}) custom-call(s32[1]{0:T(128)} %bitcast.1.me_ref, f32[64,64]{1,0:T(8,128)S(1)} %get-tuple-element.44.inv_ref, bf16[1280,192]{1,0:T(8,128)(2,1)S(1)} %get-tuple-element.45.left_ref, f32[64,320]{1,0:T(8,128)S(1)} %add.127.refs_0_, f32[64,320]{1,0:T(8,128)S(1)} %get-tuple-element.60.refs_1_, ...), custom_call_target="tpu_custom_call" | custom-call | flops 629145600 | bytes 7716864 | tf_op jit(solution)/shard_map/pallas_call | solution.py:106
  173.0 1.8 %shard_map.122 = bf16[320,1792]{1,0:T(8,128)(2,1)} custom-call(s32[14]{0:T(128)S(1)} %select_reduce_fusion.index_ref, s32[14]{0:T(128)S(1)} %convert_element_type.98.ok_ref, bf16[16,320,128]{2,1,0:T(8,128)(2,1)S(1)} %all-to-all-done.in_ref), custom_call_target="tpu_custom_call" | custom-call | bytes 2457600 | tf_op jit(solution)/shard_map/pallas_call | solution.py:106
  (100 shorter events, 5.1 us)
Async XLA Ops:
  0.6 32.8 %collective-permute-start.3 = (bf16[320,1024]{1,0:T(8,128)(2,1)}, bf16[320,1024]{1,0:T(8,128)(2,1)S(1)}, u32[]{:S(2)}, u32[]{:S(2)}) collective-permute-start(bf16[320,1024]{1,0:T(8,128)(2,1)} %bitcast.46), channel_id=1, source_target_pairs={{0,1},{1,0},{2,3},{3,2},{4,5},{5,4},{6,7},{7,6},{8,9},{9,8},{10,11... | collective-permute-start | bytes 1966088 | tf_op jit(solution)/shard_map/ppermute | solution.py:27
  1.2 18.4 %collective-permute-start.4 = (bf16[320,1024]{1,0:T(8,128)(2,1)}, bf16[320,1024]{1,0:T(8,128)(2,1)S(1)}, u32[]{:S(2)}, u32[]{:S(2)}) collective-permute-start(bf16[320,1024]{1,0:T(8,128)(2,1)} %bitcast.47), channel_id=1, source_target_pairs={{0,2},{1,3},{2,0},{3,1},{4,6},{5,7},{6,4},{7,5},{8,10},{9,11},{10,... | collective-permute-start | bytes 1966088 | tf_op jit(solution)/shard_map/ppermute | solution.py:27
  3.8 42.3 %collective-permute-start.9 = (bf16[320,1024]{1,0:T(8,128)(2,1)}, bf16[320,1024]{1,0:T(8,128)(2,1)}, u32[]{:S(2)}, u32[]{:S(2)}) collective-permute-start(bf16[320,1024]{1,0:T(8,128)(2,1)} %bitcast.51), channel_id=1, source_target_pairs={{0,1},{1,0},{2,3},{3,2},{4,5},{5,4},{6,7},{7,6},{8,9},{9,8},{10,11... | collective-permute-start | bytes 1966088 | tf_op jit(solution)/shard_map/ppermute | solution.py:27
  3.9 29.5 %collective-permute-start.10 = (bf16[320,1024]{1,0:T(8,128)(2,1)}, bf16[320,1024]{1,0:T(8,128)(2,1)}, u32[]{:S(2)}, u32[]{:S(2)}) collective-permute-start(bf16[320,1024]{1,0:T(8,128)(2,1)} %bitcast.52), channel_id=1, source_target_pairs={{0,2},{1,3},{2,0},{3,1},{4,6},{5,7},{6,4},{7,5},{8,10},{9,11},{10,... | collective-permute-start | bytes 1966088 | tf_op jit(solution)/shard_map/ppermute | solution.py:27
  4.9 14.6 %collective-permute-start = (s32[8,8]{1,0:T(8,128)S(1)}, s32[8,8]{1,0:T(8,128)S(1)}, u32[]{:S(2)}, u32[]{:S(2)}) collective-permute-start(s32[8,8]{1,0:T(8,128)S(1)} %broadcast_select_fusion.4), channel_id=1, source_target_pairs={{0,4},{4,0},{8,12},{12,8},{16,20},{20,16},{24,28},{28,24},{1,5},{5... | collective-permute-start | bytes 776 | tf_op jit(solution)/shard_map/ppermute | solution.py:27
  9.1 10.5 %copy-start.8 = (s32[8]{0:T(128)S(1)}, s32[8]{0:T(128)}, u32[]{:S(2)}) copy-start(s32[8]{0:T(128)} %param.10) | copy-start | bytes 100
  9.1 24.4 %copy-start.1 = (bf16[1024,320]{0,1:T(8,128)(2,1)S(1)}, bf16[1024,320]{0,1:T(8,128)(2,1)}, u32[]{:S(2)}) copy-start(bf16[1024,320]{0,1:T(8,128)(2,1)} %param.8) | copy-start | bytes 1966084
  9.1 24.4 %copy-start.6 = (s32[8]{0:T(128)S(1)}, s32[8]{0:T(128)}, u32[]{:S(2)}) copy-start(s32[8]{0:T(128)} %fill_ref.7) | copy-start | bytes 100
  17.0 1.7 copy-start.7
  19.6 13.9 %collective-permute-start.5 = (bf16[320,1024]{1,0:T(8,128)(2,1)S(1)}, bf16[320,1024]{1,0:T(8,128)(2,1)S(1)}, u32[]{:S(2)}, u32[]{:S(2)}) collective-permute-start(bf16[320,1024]{1,0:T(8,128)(2,1)S(1)} %collective-permute-done.4.refs_2_.refs_6_), channel_id=1, source_target_pairs={{0,1},{1,0},{2,3},{3,2},{4,5},{5,4},{6,7},{7,6},{8,9},{9,8},{10,11... | collective-permute-start | bytes 1966088 | tf_op jit(solution)/shard_map/ppermute | solution.py:27
  19.8 3.7 %collective-permute-start.1 = (s32[8,8]{1,0:T(8,128)S(1)}, s32[8,8]{1,0:T(8,128)S(1)}, u32[]{:S(2)}, u32[]{:S(2)}) collective-permute-start(s32[8,8]{1,0:T(8,128)S(1)} %get-tuple-element.64), channel_id=1, source_target_pairs={{0,8},{4,12},{8,0},{12,4},{16,24},{20,28},{24,16},{28,20},{1,9},{5... | collective-permute-start | bytes 776 | tf_op jit(solution)/shard_map/ppermute | solution.py:27
  23.5 4.6 %collective-permute-start.2 = (s32[8,8]{1,0:T(8,128)S(1)}, s32[8,8]{1,0:T(8,128)S(1)}, u32[]{:S(2)}, u32[]{:S(2)}) collective-permute-start(s32[8,8]{1,0:T(8,128)S(1)} %add.103), channel_id=1, source_target_pairs={{0,16},{4,20},{8,24},{12,28},{16,0},{20,4},{24,8},{28,12},{1,17},{... | collective-permute-start | bytes 776 | tf_op jit(solution)/shard_map/ppermute | solution.py:27
  33.5 12.6 %collective-permute-start.11 = (bf16[320,1024]{1,0:T(8,128)(2,1)}, bf16[320,1024]{1,0:T(8,128)(2,1)S(1)}, u32[]{:S(2)}, u32[]{:S(2)}) collective-permute-start(bf16[320,1024]{1,0:T(8,128)(2,1)} %collective-permute-done.10.refs_2_.refs_4_), channel_id=1, source_target_pairs={{0,1},{1,0},{2,3},{3,2},{4,5},{5,4},{6,7},{7,6},{8,9},{9,8},{10,11... | collective-permute-start | bytes 1966088 | tf_op jit(solution)/shard_map/ppermute | solution.py:27
  33.5 12.6 %copy-start.2 = (bf16[320,1024]{1,0:T(8,128)(2,1)}, bf16[320,1024]{1,0:T(8,128)(2,1)S(1)}, u32[]{:S(2)}) copy-start(bf16[320,1024]{1,0:T(8,128)(2,1)S(1)} %collective-permute-done.5.refs_3_.refs_7_) | copy-start | bytes 1966084
  33.5 12.6 %copy-start.4 = (bf16[1024,320]{0,1:T(8,128)(2,1)S(1)}, bf16[1024,320]{0,1:T(8,128)(2,1)}, u32[]{:S(2)}) copy-start(bf16[1024,320]{0,1:T(8,128)(2,1)} %param.9) | copy-start | bytes 1966084
  57.4 27.2 %copy-start = (bf16[1280,1024]{1,0:T(8,128)(2,1)S(1)}, bf16[1280,1024]{1,0:T(8,128)(2,1)}, u32[]{:S(2)}) copy-start(bf16[1280,1024]{1,0:T(8,128)(2,1)} %get-tuple-element.35.refs_9_.refs_1_) | copy-start | bytes 7864324
  57.4 2.5 %collective-permute-start.17 = (f32[2,64,320]{2,1,0:T(8,128)S(1)}, f32[2,64,320]{2,1,0:T(8,128)S(1)}, u32[]{:S(2)}, u32[]{:S(2)}) collective-permute-start(f32[2,64,320]{2,1,0:T(8,128)S(1)} %get-tuple-element.39), channel_id=1, source_target_pairs={{0,1},{1,0},{2,3},{3,2},{4,5},{5,4},{6,7},{7,6},{8,9},{9,8},{10,11... | collective-permute-start | bytes 491528 | tf_op jit(solution)/shard_map/ppermute | solution.py:27
  58.2 6.2 %collective-permute-start.12 = (bf16[64,1280]{1,0:T(8,128)(2,1)S(1)}, bf16[64,1280]{1,0:T(8,128)(2,1)S(1)}, u32[]{:S(2)}, u32[]{:S(2)}) collective-permute-start(bf16[64,1280]{1,0:T(8,128)(2,1)S(1)} %convert_element_type.110), channel_id=1, source_target_pairs={{0,4},{4,0},{8,12},{12,8},{16,20},{20,16},{24,28},{28,24},{1,5},{5... | collective-permute-start | bytes 491528 | tf_op jit(solution)/shard_map/ppermute | solution.py:27
  60.0 6.3 %collective-permute-start.18 = (f32[1,64,320]{2,1,0:T(8,128)S(1)}, f32[1,64,320]{2,1,0:T(8,128)S(1)}, u32[]{:S(2)}, u32[]{:S(2)}) collective-permute-start(f32[1,64,320]{2,1,0:T(8,128)S(1)} %slice_bitcast_fusion.6), channel_id=1, source_target_pairs={{0,2},{1,3},{2,0},{3,1},{4,6},{5,7},{6,4},{7,5},{8,10},{9,11},{10,... | collective-permute-start | bytes 245768 | tf_op jit(solution)/shard_map/ppermute | solution.py:27
  64.4 5.4 %collective-permute-start.13 = (bf16[64,1280]{1,0:T(8,128)(2,1)S(1)}, bf16[64,1280]{1,0:T(8,128)(2,1)S(1)}, u32[]{:S(2)}, u32[]{:S(2)}) collective-permute-start(bf16[64,1280]{1,0:T(8,128)(2,1)S(1)} %add_convert_fusion.5), channel_id=1, source_target_pairs={{0,8},{4,12},{8,0},{12,4},{16,24},{20,28},{24,16},{28,20},{1,9},{5... | collective-permute-start | bytes 491528 | tf_op jit(solution)/shard_map/ppermute | solution.py:27
  66.3 6.4 %collective-permute-start.19 = (f32[64,320]{1,0:T(8,128)S(1)}, f32[64,320]{1,0:T(8,128)S(1)}, u32[]{:S(2)}, u32[]{:S(2)}) collective-permute-start(f32[64,320]{1,0:T(8,128)S(1)} %fusion.5), channel_id=1, source_target_pairs={{0,4},{4,0},{8,12},{12,8},{16,20},{20,16},{24,28},{28,24},{1,5},{5... | collective-permute-start | bytes 245768 | tf_op jit(solution)/shard_map/ppermute | solution.py:27
  69.8 14.8 %collective-permute-start.14 = (bf16[64,1280]{1,0:T(8,128)(2,1)S(1)}, bf16[64,1280]{1,0:T(8,128)(2,1)S(1)}, u32[]{:S(2)}, u32[]{:S(2)}) collective-permute-start(bf16[64,1280]{1,0:T(8,128)(2,1)S(1)} %add_convert_fusion.4), channel_id=1, source_target_pairs={{0,16},{4,20},{8,24},{12,28},{16,0},{20,4},{24,8},{28,12},{1,17},{... | collective-permute-start | bytes 491528 | tf_op jit(solution)/shard_map/ppermute | solution.py:27
  72.7 4.7 %collective-permute-start.20 = (f32[64,320]{1,0:T(8,128)S(1)}, f32[64,320]{1,0:T(8,128)S(1)}, u32[]{:S(2)}, u32[]{:S(2)}) collective-permute-start(f32[64,320]{1,0:T(8,128)S(1)} %add.117), channel_id=1, source_target_pairs={{0,8},{4,12},{8,0},{12,4},{16,24},{20,28},{24,16},{28,20},{1,9},{5... | collective-permute-start | bytes 245768 | tf_op jit(solution)/shard_map/ppermute | solution.py:27
  74.4 14.6 %collective-permute-start.7 = (bf16[320,1024]{1,0:T(8,128)(2,1)S(1)}, bf16[320,1024]{1,0:T(8,128)(2,1)S(1)}, u32[]{:S(2)}, u32[]{:S(2)}) collective-permute-start(bf16[320,1024]{1,0:T(8,128)(2,1)S(1)} %get-tuple-element.33), channel_id=1, source_target_pairs={{0,1},{1,0},{2,3},{3,2},{4,5},{5,4},{6,7},{7,6},{8,9},{9,8},{10,11... | collective-permute-start | bytes 1966088 | tf_op jit(solution)/shard_map/ppermute | solution.py:27
  77.4 5.6 %collective-permute-start.21 = (f32[64,320]{1,0:T(8,128)S(1)}, f32[64,320]{1,0:T(8,128)S(1)}, u32[]{:S(2)}, u32[]{:S(2)}) collective-permute-start(f32[64,320]{1,0:T(8,128)S(1)} %add.118), channel_id=1, source_target_pairs={{0,16},{4,20},{8,24},{12,28},{16,0},{20,4},{24,8},{28,12},{1,17},{... | collective-permute-start | bytes 245768 | tf_op jit(solution)/shard_map/ppermute | solution.py:27
  79.3 30.4 %collective-permute-start.6 = (bf16[320,1024]{1,0:T(8,128)(2,1)S(1)}, bf16[320,1024]{1,0:T(8,128)(2,1)S(1)}, u32[]{:S(2)}, u32[]{:S(2)}) collective-permute-start(bf16[320,1024]{1,0:T(8,128)(2,1)S(1)} %get-tuple-element.31), channel_id=1, source_target_pairs={{0,1},{1,0},{2,3},{3,2},{4,5},{5,4},{6,7},{7,6},{8,9},{9,8},{10,11... | collective-permute-start | bytes 1966088 | tf_op jit(solution)/shard_map/ppermute | solution.py:27
  83.0 5.4 %collective-permute-start.22 = (f32[64,320]{1,0:T(8,128)S(1)}, f32[64,320]{1,0:T(8,128)S(1)}, u32[]{:S(2)}, u32[]{:S(2)}) collective-permute-start(f32[64,320]{1,0:T(8,128)S(1)} %add.119.refs_0_), channel_id=1, source_target_pairs={{0,2},{1,3},{2,0},{3,1},{4,6},{5,7},{6,4},{7,5},{8,10},{9,11},{10,... | collective-permute-start | bytes 245768 | tf_op jit(solution)/shard_map/ppermute | solution.py:27
  88.3 3.2 %copy-start.3 = (bf16[320,1024]{1,0:T(8,128)(2,1)S(1)}, bf16[320,1024]{1,0:T(8,128)(2,1)}, u32[]{:S(2)}) copy-start(bf16[320,1024]{1,0:T(8,128)(2,1)} %copy-done.2) | copy-start | bytes 1966084
  88.3 3.2 %copy-start.5 = (bf16[1280,1024]{1,0:T(8,128)(2,1)S(1)}, bf16[1280,1024]{1,0:T(8,128)(2,1)}, u32[]{:S(2)}) copy-start(bf16[1280,1024]{1,0:T(8,128)(2,1)} %get-tuple-element.42.refs_8_) | copy-start | bytes 7864324
  88.3 1.5 collective-permute-start.27
  88.4 3.0 %collective-permute-start.23 = (f32[2,64,320]{2,1,0:T(8,128)S(1)}, f32[2,64,320]{2,1,0:T(8,128)S(1)}, u32[]{:S(2)}, u32[]{:S(2)}) collective-permute-start(f32[2,64,320]{2,1,0:T(8,128)S(1)} %pad_maximum_fusion.2), channel_id=1, source_target_pairs={{0,1},{1,0},{2,3},{3,2},{4,5},{5,4},{6,7},{7,6},{8,9},{9,8},{10,11... | collective-permute-start | bytes 491528 | tf_op jit(solution)/shard_map/ppermute | solution.py:27
  89.2 25.9 %collective-permute-start.8 = (bf16[320,1024]{1,0:T(8,128)(2,1)S(1)}, bf16[320,1024]{1,0:T(8,128)(2,1)S(1)}, u32[]{:S(2)}, u32[]{:S(2)}) collective-permute-start(bf16[320,1024]{1,0:T(8,128)(2,1)S(1)} %add_convert_fusion), channel_id=1, source_target_pairs={{0,2},{1,3},{2,0},{3,1},{4,6},{5,7},{6,4},{7,5},{8,10},{9,11},{10,... | collective-permute-start | bytes 1966088 | tf_op jit(solution)/shard_map/ppermute | solution.py:27
  89.9 18.2 %collective-permute-start.28 = (f32[1,64,320]{2,1,0:T(8,128)S(1)}, f32[1,64,320]{2,1,0:T(8,128)S(1)}, u32[]{:S(2)}, u32[]{:S(2)}) collective-permute-start(f32[1,64,320]{2,1,0:T(8,128)S(1)} %slice_bitcast_fusion.2), channel_id=1, source_target_pairs={{0,2},{1,3},{2,0},{3,1},{4,6},{5,7},{6,4},{7,5},{8,10},{9,11},{10,... | collective-permute-start | bytes 245768 | tf_op jit(solution)/shard_map/ppermute | solution.py:27
  94.3 27.0 %collective-permute-start.24 = (bf16[64,1280]{1,0:T(8,128)(2,1)S(1)}, bf16[64,1280]{1,0:T(8,128)(2,1)S(1)}, u32[]{:S(2)}, u32[]{:S(2)}) collective-permute-start(bf16[64,1280]{1,0:T(8,128)(2,1)S(1)} %convert_element_type.119), channel_id=1, source_target_pairs={{0,4},{4,0},{8,12},{12,8},{16,20},{20,16},{24,28},{28,24},{1,5},{5... | collective-permute-start | bytes 491528 | tf_op jit(solution)/shard_map/ppermute | solution.py:27
  108.1 4.7 %collective-permute-start.29 = (f32[64,320]{1,0:T(8,128)S(1)}, f32[64,320]{1,0:T(8,128)S(1)}, u32[]{:S(2)}, u32[]{:S(2)}) collective-permute-start(f32[64,320]{1,0:T(8,128)S(1)} %fusion.3), channel_id=1, source_target_pairs={{0,4},{4,0},{8,12},{12,8},{16,20},{20,16},{24,28},{28,24},{1,5},{5... | collective-permute-start | bytes 245768 | tf_op jit(solution)/shard_map/ppermute | solution.py:27
  112.8 11.1 %collective-permute-start.30 = (f32[64,320]{1,0:T(8,128)S(1)}, f32[64,320]{1,0:T(8,128)S(1)}, u32[]{:S(2)}, u32[]{:S(2)}) collective-permute-start(f32[64,320]{1,0:T(8,128)S(1)} %add.125), channel_id=1, source_target_pairs={{0,8},{4,12},{8,0},{12,4},{16,24},{20,28},{24,16},{28,20},{1,9},{5... | collective-permute-start | bytes 245768 | tf_op jit(solution)/shard_map/ppermute | solution.py:27
  117.4 55.5 %all-to-all-start = ((bf16[16,320,128]{2,1,0:T(8,128)(2,1)}), bf16[16,320,128]{2,1,0:T(8,128)(2,1)S(1)}, u32[]{:S(2)}, u32[]{:S(2)}) async-start(bf16[16,320,128]{2,1,0:T(8,128)(2,1)} %shard_map.121), calls=%async_computation | async-start | bytes 2621440 | tf_op jit(solution)/shard_map/all_to_all | solution.py:510
  121.3 34.6 %collective-permute-start.25 = (bf16[64,1280]{1,0:T(8,128)(2,1)S(1)}, bf16[64,1280]{1,0:T(8,128)(2,1)S(1)}, u32[]{:S(2)}, u32[]{:S(2)}) collective-permute-start(bf16[64,1280]{1,0:T(8,128)(2,1)S(1)} %add_convert_fusion.3), channel_id=1, source_target_pairs={{0,8},{4,12},{8,0},{12,4},{16,24},{20,28},{24,16},{28,20},{1,9},{5... | collective-permute-start | bytes 491528 | tf_op jit(solution)/shard_map/ppermute | solution.py:27
  123.8 2.7 %collective-permute-start.15 = (f32[64,64]{1,0:T(8,128)S(1)}, f32[64,64]{1,0:T(8,128)S(1)}, u32[]{:S(2)}, u32[]{:S(2)}) collective-permute-start(f32[64,64]{1,0:T(8,128)S(1)} %fusion.12), channel_id=1, source_target_pairs={{0,1},{1,0},{2,3},{3,2},{4,5},{5,4},{6,7},{7,6},{8,9},{9,8},{10,11... | collective-permute-start | bytes 49160 | tf_op jit(solution)/shard_map/ppermute | solution.py:27
  123.9 30.9 %collective-permute-start.31 = (f32[64,320]{1,0:T(8,128)S(1)}, f32[64,320]{1,0:T(8,128)S(1)}, u32[]{:S(2)}, u32[]{:S(2)}) collective-permute-start(f32[64,320]{1,0:T(8,128)S(1)} %add.126), channel_id=1, source_target_pairs={{0,16},{4,20},{8,24},{12,28},{16,0},{20,4},{24,8},{28,12},{1,17},{... | collective-permute-start | bytes 245768 | tf_op jit(solution)/shard_map/ppermute | solution.py:27
  126.5 29.7 %collective-permute-start.16 = (f32[64,64]{1,0:T(8,128)S(1)}, f32[64,64]{1,0:T(8,128)S(1)}, u32[]{:S(2)}, u32[]{:S(2)}) collective-permute-start(f32[64,64]{1,0:T(8,128)S(1)} %add.113), channel_id=1, source_target_pairs={{0,2},{1,3},{2,0},{3,1},{4,6},{5,7},{6,4},{7,5},{8,10},{9,11},{10,... | collective-permute-start | bytes 49160 | tf_op jit(solution)/shard_map/ppermute | solution.py:27
  154.8 6.2 %collective-permute-start.32 = (f32[64,320]{1,0:T(8,128)S(1)}, f32[64,320]{1,0:T(8,128)S(1)}, u32[]{:S(2)}, u32[]{:S(2)}) collective-permute-start(f32[64,320]{1,0:T(8,128)S(1)} %add.127.refs_0_), channel_id=1, source_target_pairs={{0,2},{1,3},{2,0},{3,1},{4,6},{5,7},{6,4},{7,5},{8,10},{9,11},{10,... | collective-permute-start | bytes 245768 | tf_op jit(solution)/shard_map/ppermute | solution.py:27
  156.0 7.6 %collective-permute-start.26 = (bf16[64,1280]{1,0:T(8,128)(2,1)S(1)}, bf16[64,1280]{1,0:T(8,128)(2,1)S(1)}, u32[]{:S(2)}, u32[]{:S(2)}) collective-permute-start(bf16[64,1280]{1,0:T(8,128)(2,1)S(1)} %add_convert_fusion.2), channel_id=1, source_target_pairs={{0,16},{4,20},{8,24},{12,28},{16,0},{20,4},{24,8},{28,12},{1,17},{... | collective-permute-start | bytes 491528 | tf_op jit(solution)/shard_map/ppermute | solution.py:27
  161.0 7.3 %collective-permute-start.33 = (f32[2,64,320]{2,1,0:T(8,128)S(1)}, f32[2,64,320]{2,1,0:T(8,128)S(1)}, u32[]{:S(2)}, u32[]{:S(2)}) collective-permute-start(f32[2,64,320]{2,1,0:T(8,128)S(1)} %pad_maximum_fusion.3), channel_id=1, source_target_pairs={{0,1},{1,0},{2,3},{3,2},{4,5},{5,4},{6,7},{7,6},{8,9},{9,8},{10,11... | collective-permute-start | bytes 491528 | tf_op jit(solution)/shard_map/ppermute | solution.py:27

commit v3 on v2

--- a/solution.py
+++ b/solution.py
@@ -13,6 +13,7 @@
 STRIP = 128
 CAP = 2
 EXTRA = 6
+FLAG = 16
 bf16 = jnp.bfloat16
 f32 = jnp.float32
 HIGHEST = lax.Precision.HIGHEST
@@ -421,27 +422,38 @@
     )
 
 
-def pack_kernel(index_ref, a_ref, b_ref, out_ref):
+def pack_kernel(index_ref, ok_ref, a_ref, b_ref, out_ref):
+    piece = a_ref.shape[0]
     for s in range(out_ref.shape[0]):
         lanes = pl.ds(pl.multiple_of(index_ref[s] * BLOCK, BLOCK), BLOCK)
         total = a_ref[:, lanes].astype(f32) + b_ref[:, lanes].astype(f32)
-        out_ref[s] = total.astype(bf16)
-
-
-def pack(a, b, index):
-    out = struct((index.shape[0], a.shape[0], BLOCK), bf16)
-    return call(pack_kernel, out, (a, b), (index,), in_specs=[whole(a), whole(b)], out_specs=whole(out))
-
-
-def unpack_kernel(index_ref, ok_ref, in_ref, out_ref):
-    for k in range(out_ref.shape[1] // BLOCK):
-        part = in_ref[index_ref[k]]
-        out_ref[:, k * BLOCK : (k + 1) * BLOCK] = jnp.where(ok_ref[k] > 0, part, jnp.zeros_like(part))
-
-
-def unpack(got, index, ok):
-    out = struct((got.shape[1], index.shape[0] * BLOCK), bf16)
-    return call(unpack_kernel, out, (got,), (index, ok), in_specs=[whole(got)], out_specs=whole(out))
+        out_ref[s, :piece, :] = total.astype(bf16)
+        out_ref[s, piece:, :] = jnp.full((FLAG, BLOCK), ok_ref[s].astype(f32)).astype(bf16)
+
+
+def pack(a, b, index, ok):
+    out = struct((index.shape[0], a.shape[0] + FLAG, BLOCK), bf16)
+    return call(pack_kernel, out, (a, b), (index, ok), in_specs=[whole(a), whole(b)], out_specs=whole(out))
+
+
+def unpack_kernel(in_ref, out_ref):
+    piece = out_ref.shape[0]
+    out_ref[...] = jnp.zeros_like(out_ref)
+    used = [jnp.max(in_ref[s, piece:, :].astype(f32)).astype(jnp.int32) for s in range(in_ref.shape[0])]
+    at = jnp.int32(0)
+    for s, one in enumerate(used):
+
+        @pl.when(one > 0)
+        def _(s=s, at=at):
+            lanes = pl.ds(pl.multiple_of(at * BLOCK, BLOCK), BLOCK)
+            out_ref[:, lanes] = in_ref[s, :piece, :]
+
+        at = at + one
+
+
+def unpack(got, most):
+    out = struct((got.shape[1] - FLAG, most * BLOCK), bf16)
+    return call(unpack_kernel, out, (got,), in_specs=[whole(got)], out_specs=whole(out))
 
 
 def earlier(labels):
@@ -454,28 +466,8 @@
     place = ranks * CAP + earlier(ranks)
     chosen = jnp.arange(ranks_dp * CAP, dtype=jnp.int32)[:, None] == place[None, :]
     ids = jnp.arange(ranks.shape[0], dtype=jnp.int32)
-    return jnp.sum(jnp.where(chosen, ids[None, :], 0), axis=1).astype(jnp.int32)
-
-
-def recv_plan(all_ranks, per_rank, me, most):
-    total = all_ranks.shape[0]
-    ids = jnp.arange(total, dtype=jnp.int32)
-    source = ids // per_rank
-    order = earlier(all_ranks)
-    within = earlier(all_ranks + source * total)
-    place = source * CAP + within
-    mine = all_ranks == me
-    chosen = mine[None, :] & (order[None, :] == jnp.arange(most, dtype=jnp.int32)[:, None])
-    index = jnp.sum(jnp.where(chosen, place[None, :], 0), axis=1)
+    index = jnp.sum(jnp.where(chosen, ids[None, :], 0), axis=1)
     return index.astype(jnp.int32), jnp.any(chosen, axis=1).astype(jnp.int32)
-
-
-def all_ranks_of(ranks, me):
-    count = lax.axis_size("dp")
-    table = jnp.where(jnp.arange(count, dtype=jnp.int32)[:, None] == me, ranks[None, :], 0)
-    for bit in bits_of(count):
-        table = table + swap(table, "dp", bit)
-    return table.reshape(-1)
 
 
 def split_rows(x):
@@ -486,12 +478,11 @@
 def local(patches, cotangent, encoder_rank, block_fill, w_up, w_down, q_up, q_down):
     ranks_dp = lax.axis_size("dp")
     count = lax.axis_size("mp")
-    me, me_dp = lax.axis_index("mp"), lax.axis_index("dp")
+    me = lax.axis_index("mp")
     blocks = encoder_rank.shape[0]
 
     xs = gather_xor(patches.T)
     cs = gather_xor(cotangent.T)
-    every = all_ranks_of(encoder_rank, me_dp)
     up_t, down_t, down_x = prepare(w_up, w_down, me, count)
     qd = split_rows(jnp.concatenate(reorder(slices(q_down.T, count, 1), me), axis=1))
     qu = split_rows(q_up.T)
@@ -506,9 +497,9 @@
         if len(got) == 1:
             break
         have = {o: (have[o].astype(f32) + got[o].astype(f32)).astype(bf16) for o in got}
-    sent = pack(have[0], got[0], send_plan(encoder_rank, ranks_dp))
+    sent = pack(have[0], got[0], *send_plan(encoder_rank, ranks_dp))
     received = lax.all_to_all(sent, "dp", split_axis=0, concat_axis=0, tiled=True)
-    encoded = unpack(received, *recv_plan(every, blocks, me_dp, blocks + EXTRA))
+    encoded = unpack(received, blocks + EXTRA)
 
     proj_down = sum_over(proj_down, "dp", bf16)
     proj_up = sum_over(reduce_mp(even, odd), "dp", f32)

time: 175 us -> 181 us (1.034)
  waiting for transfers between devices: 65.9 us -> 75.1 us
  starting transfers between devices: 44.3 us -> 40.8 us
    ppermute x34 -> x31, waiting for transfers between devices: 65.9 us -> 75.1 us  [swap(): return lax.ppermute(x, axis, [(i, i ^ bit) for i in range(count)])]
    ppermute x34 -> x31, starting transfers between devices: 40.5 us -> 35.1 us  [swap(): return lax.ppermute(x, axis, [(i, i ^ bit) for i in range(count)])]
    all_to_all x1, starting transfers between devices: 3.82 us -> 5.66 us  [local(): lax.all_to_all(sent, 'dp', split_axis=0, concat_axis=0, tiled=True)]
  transfers between devices with their start and end apart: 35 -> 32, of which waited for: 12 -> 12; matrix products, arithmetic and copies ran while one was open for 3% -> 4% of each run, Pallas kernels for 25% -> 23%
where the time goes in v3:
time: 181 us
  waiting for transfers between devices  75.1 us (41%)
  Pallas kernels  54.9 us (30%)
  starting transfers between devices  40.8 us (23%)
  other arithmetic  6.04 us (3%)
  local copies, waits for them, and re-layouts  2.54 us (1%)
    ppermute x31, waiting for transfers between devices, swap(): return lax.ppermute(x, axis, [(i, i ^ bit) for i in range(count)])  75.1 us
    pallas_call x10, Pallas kernels, kernel_call(): pl.pallas_call(body, out_shape=out_shape, grid_spec=pltpu.PrefetchScalarG...  54.9 us
    ppermute x31, starting transfers between devices, swap(): return lax.ppermute(x, axis, [(i, i ^ bit) for i in range(count)])  35.1 us
    all_to_all x1, starting transfers between devices, local(): lax.all_to_all(sent, 'dp', split_axis=0, concat_axis=0, tiled=True)  5.66 us
  transfers between devices with their start and end apart: 32, of which 12 were waited for; matrix products, arithmetic and copies ran while one was open for 4% of the time, Pallas kernels for 23%

profile of v3, /device:TPU:0, one launch (start us, length us, event | category | flops | bytes accessed | tf_op | source)
XLA Modules:
  0.0 180.8 jit_solution(9860910006792908298)
XLA Ops:
  0.6 0.6 collective-permute-start
  1.2 2.6 %collective-permute-start.1 = (bf16[320,1024]{1,0:T(8,128)(2,1)}, bf16[320,1024]{1,0:T(8,128)(2,1)S(1)}, u32[]{:S(2)}, u32[]{:S(2)}) collective-permute-start(bf16[320,1024]{1,0:T(8,128)(2,1)} %bitcast.47), channel_id=1, source_target_pairs={{0,2},{1,3},{2,0},{3,1},{4,6},{5,7},{6,4},{7,5},{8,10},{9,11},{10,... | collective-permute-start | bytes 1966088 | tf_op jit(solution)/shard_map/ppermute | solution.py:28
  4.2 1.2 broadcast_select_fusion
  5.5 1.0 reduce-precision_convert_fusion.1
  6.6 13.0 %collective-permute-done.1.refs_2_.refs_6_ = bf16[320,1024]{1,0:T(8,128)(2,1)S(1)} collective-permute-done((bf16[320,1024]{1,0:T(8,128)(2,1)}, bf16[320,1024]{1,0:T(8,128)(2,1)S(1)}, u32[]{:S(2)}, u32[]{:S(2)}) %collective-permute-start.1) | collective-permute-done | bytes 655392 | tf_op jit(solution)/shard_map/ppermute | solution.py:28
  19.7 13.7 %collective-permute-done.7.refs_2_.refs_4_ = bf16[320,1024]{1,0:T(8,128)(2,1)S(1)} collective-permute-done((bf16[320,1024]{1,0:T(8,128)(2,1)}, bf16[320,1024]{1,0:T(8,128)(2,1)S(1)}, u32[]{:S(2)}, u32[]{:S(2)}) %collective-permute-start.7) | collective-permute-done | bytes 655392 | tf_op jit(solution)/shard_map/ppermute | solution.py:28
  33.6 7.9 %shard_map.119 = (bf16[1280,1280]{1,0:T(8,128)(2,1)S(1)}, bf16[1280,1280]{1,0:T(8,128)(2,1)}, bf16[1280,1280]{1,0:T(8,128)(2,1)}) custom-call(s32[1]{0:T(128)} %bitcast.1.me_ref, bf16[1280,1280]{1,0:T(8,128)(2,1)} %up_ref.1, bf16[1280,1280]{1,0:T(8,128)(2,1)} %down_ref.1), custom_call_target="tpu_custom_call" | custom-call | bytes 16384000 | tf_op jit(solution)/shard_map/pallas_call | solution.py:107
  41.5 1.7 copy-done.7
  43.2 12.5 %shard_map.120 = (bf16[1280,1024]{1,0:T(8,128)(2,1)}, bf16[1280,1024]{1,0:T(8,128)(2,1)}, bf16[320,1024]{1,0:T(8,128)(2,1)S(1)}, bf16[320,1024]{1,0:T(8,128)(2,1...) custom-call(s32[8]{0:T(128)S(1)} %copy-done.6, bf16[320,1024]{1,0:T(8,128)(2,1)S(1)} %bitcast.48, ...), custom_call_target="tpu_custom_call" | custom-call | flops 6710886400 | bytes 17039360 | tf_op jit(solution)/shard_map/pallas_call | solution.py:107
  55.8 11.3 %shard_map.123 = (bf16[1280,1024]{1,0:T(8,128)(2,1)}, f32[2,64,320]{2,1,0:T(8,128)S(1)}, f32[2,64,320]{2,1,0:T(8,128)S(1)}, f32[64,1280]{1,0:T(8,128)S(1)}) custom-call(s32[8]{0:T(128)S(1)} %copy-done.6, bf16[320,1024]{1,0:T(8,128)(2,1)S(1)} %bitcast.53, bf16[320,1024]{1,0:T(8,128)(2,1)S(1)} %collective-permute-done.6.refs_1_.refs_3_, ...), custom_call_target="tpu_custom_call" | custom-call | flops 3355443200 | bytes 17694720 | tf_op jit(solution)/shard_map/pallas_call | solution.py:107
  67.1 0.5 collective-permute-start.14
  67.6 1.8 collective-permute-start.9
  69.4 1.6 collective-permute-start.15
  71.0 2.8 %collective-permute-done.9 = bf16[64,1280]{1,0:T(8,128)(2,1)S(1)} collective-permute-done((bf16[64,1280]{1,0:T(8,128)(2,1)S(1)}, bf16[64,1280]{1,0:T(8,128)(2,1)S(1)}, u32[]{:S(2)}, u32[]{:S(2)}) %collective-permute-start.9) | collective-permute-done | bytes 163872 | tf_op jit(solution)/shard_map/ppermute | solution.py:28
  73.8 1.9 %collective-permute-start.10 = (bf16[64,1280]{1,0:T(8,128)(2,1)S(1)}, bf16[64,1280]{1,0:T(8,128)(2,1)S(1)}, u32[]{:S(2)}, u32[]{:S(2)}) collective-permute-start(bf16[64,1280]{1,0:T(8,128)(2,1)S(1)} %add_convert_fusion.5), channel_id=1, source_target_pairs={{0,8},{4,12},{8,0},{12,4},{16,24},{20,28},{24,16},{28,20},{1,9},{5... | collective-permute-start | bytes 491528 | tf_op jit(solution)/shard_map/ppermute | solution.py:28
  75.7 1.6 collective-permute-start.16
  77.3 1.9 %collective-permute-done.10 = bf16[64,1280]{1,0:T(8,128)(2,1)S(1)} collective-permute-done((bf16[64,1280]{1,0:T(8,128)(2,1)S(1)}, bf16[64,1280]{1,0:T(8,128)(2,1)S(1)}, u32[]{:S(2)}, u32[]{:S(2)}) %collective-permute-start.10) | collective-permute-done | bytes 163872 | tf_op jit(solution)/shard_map/ppermute | solution.py:28
  79.3 2.9 %collective-permute-start.11 = (bf16[64,1280]{1,0:T(8,128)(2,1)S(1)}, bf16[64,1280]{1,0:T(8,128)(2,1)S(1)}, u32[]{:S(2)}, u32[]{:S(2)}) collective-permute-start(bf16[64,1280]{1,0:T(8,128)(2,1)S(1)} %add_convert_fusion.4), channel_id=1, source_target_pairs={{0,16},{4,20},{8,24},{12,28},{16,0},{20,4},{24,8},{28,12},{1,17},{... | collective-permute-start | bytes 491528 | tf_op jit(solution)/shard_map/ppermute | solution.py:28
  82.2 1.6 collective-permute-start.17
  83.9 2.9 %collective-permute-done.17 = f32[64,320]{1,0:T(8,128)S(1)} collective-permute-done((f32[64,320]{1,0:T(8,128)S(1)}, f32[64,320]{1,0:T(8,128)S(1)}, u32[]{:S(2)}, u32[]{:S(2)}) %collective-permute-start.17) | collective-permute-done | bytes 81952 | tf_op jit(solution)/shard_map/ppermute | solution.py:28
  86.9 1.7 collective-permute-start.18
  88.7 3.8 %collective-permute-done.18 = f32[64,320]{1,0:T(8,128)S(1)} collective-permute-done((f32[64,320]{1,0:T(8,128)S(1)}, f32[64,320]{1,0:T(8,128)S(1)}, u32[]{:S(2)}, u32[]{:S(2)}) %collective-permute-start.18) | collective-permute-done | bytes 81952 | tf_op jit(solution)/shard_map/ppermute | solution.py:28
  92.5 1.6 collective-permute-start.19
  94.1 2.8 %shard_map.127 = (f32[2,64,320]{2,1,0:T(8,128)S(1)}, f32[2,64,320]{2,1,0:T(8,128)S(1)}) custom-call(s32[8]{0:T(128)S(1)} %copy-done.6, f32[64,1280]{1,0:T(8,128)S(1)} %convert_add_fusion.1.down_ref.refs_0_, bf16[1280,1024]{1,0:T(8,128)(2,1)S(1)} %copy-done, bf16[320,1024]{1,0:T(8,128)(2,1)S(1)} %bitcast.54, ...), custom_call_target="tpu_custom_call" | custom-call | flops 671088640 | bytes 5898240 | tf_op jit(solution)/shard_map/pallas_call | solution.py:107
  97.9 1.2 collective-permute-start.5
  99.1 0.6 slice_bitcast_fusion.2
  99.8 0.9 collective-permute-start.25
  101.0 2.7 %shard_map.125 = f32[64,1280]{1,0:T(8,128)S(1)} custom-call(s32[8]{0:T(128)S(1)} %copy-done.6, f32[64,320]{1,0:T(8,128)S(1)} %add.75.refs_0_, f32[64,320]{1,0:T(8,128)S(1)} %get-tuple-element.62.refs_1_, f32[64,320]{1,0:T(8,128)S(1)} %collective-permute-done.19.refs_2_, f32[64,320]{1,0:T(8,128)S(1)} %get-tuple-element.61.refs_3_, ...), custom_call_target="tpu_custom_call" | custom-call | flops 671088640 | bytes 5898240 | tf_op jit(solution)/shard_map/pallas_call | solution.py:107
  103.7 0.7 convert_element_type.111
  104.4 1.5 collective-permute-start.21
  105.9 9.7 %collective-permute-done.5.b_ref = bf16[320,1024]{1,0:T(8,128)(2,1)S(1)} collective-permute-done((bf16[320,1024]{1,0:T(8,128)(2,1)S(1)}, bf16[320,1024]{1,0:T(8,128)(2,1)S(1)}, u32[]{:S(2)}, u32[]{:S(2)}) %collective-permute-start.5) | collective-permute-done | bytes 655392 | tf_op jit(solution)/shard_map/ppermute | solution.py:28
  115.6 2.3 %shard_map.121 = bf16[16,336,128]{2,1,0:T(8,128)(2,1)} custom-call(s32[16]{0:T(128)S(1)} %select_reduce_fusion.index_ref, s32[16]{0:T(128)S(1)} %convert_element_type.91.ok_ref, bf16[320,1024]{1,0:T(8,128)(2,1)S(1)} %add_convert_fusion.1.a_ref, bf16[320,1024]{1,0:T(8,128)(2,1)S(1)} %collective-permute-done.5.b_ref), custom_call_target="tpu_custom_call" | custom-call | bytes 2686976 | tf_op jit(solution)/shard_map/pallas_call | solution.py:107
  117.9 5.7 %all-to-all-start = ((bf16[16,336,128]{2,1,0:T(8,128)(2,1)}), bf16[16,336,128]{2,1,0:T(8,128)(2,1)S(1)}, u32[]{:S(2)}, u32[]{:S(2)}) async-start(bf16[16,336,128]{2,1,0:T(8,128)(2,1)} %shard_map.121), calls=%async_computation | async-start | bytes 2752512 | tf_op jit(solution)/shard_map/all_to_all | solution.py:501
  123.6 0.9 fusion.3
  124.5 2.1 %collective-permute-start.26 = (f32[64,320]{1,0:T(8,128)S(1)}, f32[64,320]{1,0:T(8,128)S(1)}, u32[]{:S(2)}, u32[]{:S(2)}) collective-permute-start(f32[64,320]{1,0:T(8,128)S(1)} %fusion.3), channel_id=1, source_target_pairs={{0,4},{4,0},{8,12},{12,8},{16,20},{20,16},{24,28},{28,24},{1,5},{5... | collective-permute-start | bytes 245768 | tf_op jit(solution)/shard_map/ppermute | solution.py:28
  126.5 10.0 %collective-permute-done.26 = f32[64,320]{1,0:T(8,128)S(1)} collective-permute-done((f32[64,320]{1,0:T(8,128)S(1)}, f32[64,320]{1,0:T(8,128)S(1)}, u32[]{:S(2)}, u32[]{:S(2)}) %collective-permute-start.26) | collective-permute-done | bytes 81952 | tf_op jit(solution)/shard_map/ppermute | solution.py:28
  136.5 0.8 collective-permute-start.27
  137.3 0.9 add_convert_fusion.3
  138.3 1.4 collective-permute-start.22
  139.6 8.8 %collective-permute-done.27 = f32[64,320]{1,0:T(8,128)S(1)} collective-permute-done((f32[64,320]{1,0:T(8,128)S(1)}, f32[64,320]{1,0:T(8,128)S(1)}, u32[]{:S(2)}, u32[]{:S(2)}) %collective-permute-start.27) | collective-permute-done | bytes 81952 | tf_op jit(solution)/shard_map/ppermute | solution.py:28
  148.4 5.6 %collective-permute-start.28 = (f32[64,320]{1,0:T(8,128)S(1)}, f32[64,320]{1,0:T(8,128)S(1)}, u32[]{:S(2)}, u32[]{:S(2)}) collective-permute-start(f32[64,320]{1,0:T(8,128)S(1)} %add.82), channel_id=1, source_target_pairs={{0,16},{4,20},{8,24},{12,28},{16,0},{20,4},{24,8},{28,12},{1,17},{... | collective-permute-start | bytes 245768 | tf_op jit(solution)/shard_map/ppermute | solution.py:28
  154.5 4.9 %collective-permute-done.28 = f32[64,320]{1,0:T(8,128)S(1)} collective-permute-done((f32[64,320]{1,0:T(8,128)S(1)}, f32[64,320]{1,0:T(8,128)S(1)}, u32[]{:S(2)}, u32[]{:S(2)}) %collective-permute-start.28) | collective-permute-done | bytes 81952 | tf_op jit(solution)/shard_map/ppermute | solution.py:28
  159.4 1.8 %collective-permute-start.29 = (f32[64,320]{1,0:T(8,128)S(1)}, f32[64,320]{1,0:T(8,128)S(1)}, u32[]{:S(2)}, u32[]{:S(2)}) collective-permute-start(f32[64,320]{1,0:T(8,128)S(1)} %add.83.refs_0_), channel_id=1, source_target_pairs={{0,2},{1,3},{2,0},{3,1},{4,6},{5,7},{6,4},{7,5},{8,10},{9,11},{10,... | collective-permute-start | bytes 245768 | tf_op jit(solution)/shard_map/ppermute | solution.py:28
  161.8 3.5 %collective-permute-done.13 = f32[64,64]{1,0:T(8,128)S(1)} collective-permute-done((f32[64,64]{1,0:T(8,128)S(1)}, f32[64,64]{1,0:T(8,128)S(1)}, u32[]{:S(2)}, u32[]{:S(2)}) %collective-permute-start.13) | collective-permute-done | bytes 16416 | tf_op jit(solution)/shard_map/ppermute | solution.py:28
  165.4 4.7 %shard_map.124 = (f32[64,64]{1,0:T(8,128)S(1)}, f32[64,64]{1,0:T(8,128)S(1)}, bf16[1280,192]{1,0:T(8,128)(2,1)S(1)}, bf16[1280,192]{1,0:T(8,128)(2,1)S(1)}) custom-call(s32[1]{0:T(128)} %bitcast.1.me_ref, f32[64,64]{1,0:T(8,128)S(1)} %add.70.gram_ref, f32[64,1280]{1,0:T(8,128)S(1)} %convert_add_fusion.1.down_ref.refs_0_, f32[64,320]{1,0:T(8,128)S(1)} %add.75.refs_0_, ...), custom_call_target="tpu_custom_call" | custom-call | flops 268435456 | bytes 1687552 | tf_op jit(solution)/shard_map/pallas_call | solution.py:107
  170.3 4.6 %shard_map.126 = (f32[64,1280]{1,0:T(8,128)}, f32[1280,1280]{1,0:T(8,128)}) custom-call(s32[1]{0:T(128)} %bitcast.1.me_ref, f32[64,64]{1,0:T(8,128)S(1)} %get-tuple-element.40.inv_ref, bf16[1280,192]{1,0:T(8,128)(2,1)S(1)} %get-tuple-element.41.left_ref, f32[64,1280]{1,0:T(8,128)S(1)} %convert_add_fusion.refs_0_), custom_call_target="tpu_custom_call" | custom-call | flops 629145600 | bytes 7716864 | tf_op jit(solution)/shard_map/pallas_call | solution.py:107
  174.9 4.7 %shard_map.128 = (f32[64,1280]{1,0:T(8,128)}, f32[1280,1280]{1,0:T(8,128)}) custom-call(s32[1]{0:T(128)} %bitcast.1.me_ref, f32[64,64]{1,0:T(8,128)S(1)} %get-tuple-element.44.inv_ref, bf16[1280,192]{1,0:T(8,128)(2,1)S(1)} %get-tuple-element.45.left_ref, f32[64,320]{1,0:T(8,128)S(1)} %add.83.refs_0_, f32[64,320]{1,0:T(8,128)S(1)} %get-tuple-element.60.refs_1_, ...), custom_call_target="tpu_custom_call" | custom-call | flops 629145600 | bytes 7716864 | tf_op jit(solution)/shard_map/pallas_call | solution.py:107
  179.5 1.3 shard_map.122
  (87 shorter events, 3.8 us)
Async XLA Ops:
  0.6 32.7 %copy-start.10 = (s32[8]{0:T(128)S(1)}, s32[8]{0:T(128)}, u32[]{:S(2)}) copy-start(s32[8]{0:T(128)} %param.10) | copy-start | bytes 100
  0.6 42.5 %collective-permute-start = (bf16[320,1024]{1,0:T(8,128)(2,1)}, bf16[320,1024]{1,0:T(8,128)(2,1)S(1)}, u32[]{:S(2)}, u32[]{:S(2)}) collective-permute-start(bf16[320,1024]{1,0:T(8,128)(2,1)} %bitcast.46), channel_id=1, source_target_pairs={{0,1},{1,0},{2,3},{3,2},{4,5},{5,4},{6,7},{7,6},{8,9},{9,8},{10,11... | collective-permute-start | bytes 1966088 | tf_op jit(solution)/shard_map/ppermute | solution.py:28
  1.2 18.4 %collective-permute-start.1 = (bf16[320,1024]{1,0:T(8,128)(2,1)}, bf16[320,1024]{1,0:T(8,128)(2,1)S(1)}, u32[]{:S(2)}, u32[]{:S(2)}) collective-permute-start(bf16[320,1024]{1,0:T(8,128)(2,1)} %bitcast.47), channel_id=1, source_target_pairs={{0,2},{1,3},{2,0},{3,1},{4,6},{5,7},{6,4},{7,5},{8,10},{9,11},{10,... | collective-permute-start | bytes 1966088 | tf_op jit(solution)/shard_map/ppermute | solution.py:28
  3.8 52.0 %collective-permute-start.6 = (bf16[320,1024]{1,0:T(8,128)(2,1)}, bf16[320,1024]{1,0:T(8,128)(2,1)S(1)}, u32[]{:S(2)}, u32[]{:S(2)}) collective-permute-start(bf16[320,1024]{1,0:T(8,128)(2,1)} %bitcast.51), channel_id=1, source_target_pairs={{0,1},{1,0},{2,3},{3,2},{4,5},{5,4},{6,7},{7,6},{8,9},{9,8},{10,11... | collective-permute-start | bytes 1966088 | tf_op jit(solution)/shard_map/ppermute | solution.py:28
  3.9 29.4 %collective-permute-start.7 = (bf16[320,1024]{1,0:T(8,128)(2,1)}, bf16[320,1024]{1,0:T(8,128)(2,1)S(1)}, u32[]{:S(2)}, u32[]{:S(2)}) collective-permute-start(bf16[320,1024]{1,0:T(8,128)(2,1)} %bitcast.52), channel_id=1, source_target_pairs={{0,2},{1,3},{2,0},{3,1},{4,6},{5,7},{6,4},{7,5},{8,10},{9,11},{10,... | collective-permute-start | bytes 1966088 | tf_op jit(solution)/shard_map/ppermute | solution.py:28
  19.6 23.6 %collective-permute-start.2 = (bf16[320,1024]{1,0:T(8,128)(2,1)S(1)}, bf16[320,1024]{1,0:T(8,128)(2,1)S(1)}, u32[]{:S(2)}, u32[]{:S(2)}) collective-permute-start(bf16[320,1024]{1,0:T(8,128)(2,1)S(1)} %collective-permute-done.1.refs_2_.refs_6_), channel_id=1, source_target_pairs={{0,1},{1,0},{2,3},{3,2},{4,5},{5,4},{6,7},{7,6},{8,9},{9,8},{10,11... | collective-permute-start | bytes 1966088 | tf_op jit(solution)/shard_map/ppermute | solution.py:28
  33.4 22.4 %collective-permute-start.8 = (bf16[320,1024]{1,0:T(8,128)(2,1)S(1)}, bf16[320,1024]{1,0:T(8,128)(2,1)S(1)}, u32[]{:S(2)}, u32[]{:S(2)}) collective-permute-start(bf16[320,1024]{1,0:T(8,128)(2,1)S(1)} %collective-permute-done.7.refs_2_.refs_4_), channel_id=1, source_target_pairs={{0,1},{1,0},{2,3},{3,2},{4,5},{5,4},{6,7},{7,6},{8,9},{9,8},{10,11... | collective-permute-start | bytes 1966088 | tf_op jit(solution)/shard_map/ppermute | solution.py:28
  33.5 9.6 %copy-start.1 = (bf16[1024,320]{0,1:T(8,128)(2,1)S(1)}, bf16[1024,320]{0,1:T(8,128)(2,1)}, u32[]{:S(2)}) copy-start(bf16[1024,320]{0,1:T(8,128)(2,1)} %param.8) | copy-start | bytes 1966084
  33.6 9.6 %copy-start.6 = (s32[8]{0:T(128)S(1)}, s32[8]{0:T(128)}, u32[]{:S(2)}) copy-start(s32[8]{0:T(128)} %fill_ref.7) | copy-start | bytes 100
  41.5 1.7 copy-start.7
  43.2 12.6 %copy-start.2 = (bf16[320,1024]{1,0:T(8,128)(2,1)}, bf16[320,1024]{1,0:T(8,128)(2,1)S(1)}, u32[]{:S(2)}) copy-start(bf16[320,1024]{1,0:T(8,128)(2,1)S(1)} %collective-permute-done.2.refs_3_.refs_7_) | copy-start | bytes 1966084
  43.2 12.6 %copy-start.4 = (bf16[1024,320]{0,1:T(8,128)(2,1)S(1)}, bf16[1024,320]{0,1:T(8,128)(2,1)}, u32[]{:S(2)}) copy-start(bf16[1024,320]{0,1:T(8,128)(2,1)} %param.9) | copy-start | bytes 1966084
  67.1 27.0 %copy-start = (bf16[1280,1024]{1,0:T(8,128)(2,1)S(1)}, bf16[1280,1024]{1,0:T(8,128)(2,1)}, u32[]{:S(2)}) copy-start(bf16[1280,1024]{1,0:T(8,128)(2,1)} %get-tuple-element.35.refs_9_.refs_1_) | copy-start | bytes 7864324
  67.1 2.3 %collective-permute-start.14 = (f32[2,64,320]{2,1,0:T(8,128)S(1)}, f32[2,64,320]{2,1,0:T(8,128)S(1)}, u32[]{:S(2)}, u32[]{:S(2)}) collective-permute-start(f32[2,64,320]{2,1,0:T(8,128)S(1)} %get-tuple-element.39), channel_id=1, source_target_pairs={{0,1},{1,0},{2,3},{3,2},{4,5},{5,4},{6,7},{7,6},{8,9},{9,8},{10,11... | collective-permute-start | bytes 491528 | tf_op jit(solution)/shard_map/ppermute | solution.py:28
  67.6 6.2 %collective-permute-start.9 = (bf16[64,1280]{1,0:T(8,128)(2,1)S(1)}, bf16[64,1280]{1,0:T(8,128)(2,1)S(1)}, u32[]{:S(2)}, u32[]{:S(2)}) collective-permute-start(bf16[64,1280]{1,0:T(8,128)(2,1)S(1)} %convert_element_type.102), channel_id=1, source_target_pairs={{0,4},{4,0},{8,12},{12,8},{16,20},{20,16},{24,28},{28,24},{1,5},{5... | collective-permute-start | bytes 491528 | tf_op jit(solution)/shard_map/ppermute | solution.py:28
  69.4 6.3 %collective-permute-start.15 = (f32[1,64,320]{2,1,0:T(8,128)S(1)}, f32[1,64,320]{2,1,0:T(8,128)S(1)}, u32[]{:S(2)}, u32[]{:S(2)}) collective-permute-start(f32[1,64,320]{2,1,0:T(8,128)S(1)} %slice_bitcast_fusion.6), channel_id=1, source_target_pairs={{0,2},{1,3},{2,0},{3,1},{4,6},{5,7},{6,4},{7,5},{8,10},{9,11},{10,... | collective-permute-start | bytes 245768 | tf_op jit(solution)/shard_map/ppermute | solution.py:28
  73.8 5.4 %collective-permute-start.10 = (bf16[64,1280]{1,0:T(8,128)(2,1)S(1)}, bf16[64,1280]{1,0:T(8,128)(2,1)S(1)}, u32[]{:S(2)}, u32[]{:S(2)}) collective-permute-start(bf16[64,1280]{1,0:T(8,128)(2,1)S(1)} %add_convert_fusion.5), channel_id=1, source_target_pairs={{0,8},{4,12},{8,0},{12,4},{16,24},{20,28},{24,16},{28,20},{1,9},{5... | collective-permute-start | bytes 491528 | tf_op jit(solution)/shard_map/ppermute | solution.py:28
  75.7 6.4 %collective-permute-start.16 = (f32[64,320]{1,0:T(8,128)S(1)}, f32[64,320]{1,0:T(8,128)S(1)}, u32[]{:S(2)}, u32[]{:S(2)}) collective-permute-start(f32[64,320]{1,0:T(8,128)S(1)} %fusion.5), channel_id=1, source_target_pairs={{0,4},{4,0},{8,12},{12,8},{16,20},{20,16},{24,28},{28,24},{1,5},{5... | collective-permute-start | bytes 245768 | tf_op jit(solution)/shard_map/ppermute | solution.py:28
  79.3 14.8 %collective-permute-start.11 = (bf16[64,1280]{1,0:T(8,128)(2,1)S(1)}, bf16[64,1280]{1,0:T(8,128)(2,1)S(1)}, u32[]{:S(2)}, u32[]{:S(2)}) collective-permute-start(bf16[64,1280]{1,0:T(8,128)(2,1)S(1)} %add_convert_fusion.4), channel_id=1, source_target_pairs={{0,16},{4,20},{8,24},{12,28},{16,0},{20,4},{24,8},{28,12},{1,17},{... | collective-permute-start | bytes 491528 | tf_op jit(solution)/shard_map/ppermute | solution.py:28
  82.2 4.7 %collective-permute-start.17 = (f32[64,320]{1,0:T(8,128)S(1)}, f32[64,320]{1,0:T(8,128)S(1)}, u32[]{:S(2)}, u32[]{:S(2)}) collective-permute-start(f32[64,320]{1,0:T(8,128)S(1)} %add.73), channel_id=1, source_target_pairs={{0,8},{4,12},{8,0},{12,4},{16,24},{20,28},{24,16},{28,20},{1,9},{5... | collective-permute-start | bytes 245768 | tf_op jit(solution)/shard_map/ppermute | solution.py:28
  83.9 13.7 %collective-permute-start.4 = (bf16[320,1024]{1,0:T(8,128)(2,1)S(1)}, bf16[320,1024]{1,0:T(8,128)(2,1)S(1)}, u32[]{:S(2)}, u32[]{:S(2)}) collective-permute-start(bf16[320,1024]{1,0:T(8,128)(2,1)S(1)} %get-tuple-element.33), channel_id=1, source_target_pairs={{0,1},{1,0},{2,3},{3,2},{4,5},{5,4},{6,7},{7,6},{8,9},{9,8},{10,11... | collective-permute-start | bytes 1966088 | tf_op jit(solution)/shard_map/ppermute | solution.py:28
  86.9 5.6 %collective-permute-start.18 = (f32[64,320]{1,0:T(8,128)S(1)}, f32[64,320]{1,0:T(8,128)S(1)}, u32[]{:S(2)}, u32[]{:S(2)}) collective-permute-start(f32[64,320]{1,0:T(8,128)S(1)} %add.74), channel_id=1, source_target_pairs={{0,16},{4,20},{8,24},{12,28},{16,0},{20,4},{24,8},{28,12},{1,17},{... | collective-permute-start | bytes 245768 | tf_op jit(solution)/shard_map/ppermute | solution.py:28
  88.6 12.0 %collective-permute-start.3 = (bf16[320,1024]{1,0:T(8,128)(2,1)S(1)}, bf16[320,1024]{1,0:T(8,128)(2,1)S(1)}, u32[]{:S(2)}, u32[]{:S(2)}) collective-permute-start(bf16[320,1024]{1,0:T(8,128)(2,1)S(1)} %get-tuple-element.31), channel_id=1, source_target_pairs={{0,1},{1,0},{2,3},{3,2},{4,5},{5,4},{6,7},{7,6},{8,9},{9,8},{10,11... | collective-permute-start | bytes 1966088 | tf_op jit(solution)/shard_map/ppermute | solution.py:28
  92.5 4.7 %collective-permute-start.19 = (f32[64,320]{1,0:T(8,128)S(1)}, f32[64,320]{1,0:T(8,128)S(1)}, u32[]{:S(2)}, u32[]{:S(2)}) collective-permute-start(f32[64,320]{1,0:T(8,128)S(1)} %add.75.refs_0_), channel_id=1, source_target_pairs={{0,2},{1,3},{2,0},{3,1},{4,6},{5,7},{6,4},{7,5},{8,10},{9,11},{10,... | collective-permute-start | bytes 245768 | tf_op jit(solution)/shard_map/ppermute | solution.py:28
  94.0 2.9 %copy-start.8 = (bf16[64,1280]{1,0:T(8,128)(2,1)}, bf16[64,1280]{1,0:T(8,128)(2,1)S(1)}, u32[]{:S(2)}) copy-start(bf16[64,1280]{1,0:T(8,128)(2,1)S(1)} %collective-permute-done.11) | copy-start | bytes 491524
  96.9 2.2 %collective-permute-start.24 = (f32[2,64,320]{2,1,0:T(8,128)S(1)}, f32[2,64,320]{2,1,0:T(8,128)S(1)}, u32[]{:S(2)}, u32[]{:S(2)}) collective-permute-start(f32[2,64,320]{2,1,0:T(8,128)S(1)} %get-tuple-element.47), channel_id=1, source_target_pairs={{0,1},{1,0},{2,3},{3,2},{4,5},{5,4},{6,7},{7,6},{8,9},{9,8},{10,11... | collective-permute-start | bytes 491528 | tf_op jit(solution)/shard_map/ppermute | solution.py:28
  97.2 3.8 %copy-start.3 = (bf16[320,1024]{1,0:T(8,128)(2,1)S(1)}, bf16[320,1024]{1,0:T(8,128)(2,1)}, u32[]{:S(2)}) copy-start(bf16[320,1024]{1,0:T(8,128)(2,1)} %copy-done.2) | copy-start | bytes 1966084
  97.2 3.8 %copy-start.5 = (bf16[1280,1024]{1,0:T(8,128)(2,1)S(1)}, bf16[1280,1024]{1,0:T(8,128)(2,1)}, u32[]{:S(2)}) copy-start(bf16[1280,1024]{1,0:T(8,128)(2,1)} %get-tuple-element.42.refs_8_) | copy-start | bytes 7864324
  97.2 3.7 %collective-permute-start.20 = (f32[2,64,320]{2,1,0:T(8,128)S(1)}, f32[2,64,320]{2,1,0:T(8,128)S(1)}, u32[]{:S(2)}, u32[]{:S(2)}) collective-permute-start(f32[2,64,320]{2,1,0:T(8,128)S(1)} %pad_maximum_fusion.2), channel_id=1, source_target_pairs={{0,1},{1,0},{2,3},{3,2},{4,5},{5,4},{6,7},{7,6},{8,9},{9,8},{10,11... | collective-permute-start | bytes 491528 | tf_op jit(solution)/shard_map/ppermute | solution.py:28
  97.9 17.7 %collective-permute-start.5 = (bf16[320,1024]{1,0:T(8,128)(2,1)S(1)}, bf16[320,1024]{1,0:T(8,128)(2,1)S(1)}, u32[]{:S(2)}, u32[]{:S(2)}) collective-permute-start(bf16[320,1024]{1,0:T(8,128)(2,1)S(1)} %add_convert_fusion), channel_id=1, source_target_pairs={{0,2},{1,3},{2,0},{3,1},{4,6},{5,7},{6,4},{7,5},{8,10},{9,11},{10,... | collective-permute-start | bytes 1966088 | tf_op jit(solution)/shard_map/ppermute | solution.py:28
  99.8 23.8 %collective-permute-start.25 = (f32[1,64,320]{2,1,0:T(8,128)}, f32[1,64,320]{2,1,0:T(8,128)}, u32[]{:S(2)}, u32[]{:S(2)}) collective-permute-start(f32[1,64,320]{2,1,0:T(8,128)} %slice_bitcast_fusion.2), channel_id=1, source_target_pairs={{0,2},{1,3},{2,0},{3,1},{4,6},{5,7},{6,4},{7,5},{8,10},{9,11},{10,... | collective-permute-start | bytes 245768 | tf_op jit(solution)/shard_map/ppermute | solution.py:28
  104.4 32.9 %collective-permute-start.21 = (bf16[64,1280]{1,0:T(8,128)(2,1)}, bf16[64,1280]{1,0:T(8,128)(2,1)}, u32[]{:S(2)}, u32[]{:S(2)}) collective-permute-start(bf16[64,1280]{1,0:T(8,128)(2,1)} %convert_element_type.111), channel_id=1, source_target_pairs={{0,4},{4,0},{8,12},{12,8},{16,20},{20,16},{24,28},{28,24},{1,5},{5... | collective-permute-start | bytes 491528 | tf_op jit(solution)/shard_map/ppermute | solution.py:28
  117.9 36.1 %copy-start.9 = (bf16[64,1280]{1,0:T(8,128)(2,1)S(1)}, bf16[64,1280]{1,0:T(8,128)(2,1)}, u32[]{:S(2)}) copy-start(bf16[64,1280]{1,0:T(8,128)(2,1)} %copy-done.8) | copy-start | bytes 491524
  117.9 61.6 %all-to-all-start = ((bf16[16,336,128]{2,1,0:T(8,128)(2,1)}), bf16[16,336,128]{2,1,0:T(8,128)(2,1)S(1)}, u32[]{:S(2)}, u32[]{:S(2)}) async-start(bf16[16,336,128]{2,1,0:T(8,128)(2,1)} %shard_map.121), calls=%async_computation | async-start | bytes 2752512 | tf_op jit(solution)/shard_map/all_to_all | solution.py:501
  124.5 12.0 %collective-permute-start.26 = (f32[64,320]{1,0:T(8,128)S(1)}, f32[64,320]{1,0:T(8,128)S(1)}, u32[]{:S(2)}, u32[]{:S(2)}) collective-permute-start(f32[64,320]{1,0:T(8,128)S(1)} %fusion.3), channel_id=1, source_target_pairs={{0,4},{4,0},{8,12},{12,8},{16,20},{20,16},{24,28},{28,24},{1,5},{5... | collective-permute-start | bytes 245768 | tf_op jit(solution)/shard_map/ppermute | solution.py:28
  136.5 11.9 %collective-permute-start.27 = (f32[64,320]{1,0:T(8,128)S(1)}, f32[64,320]{1,0:T(8,128)S(1)}, u32[]{:S(2)}, u32[]{:S(2)}) collective-permute-start(f32[64,320]{1,0:T(8,128)S(1)} %add.81), channel_id=1, source_target_pairs={{0,8},{4,12},{8,0},{12,4},{16,24},{20,28},{24,16},{28,20},{1,9},{5... | collective-permute-start | bytes 245768 | tf_op jit(solution)/shard_map/ppermute | solution.py:28
  138.3 22.9 %collective-permute-start.22 = (bf16[64,1280]{1,0:T(8,128)(2,1)S(1)}, bf16[64,1280]{1,0:T(8,128)(2,1)S(1)}, u32[]{:S(2)}, u32[]{:S(2)}) collective-permute-start(bf16[64,1280]{1,0:T(8,128)(2,1)S(1)} %add_convert_fusion.3), channel_id=1, source_target_pairs={{0,8},{4,12},{8,0},{12,4},{16,24},{20,28},{24,16},{28,20},{1,9},{5... | collective-permute-start | bytes 491528 | tf_op jit(solution)/shard_map/ppermute | solution.py:28
  148.4 11.0 %collective-permute-start.28 = (f32[64,320]{1,0:T(8,128)S(1)}, f32[64,320]{1,0:T(8,128)S(1)}, u32[]{:S(2)}, u32[]{:S(2)}) collective-permute-start(f32[64,320]{1,0:T(8,128)S(1)} %add.82), channel_id=1, source_target_pairs={{0,16},{4,20},{8,24},{12,28},{16,0},{20,4},{24,8},{28,12},{1,17},{... | collective-permute-start | bytes 245768 | tf_op jit(solution)/shard_map/ppermute | solution.py:28
  154.4 6.9 %collective-permute-start.12 = (f32[64,64]{1,0:T(8,128)S(1)}, f32[64,64]{1,0:T(8,128)S(1)}, u32[]{:S(2)}, u32[]{:S(2)}) collective-permute-start(f32[64,64]{1,0:T(8,128)S(1)} %fusion.8), channel_id=1, source_target_pairs={{0,1},{1,0},{2,3},{3,2},{4,5},{5,4},{6,7},{7,6},{8,9},{9,8},{10,11... | collective-permute-start | bytes 49160 | tf_op jit(solution)/shard_map/ppermute | solution.py:28
  159.4 10.7 %collective-permute-start.29 = (f32[64,320]{1,0:T(8,128)S(1)}, f32[64,320]{1,0:T(8,128)S(1)}, u32[]{:S(2)}, u32[]{:S(2)}) collective-permute-start(f32[64,320]{1,0:T(8,128)S(1)} %add.83.refs_0_), channel_id=1, source_target_pairs={{0,2},{1,3},{2,0},{3,1},{4,6},{5,7},{6,4},{7,5},{8,10},{9,11},{10,... | collective-permute-start | bytes 245768 | tf_op jit(solution)/shard_map/ppermute | solution.py:28
  161.3 8.9 %collective-permute-start.23 = (bf16[64,1280]{1,0:T(8,128)(2,1)S(1)}, bf16[64,1280]{1,0:T(8,128)(2,1)S(1)}, u32[]{:S(2)}, u32[]{:S(2)}) collective-permute-start(bf16[64,1280]{1,0:T(8,128)(2,1)S(1)} %add_convert_fusion.2), channel_id=1, source_target_pairs={{0,16},{4,20},{8,24},{12,28},{16,0},{20,4},{24,8},{28,12},{1,17},{... | collective-permute-start | bytes 491528 | tf_op jit(solution)/shard_map/ppermute | solution.py:28
  161.4 4.0 %collective-permute-start.13 = (f32[64,64]{1,0:T(8,128)S(1)}, f32[64,64]{1,0:T(8,128)S(1)}, u32[]{:S(2)}, u32[]{:S(2)}) collective-permute-start(f32[64,64]{1,0:T(8,128)S(1)} %add.69), channel_id=1, source_target_pairs={{0,2},{1,3},{2,0},{3,1},{4,6},{5,7},{6,4},{7,5},{8,10},{9,11},{10,... | collective-permute-start | bytes 49160 | tf_op jit(solution)/shard_map/ppermute | solution.py:28
  170.1 4.7 %collective-permute-start.30 = (f32[2,64,320]{2,1,0:T(8,128)S(1)}, f32[2,64,320]{2,1,0:T(8,128)S(1)}, u32[]{:S(2)}, u32[]{:S(2)}) collective-permute-start(f32[2,64,320]{2,1,0:T(8,128)S(1)} %pad_maximum_fusion.3), channel_id=1, source_target_pairs={{0,1},{1,0},{2,3},{3,2},{4,5},{5,4},{6,7},{7,6},{8,9},{9,8},{10,11... | collective-permute-start | bytes 491528 | tf_op jit(solution)/shard_map/ppermute | solution.py:28

commit v4 on v3

--- a/solution.py
+++ b/solution.py
@@ -172,12 +172,19 @@
         at += ref.shape[0]
 
 
+def joined(refs, held):
+    if len(refs) == 1:
+        return refs[0]
+    assemble(refs, held)
+    return held
+
+
 def lanes_kept(fill_ref, block):
     return lax.broadcasted_iota(jnp.int32, (1, BLOCK), 1) < fill_ref[block]
 
 
 def mask_tokens(x, fill_ref):
-    per = TILE // BLOCK
+    per = x.shape[1] // BLOCK
     parts = []
     for b in range(per):
         keep = lanes_kept(fill_ref, pl.program_id(0) * per + b)
@@ -285,27 +292,17 @@
     left_refs, refs = refs[:n_left], refs[n_left:]
     first_refs, refs = refs[:n_first], refs[n_first:]
     second_refs, refs = refs[:n_second], refs[n_second:]
-    out_refs, (left, first, second, acc) = refs[:-4], refs[-4:]
-
-    @pl.when(pl.program_id(0) == 0)
-    def _():
-        acc[...] = jnp.zeros_like(acc)
-        joined = jnp.concatenate([r[...] for r in left_refs], axis=1)
-        left[...] = stacked(joined)
-
-    assemble(first_refs, first)
-    assemble(second_refs, second)
+    out_refs, (left, first, second) = refs[:-3], refs[-3:]
+    left[...] = stacked(jnp.concatenate([r[...] for r in left_refs], axis=1))
+    first, second = joined(first_refs, first), joined(second_refs, second)
     v = fold(dot(left[...], first[...]))
     if masked:
         v = mask_tokens(v, fill_ref)
-    acc[...] += fold(dot(stacked(v), second[...], (1, 1)))
-
-    @pl.when(pl.program_id(0) == pl.num_programs(0) - 1)
-    def _():
-        if masked:
-            write_pieces(acc[...], *out_refs)
-        else:
-            out_refs[0][...] = acc[...]
+    product = fold(dot(stacked(v), second[...], (1, 1)))
+    if masked:
+        write_pieces(product, *out_refs)
+    else:
+        out_refs[0][...] = product
 
 
 def two_sided(lefts, firsts, seconds, fill, masked):
@@ -323,14 +320,12 @@
         outs,
         (*lefts, *firsts, *seconds),
         (fill,),
-        grid=(total // TILE,),
-        in_specs=[whole(x) for x in lefts] + [tokens_of(x) for x in (*firsts, *seconds)],
+        in_specs=[whole(x) for x in (*lefts, *firsts, *seconds)],
         out_specs=[whole(o) for o in outs],
         scratch=[
             pltpu.VMEM((2 * rank, inner), bf16),
-            pltpu.VMEM((inner, TILE), bf16),
-            pltpu.VMEM((outer, TILE), bf16),
-            pltpu.VMEM((rank, outer), f32),
+            pltpu.VMEM((inner, total), bf16),
+            pltpu.VMEM((outer, total), bf16),
         ],
         flops=4 * rank * (inner + outer) * total,
     )
@@ -407,7 +402,7 @@
 def outer(inv, left, raws, me):
     rows, triple = left.shape
     columns = sum(r.shape[1] for r in raws)
-    strip = 2 * BLOCK if rows % (2 * BLOCK) == 0 else BLOCK
+    strip = rows // 2
     outs = [struct((triple // 3, columns), f32), struct((rows, columns), f32)]
     return call(
         functools.partial(outer_kernel, len(raws)),

time: 181 us -> 180 us (level)
  Pallas kernels: 54.9 us -> 52 us
  waiting for transfers between devices: 75.1 us -> 77.8 us
    pallas_call x10, Pallas kernels: 54.9 us -> 52 us  [kernel_call(): pl.pallas_call(body, out_shape=out_shape, grid_spec=pltpu.PrefetchScalarG...]
    ppermute x31, waiting for transfers between devices: 75.1 us -> 77.8 us  [swap(): return lax.ppermute(x, axis, [(i, i ^ bit) for i in range(count)])]
  transfers between devices with their start and end apart: 32 -> 32, of which waited for: 12 -> 12; matrix products, arithmetic and copies ran while one was open for 4% -> 4% of each run, Pallas kernels for 23% -> 22%
where the time goes in v4:
time: 180 us; the launch traced here: 179 us
  waiting for transfers between devices  77.8 us (43%)
  Pallas kernels  52 us (29%)
  starting transfers between devices  39.6 us (22%)
  other arithmetic  6.04 us (3%)
  local copies, waits for them, and re-layouts  2.54 us (1%)
    ppermute x31, waiting for transfers between devices, swap(): return lax.ppermute(x, axis, [(i, i ^ bit) for i in range(count)])  77.8 us
    pallas_call x10, Pallas kernels, kernel_call(): pl.pallas_call(body, out_shape=out_shape, grid_spec=pltpu.PrefetchScalarG...  52 us
    ppermute x31, starting transfers between devices, swap(): return lax.ppermute(x, axis, [(i, i ^ bit) for i in range(count)])  33.9 us
    all_to_all x1, starting transfers between devices, local(): lax.all_to_all(sent, 'dp', split_axis=0, concat_axis=0, tiled=True)  5.67 us
  transfers between devices with their start and end apart: 32, of which 12 were waited for; matrix products, arithmetic and copies ran while one was open for 4% of the time, Pallas kernels for 22%

profile of v4, /device:TPU:0, one launch (start us, length us, event | category | flops | bytes accessed | tf_op | source)
XLA Modules:
  0.0 179.5 jit_solution(10736384609078860764)
XLA Ops:
  0.6 0.6 collective-permute-start
  1.2 2.6 %collective-permute-start.1 = (bf16[320,1024]{1,0:T(8,128)(2,1)}, bf16[320,1024]{1,0:T(8,128)(2,1)S(1)}, u32[]{:S(2)}, u32[]{:S(2)}) collective-permute-start(bf16[320,1024]{1,0:T(8,128)(2,1)} %bitcast.47), channel_id=1, source_target_pairs={{0,2},{1,3},{2,0},{3,1},{4,6},{5,7},{6,4},{7,5},{8,10},{9,11},{10,... | collective-permute-start | bytes 1966088 | tf_op jit(solution)/shard_map/ppermute | solution.py:28
  4.2 1.2 broadcast_select_fusion
  5.5 1.0 reduce-precision_convert_fusion.1
  6.6 13.0 %collective-permute-done.1.refs_2_.refs_6_ = bf16[320,1024]{1,0:T(8,128)(2,1)S(1)} collective-permute-done((bf16[320,1024]{1,0:T(8,128)(2,1)}, bf16[320,1024]{1,0:T(8,128)(2,1)S(1)}, u32[]{:S(2)}, u32[]{:S(2)}) %collective-permute-start.1) | collective-permute-done | bytes 655392 | tf_op jit(solution)/shard_map/ppermute | solution.py:28
  19.7 13.7 %collective-permute-done.7.refs_2_.refs_4_ = bf16[320,1024]{1,0:T(8,128)(2,1)S(1)} collective-permute-done((bf16[320,1024]{1,0:T(8,128)(2,1)}, bf16[320,1024]{1,0:T(8,128)(2,1)S(1)}, u32[]{:S(2)}, u32[]{:S(2)}) %collective-permute-start.7) | collective-permute-done | bytes 655392 | tf_op jit(solution)/shard_map/ppermute | solution.py:28
  33.6 7.9 %shard_map.119 = (bf16[1280,1280]{1,0:T(8,128)(2,1)S(1)}, bf16[1280,1280]{1,0:T(8,128)(2,1)}, bf16[1280,1280]{1,0:T(8,128)(2,1)}) custom-call(s32[1]{0:T(128)} %bitcast.1.me_ref, bf16[1280,1280]{1,0:T(8,128)(2,1)} %up_ref.1, bf16[1280,1280]{1,0:T(8,128)(2,1)} %down_ref.1), custom_call_target="tpu_custom_call" | custom-call | bytes 16384000 | tf_op jit(solution)/shard_map/pallas_call | solution.py:107
  41.5 1.7 copy-done.7
  43.2 12.5 %shard_map.120 = (bf16[1280,1024]{1,0:T(8,128)(2,1)}, bf16[1280,1024]{1,0:T(8,128)(2,1)}, bf16[320,1024]{1,0:T(8,128)(2,1)S(1)}, bf16[320,1024]{1,0:T(8,128)(2,1...) custom-call(s32[8]{0:T(128)S(1)} %copy-done.6, bf16[320,1024]{1,0:T(8,128)(2,1)S(1)} %bitcast.48, ...), custom_call_target="tpu_custom_call" | custom-call | flops 6710886400 | bytes 17039360 | tf_op jit(solution)/shard_map/pallas_call | solution.py:107
  55.8 11.3 %shard_map.123 = (bf16[1280,1024]{1,0:T(8,128)(2,1)}, f32[2,64,320]{2,1,0:T(8,128)S(1)}, f32[2,64,320]{2,1,0:T(8,128)S(1)}, f32[64,1280]{1,0:T(8,128)S(1)}) custom-call(s32[8]{0:T(128)S(1)} %copy-done.6, bf16[320,1024]{1,0:T(8,128)(2,1)S(1)} %bitcast.53, bf16[320,1024]{1,0:T(8,128)(2,1)S(1)} %collective-permute-done.6.refs_1_.refs_3_, ...), custom_call_target="tpu_custom_call" | custom-call | flops 3355443200 | bytes 17694720 | tf_op jit(solution)/shard_map/pallas_call | solution.py:107
  67.6 1.8 collective-permute-start.9
  69.4 1.6 collective-permute-start.15
  71.0 2.8 %collective-permute-done.9 = bf16[64,1280]{1,0:T(8,128)(2,1)S(1)} collective-permute-done((bf16[64,1280]{1,0:T(8,128)(2,1)S(1)}, bf16[64,1280]{1,0:T(8,128)(2,1)S(1)}, u32[]{:S(2)}, u32[]{:S(2)}) %collective-permute-start.9) | collective-permute-done | bytes 163872 | tf_op jit(solution)/shard_map/ppermute | solution.py:28
  73.8 1.9 %collective-permute-start.10 = (bf16[64,1280]{1,0:T(8,128)(2,1)S(1)}, bf16[64,1280]{1,0:T(8,128)(2,1)S(1)}, u32[]{:S(2)}, u32[]{:S(2)}) collective-permute-start(bf16[64,1280]{1,0:T(8,128)(2,1)S(1)} %add_convert_fusion.5), channel_id=1, source_target_pairs={{0,8},{4,12},{8,0},{12,4},{16,24},{20,28},{24,16},{28,20},{1,9},{5... | collective-permute-start | bytes 491528 | tf_op jit(solution)/shard_map/ppermute | solution.py:28
  75.7 1.6 collective-permute-start.16
  77.3 1.9 %collective-permute-done.10 = bf16[64,1280]{1,0:T(8,128)(2,1)S(1)} collective-permute-done((bf16[64,1280]{1,0:T(8,128)(2,1)S(1)}, bf16[64,1280]{1,0:T(8,128)(2,1)S(1)}, u32[]{:S(2)}, u32[]{:S(2)}) %collective-permute-start.10) | collective-permute-done | bytes 163872 | tf_op jit(solution)/shard_map/ppermute | solution.py:28
  79.3 2.9 %collective-permute-start.11 = (bf16[64,1280]{1,0:T(8,128)(2,1)S(1)}, bf16[64,1280]{1,0:T(8,128)(2,1)S(1)}, u32[]{:S(2)}, u32[]{:S(2)}) collective-permute-start(bf16[64,1280]{1,0:T(8,128)(2,1)S(1)} %add_convert_fusion.4), channel_id=1, source_target_pairs={{0,16},{4,20},{8,24},{12,28},{16,0},{20,4},{24,8},{28,12},{1,17},{... | collective-permute-start | bytes 491528 | tf_op jit(solution)/shard_map/ppermute | solution.py:28
  82.2 1.6 collective-permute-start.17
  83.9 2.9 %collective-permute-done.17 = f32[64,320]{1,0:T(8,128)S(1)} collective-permute-done((f32[64,320]{1,0:T(8,128)S(1)}, f32[64,320]{1,0:T(8,128)S(1)}, u32[]{:S(2)}, u32[]{:S(2)}) %collective-permute-start.17) | collective-permute-done | bytes 81952 | tf_op jit(solution)/shard_map/ppermute | solution.py:28
  86.9 1.7 collective-permute-start.18
  88.7 3.8 %collective-permute-done.18 = f32[64,320]{1,0:T(8,128)S(1)} collective-permute-done((f32[64,320]{1,0:T(8,128)S(1)}, f32[64,320]{1,0:T(8,128)S(1)}, u32[]{:S(2)}, u32[]{:S(2)}) %collective-permute-start.18) | collective-permute-done | bytes 81952 | tf_op jit(solution)/shard_map/ppermute | solution.py:28
  92.5 1.6 collective-permute-start.19
  94.1 2.0 %shard_map.127 = (f32[2,64,320]{2,1,0:T(8,128)S(1)}, f32[2,64,320]{2,1,0:T(8,128)S(1)}) custom-call(s32[8]{0:T(128)S(1)} %copy-done.6, f32[64,1280]{1,0:T(8,128)S(1)} %convert_add_fusion.1.down_ref.refs_0_, bf16[1280,1024]{1,0:T(8,128)(2,1)S(1)} %copy-done, bf16[320,1024]{1,0:T(8,128)(2,1)S(1)} %bitcast.54, ...), custom_call_target="tpu_custom_call" | custom-call | flops 671088640 | bytes 5898240 | tf_op jit(solution)/shard_map/pallas_call | solution.py:107
  96.2 0.9 collective-permute-done.19.refs_2_
  97.5 1.6 collective-permute-start.5
  99.1 0.6 slice_bitcast_fusion.2
  100.6 2.0 %shard_map.125 = f32[64,1280]{1,0:T(8,128)S(1)} custom-call(s32[8]{0:T(128)S(1)} %copy-done.6, f32[64,320]{1,0:T(8,128)S(1)} %add.75.refs_0_, f32[64,320]{1,0:T(8,128)S(1)} %get-tuple-element.62.refs_1_, f32[64,320]{1,0:T(8,128)S(1)} %collective-permute-done.19.refs_2_, f32[64,320]{1,0:T(8,128)S(1)} %get-tuple-element.61.refs_3_, ...), custom_call_target="tpu_custom_call" | custom-call | flops 671088640 | bytes 5898240 | tf_op jit(solution)/shard_map/pallas_call | solution.py:107
  102.6 0.7 convert_element_type.111
  103.3 1.5 collective-permute-start.21
  104.7 10.4 %collective-permute-done.5.b_ref = bf16[320,1024]{1,0:T(8,128)(2,1)S(1)} collective-permute-done((bf16[320,1024]{1,0:T(8,128)(2,1)S(1)}, bf16[320,1024]{1,0:T(8,128)(2,1)S(1)}, u32[]{:S(2)}, u32[]{:S(2)}) %collective-permute-start.5) | collective-permute-done | bytes 655392 | tf_op jit(solution)/shard_map/ppermute | solution.py:28
  115.2 2.3 %shard_map.121 = bf16[16,336,128]{2,1,0:T(8,128)(2,1)} custom-call(s32[16]{0:T(128)S(1)} %select_reduce_fusion.index_ref, s32[16]{0:T(128)S(1)} %convert_element_type.91.ok_ref, bf16[320,1024]{1,0:T(8,128)(2,1)S(1)} %add_convert_fusion.1.a_ref, bf16[320,1024]{1,0:T(8,128)(2,1)S(1)} %collective-permute-done.5.b_ref), custom_call_target="tpu_custom_call" | custom-call | bytes 2686976 | tf_op jit(solution)/shard_map/pallas_call | solution.py:107
  117.5 5.7 %all-to-all-start = ((bf16[16,336,128]{2,1,0:T(8,128)(2,1)}), bf16[16,336,128]{2,1,0:T(8,128)(2,1)S(1)}, u32[]{:S(2)}, u32[]{:S(2)}) async-start(bf16[16,336,128]{2,1,0:T(8,128)(2,1)} %shard_map.121), calls=%async_computation | async-start | bytes 2752512 | tf_op jit(solution)/shard_map/all_to_all | solution.py:496
  123.2 0.9 fusion.3
  124.1 2.1 %collective-permute-start.26 = (f32[64,320]{1,0:T(8,128)S(1)}, f32[64,320]{1,0:T(8,128)S(1)}, u32[]{:S(2)}, u32[]{:S(2)}) collective-permute-start(f32[64,320]{1,0:T(8,128)S(1)} %fusion.3), channel_id=1, source_target_pairs={{0,4},{4,0},{8,12},{12,8},{16,20},{20,16},{24,28},{28,24},{1,5},{5... | collective-permute-start | bytes 245768 | tf_op jit(solution)/shard_map/ppermute | solution.py:28
  126.2 10.5 %collective-permute-done.26 = f32[64,320]{1,0:T(8,128)S(1)} collective-permute-done((f32[64,320]{1,0:T(8,128)S(1)}, f32[64,320]{1,0:T(8,128)S(1)}, u32[]{:S(2)}, u32[]{:S(2)}) %collective-permute-start.26) | collective-permute-done | bytes 81952 | tf_op jit(solution)/shard_map/ppermute | solution.py:28
  136.7 1.0 collective-permute-start.27
  137.7 0.9 add_convert_fusion.3
  138.6 1.2 collective-permute-start.22
  139.8 8.9 %collective-permute-done.27 = f32[64,320]{1,0:T(8,128)S(1)} collective-permute-done((f32[64,320]{1,0:T(8,128)S(1)}, f32[64,320]{1,0:T(8,128)S(1)}, u32[]{:S(2)}, u32[]{:S(2)}) %collective-permute-start.27) | collective-permute-done | bytes 81952 | tf_op jit(solution)/shard_map/ppermute | solution.py:28
  148.7 4.9 %collective-permute-start.28 = (f32[64,320]{1,0:T(8,128)S(1)}, f32[64,320]{1,0:T(8,128)S(1)}, u32[]{:S(2)}, u32[]{:S(2)}) collective-permute-start(f32[64,320]{1,0:T(8,128)S(1)} %add.82), channel_id=1, source_target_pairs={{0,16},{4,20},{8,24},{12,28},{16,0},{20,4},{24,8},{28,12},{1,17},{... | collective-permute-start | bytes 245768 | tf_op jit(solution)/shard_map/ppermute | solution.py:28
  154.1 5.5 %collective-permute-done.28 = f32[64,320]{1,0:T(8,128)S(1)} collective-permute-done((f32[64,320]{1,0:T(8,128)S(1)}, f32[64,320]{1,0:T(8,128)S(1)}, u32[]{:S(2)}, u32[]{:S(2)}) %collective-permute-start.28) | collective-permute-done | bytes 81952 | tf_op jit(solution)/shard_map/ppermute | solution.py:28
  159.6 1.6 collective-permute-start.29
  161.4 0.6 collective-permute-start.13
  161.9 3.4 %collective-permute-done.13 = f32[64,64]{1,0:T(8,128)S(1)} collective-permute-done((f32[64,64]{1,0:T(8,128)S(1)}, f32[64,64]{1,0:T(8,128)S(1)}, u32[]{:S(2)}, u32[]{:S(2)}) %collective-permute-start.13) | collective-permute-done | bytes 16416 | tf_op jit(solution)/shard_map/ppermute | solution.py:28
  165.4 4.7 %shard_map.124 = (f32[64,64]{1,0:T(8,128)S(1)}, f32[64,64]{1,0:T(8,128)S(1)}, bf16[1280,192]{1,0:T(8,128)(2,1)S(1)}, bf16[1280,192]{1,0:T(8,128)(2,1)S(1)}) custom-call(s32[1]{0:T(128)} %bitcast.1.me_ref, f32[64,64]{1,0:T(8,128)S(1)} %add.70.gram_ref, f32[64,1280]{1,0:T(8,128)S(1)} %convert_add_fusion.1.down_ref.refs_0_, f32[64,320]{1,0:T(8,128)S(1)} %add.75.refs_0_, ...), custom_call_target="tpu_custom_call" | custom-call | flops 268435456 | bytes 1687552 | tf_op jit(solution)/shard_map/pallas_call | solution.py:107
  170.3 3.9 %shard_map.126 = (f32[64,1280]{1,0:T(8,128)}, f32[1280,1280]{1,0:T(8,128)}) custom-call(s32[1]{0:T(128)} %bitcast.1.me_ref, f32[64,64]{1,0:T(8,128)S(1)} %get-tuple-element.40.inv_ref, bf16[1280,192]{1,0:T(8,128)(2,1)S(1)} %get-tuple-element.41.left_ref, f32[64,1280]{1,0:T(8,128)S(1)} %convert_add_fusion.refs_0_), custom_call_target="tpu_custom_call" | custom-call | flops 629145600 | bytes 7716864 | tf_op jit(solution)/shard_map/pallas_call | solution.py:107
  174.2 4.0 %shard_map.128 = (f32[64,1280]{1,0:T(8,128)}, f32[1280,1280]{1,0:T(8,128)}) custom-call(s32[1]{0:T(128)} %bitcast.1.me_ref, f32[64,64]{1,0:T(8,128)S(1)} %get-tuple-element.44.inv_ref, bf16[1280,192]{1,0:T(8,128)(2,1)S(1)} %get-tuple-element.45.left_ref, f32[64,320]{1,0:T(8,128)S(1)} %add.83.refs_0_, f32[64,320]{1,0:T(8,128)S(1)} %get-tuple-element.60.refs_1_, ...), custom_call_target="tpu_custom_call" | custom-call | flops 629145600 | bytes 7716864 | tf_op jit(solution)/shard_map/pallas_call | solution.py:107
  178.2 1.3 shard_map.122
  (87 shorter events, 3.9 us)
Async XLA Ops:
  0.6 32.7 %copy-start.10 = (s32[8]{0:T(128)S(1)}, s32[8]{0:T(128)}, u32[]{:S(2)}) copy-start(s32[8]{0:T(128)} %param.10) | copy-start | bytes 100
  0.6 42.5 %collective-permute-start = (bf16[320,1024]{1,0:T(8,128)(2,1)}, bf16[320,1024]{1,0:T(8,128)(2,1)S(1)}, u32[]{:S(2)}, u32[]{:S(2)}) collective-permute-start(bf16[320,1024]{1,0:T(8,128)(2,1)} %bitcast.46), channel_id=1, source_target_pairs={{0,1},{1,0},{2,3},{3,2},{4,5},{5,4},{6,7},{7,6},{8,9},{9,8},{10,11... | collective-permute-start | bytes 1966088 | tf_op jit(solution)/shard_map/ppermute | solution.py:28
  1.2 18.4 %collective-permute-start.1 = (bf16[320,1024]{1,0:T(8,128)(2,1)}, bf16[320,1024]{1,0:T(8,128)(2,1)S(1)}, u32[]{:S(2)}, u32[]{:S(2)}) collective-permute-start(bf16[320,1024]{1,0:T(8,128)(2,1)} %bitcast.47), channel_id=1, source_target_pairs={{0,2},{1,3},{2,0},{3,1},{4,6},{5,7},{6,4},{7,5},{8,10},{9,11},{10,... | collective-permute-start | bytes 1966088 | tf_op jit(solution)/shard_map/ppermute | solution.py:28
  3.8 52.0 %collective-permute-start.6 = (bf16[320,1024]{1,0:T(8,128)(2,1)}, bf16[320,1024]{1,0:T(8,128)(2,1)S(1)}, u32[]{:S(2)}, u32[]{:S(2)}) collective-permute-start(bf16[320,1024]{1,0:T(8,128)(2,1)} %bitcast.51), channel_id=1, source_target_pairs={{0,1},{1,0},{2,3},{3,2},{4,5},{5,4},{6,7},{7,6},{8,9},{9,8},{10,11... | collective-permute-start | bytes 1966088 | tf_op jit(solution)/shard_map/ppermute | solution.py:28
  3.9 29.4 %collective-permute-start.7 = (bf16[320,1024]{1,0:T(8,128)(2,1)}, bf16[320,1024]{1,0:T(8,128)(2,1)S(1)}, u32[]{:S(2)}, u32[]{:S(2)}) collective-permute-start(bf16[320,1024]{1,0:T(8,128)(2,1)} %bitcast.52), channel_id=1, source_target_pairs={{0,2},{1,3},{2,0},{3,1},{4,6},{5,7},{6,4},{7,5},{8,10},{9,11},{10,... | collective-permute-start | bytes 1966088 | tf_op jit(solution)/shard_map/ppermute | solution.py:28
  19.6 23.6 %collective-permute-start.2 = (bf16[320,1024]{1,0:T(8,128)(2,1)S(1)}, bf16[320,1024]{1,0:T(8,128)(2,1)S(1)}, u32[]{:S(2)}, u32[]{:S(2)}) collective-permute-start(bf16[320,1024]{1,0:T(8,128)(2,1)S(1)} %collective-permute-done.1.refs_2_.refs_6_), channel_id=1, source_target_pairs={{0,1},{1,0},{2,3},{3,2},{4,5},{5,4},{6,7},{7,6},{8,9},{9,8},{10,11... | collective-permute-start | bytes 1966088 | tf_op jit(solution)/shard_map/ppermute | solution.py:28
  33.4 22.4 %collective-permute-start.8 = (bf16[320,1024]{1,0:T(8,128)(2,1)S(1)}, bf16[320,1024]{1,0:T(8,128)(2,1)S(1)}, u32[]{:S(2)}, u32[]{:S(2)}) collective-permute-start(bf16[320,1024]{1,0:T(8,128)(2,1)S(1)} %collective-permute-done.7.refs_2_.refs_4_), channel_id=1, source_target_pairs={{0,1},{1,0},{2,3},{3,2},{4,5},{5,4},{6,7},{7,6},{8,9},{9,8},{10,11... | collective-permute-start | bytes 1966088 | tf_op jit(solution)/shard_map/ppermute | solution.py:28
  33.5 9.6 %copy-start.1 = (bf16[1024,320]{0,1:T(8,128)(2,1)S(1)}, bf16[1024,320]{0,1:T(8,128)(2,1)}, u32[]{:S(2)}) copy-start(bf16[1024,320]{0,1:T(8,128)(2,1)} %param.8) | copy-start | bytes 1966084
  33.6 9.6 %copy-start.6 = (s32[8]{0:T(128)S(1)}, s32[8]{0:T(128)}, u32[]{:S(2)}) copy-start(s32[8]{0:T(128)} %fill_ref.7) | copy-start | bytes 100
  41.5 1.7 copy-start.7
  43.2 12.6 %copy-start.2 = (bf16[320,1024]{1,0:T(8,128)(2,1)}, bf16[320,1024]{1,0:T(8,128)(2,1)S(1)}, u32[]{:S(2)}) copy-start(bf16[320,1024]{1,0:T(8,128)(2,1)S(1)} %collective-permute-done.2.refs_3_.refs_7_) | copy-start | bytes 1966084
  43.2 12.6 %copy-start.4 = (bf16[1024,320]{0,1:T(8,128)(2,1)S(1)}, bf16[1024,320]{0,1:T(8,128)(2,1)}, u32[]{:S(2)}) copy-start(bf16[1024,320]{0,1:T(8,128)(2,1)} %param.9) | copy-start | bytes 1966084
  67.1 27.0 %copy-start = (bf16[1280,1024]{1,0:T(8,128)(2,1)S(1)}, bf16[1280,1024]{1,0:T(8,128)(2,1)}, u32[]{:S(2)}) copy-start(bf16[1280,1024]{1,0:T(8,128)(2,1)} %get-tuple-element.35.refs_9_.refs_1_) | copy-start | bytes 7864324
  67.1 2.3 %collective-permute-start.14 = (f32[2,64,320]{2,1,0:T(8,128)S(1)}, f32[2,64,320]{2,1,0:T(8,128)S(1)}, u32[]{:S(2)}, u32[]{:S(2)}) collective-permute-start(f32[2,64,320]{2,1,0:T(8,128)S(1)} %get-tuple-element.39), channel_id=1, source_target_pairs={{0,1},{1,0},{2,3},{3,2},{4,5},{5,4},{6,7},{7,6},{8,9},{9,8},{10,11... | collective-permute-start | bytes 491528 | tf_op jit(solution)/shard_map/ppermute | solution.py:28
  67.6 6.2 %collective-permute-start.9 = (bf16[64,1280]{1,0:T(8,128)(2,1)S(1)}, bf16[64,1280]{1,0:T(8,128)(2,1)S(1)}, u32[]{:S(2)}, u32[]{:S(2)}) collective-permute-start(bf16[64,1280]{1,0:T(8,128)(2,1)S(1)} %convert_element_type.102), channel_id=1, source_target_pairs={{0,4},{4,0},{8,12},{12,8},{16,20},{20,16},{24,28},{28,24},{1,5},{5... | collective-permute-start | bytes 491528 | tf_op jit(solution)/shard_map/ppermute | solution.py:28
  69.4 6.3 %collective-permute-start.15 = (f32[1,64,320]{2,1,0:T(8,128)S(1)}, f32[1,64,320]{2,1,0:T(8,128)S(1)}, u32[]{:S(2)}, u32[]{:S(2)}) collective-permute-start(f32[1,64,320]{2,1,0:T(8,128)S(1)} %slice_bitcast_fusion.6), channel_id=1, source_target_pairs={{0,2},{1,3},{2,0},{3,1},{4,6},{5,7},{6,4},{7,5},{8,10},{9,11},{10,... | collective-permute-start | bytes 245768 | tf_op jit(solution)/shard_map/ppermute | solution.py:28
  73.8 5.4 %collective-permute-start.10 = (bf16[64,1280]{1,0:T(8,128)(2,1)S(1)}, bf16[64,1280]{1,0:T(8,128)(2,1)S(1)}, u32[]{:S(2)}, u32[]{:S(2)}) collective-permute-start(bf16[64,1280]{1,0:T(8,128)(2,1)S(1)} %add_convert_fusion.5), channel_id=1, source_target_pairs={{0,8},{4,12},{8,0},{12,4},{16,24},{20,28},{24,16},{28,20},{1,9},{5... | collective-permute-start | bytes 491528 | tf_op jit(solution)/shard_map/ppermute | solution.py:28
  75.7 6.4 %collective-permute-start.16 = (f32[64,320]{1,0:T(8,128)S(1)}, f32[64,320]{1,0:T(8,128)S(1)}, u32[]{:S(2)}, u32[]{:S(2)}) collective-permute-start(f32[64,320]{1,0:T(8,128)S(1)} %fusion.5), channel_id=1, source_target_pairs={{0,4},{4,0},{8,12},{12,8},{16,20},{20,16},{24,28},{28,24},{1,5},{5... | collective-permute-start | bytes 245768 | tf_op jit(solution)/shard_map/ppermute | solution.py:28
  79.3 14.8 %collective-permute-start.11 = (bf16[64,1280]{1,0:T(8,128)(2,1)S(1)}, bf16[64,1280]{1,0:T(8,128)(2,1)S(1)}, u32[]{:S(2)}, u32[]{:S(2)}) collective-permute-start(bf16[64,1280]{1,0:T(8,128)(2,1)S(1)} %add_convert_fusion.4), channel_id=1, source_target_pairs={{0,16},{4,20},{8,24},{12,28},{16,0},{20,4},{24,8},{28,12},{1,17},{... | collective-permute-start | bytes 491528 | tf_op jit(solution)/shard_map/ppermute | solution.py:28
  82.2 4.7 %collective-permute-start.17 = (f32[64,320]{1,0:T(8,128)S(1)}, f32[64,320]{1,0:T(8,128)S(1)}, u32[]{:S(2)}, u32[]{:S(2)}) collective-permute-start(f32[64,320]{1,0:T(8,128)S(1)} %add.73), channel_id=1, source_target_pairs={{0,8},{4,12},{8,0},{12,4},{16,24},{20,28},{24,16},{28,20},{1,9},{5... | collective-permute-start | bytes 245768 | tf_op jit(solution)/shard_map/ppermute | solution.py:28
  83.9 13.4 %collective-permute-start.4 = (bf16[320,1024]{1,0:T(8,128)(2,1)S(1)}, bf16[320,1024]{1,0:T(8,128)(2,1)S(1)}, u32[]{:S(2)}, u32[]{:S(2)}) collective-permute-start(bf16[320,1024]{1,0:T(8,128)(2,1)S(1)} %get-tuple-element.33), channel_id=1, source_target_pairs={{0,1},{1,0},{2,3},{3,2},{4,5},{5,4},{6,7},{7,6},{8,9},{9,8},{10,11... | collective-permute-start | bytes 1966088 | tf_op jit(solution)/shard_map/ppermute | solution.py:28
  86.9 5.6 %collective-permute-start.18 = (f32[64,320]{1,0:T(8,128)S(1)}, f32[64,320]{1,0:T(8,128)S(1)}, u32[]{:S(2)}, u32[]{:S(2)}) collective-permute-start(f32[64,320]{1,0:T(8,128)S(1)} %add.74), channel_id=1, source_target_pairs={{0,16},{4,20},{8,24},{12,28},{16,0},{20,4},{24,8},{28,12},{1,17},{... | collective-permute-start | bytes 245768 | tf_op jit(solution)/shard_map/ppermute | solution.py:28
  88.6 11.7 %collective-permute-start.3 = (bf16[320,1024]{1,0:T(8,128)(2,1)S(1)}, bf16[320,1024]{1,0:T(8,128)(2,1)S(1)}, u32[]{:S(2)}, u32[]{:S(2)}) collective-permute-start(bf16[320,1024]{1,0:T(8,128)(2,1)S(1)} %get-tuple-element.31), channel_id=1, source_target_pairs={{0,1},{1,0},{2,3},{3,2},{4,5},{5,4},{6,7},{7,6},{8,9},{9,8},{10,11... | collective-permute-start | bytes 1966088 | tf_op jit(solution)/shard_map/ppermute | solution.py:28
  92.5 4.7 %collective-permute-start.19 = (f32[64,320]{1,0:T(8,128)S(1)}, f32[64,320]{1,0:T(8,128)S(1)}, u32[]{:S(2)}, u32[]{:S(2)}) collective-permute-start(f32[64,320]{1,0:T(8,128)S(1)} %add.75.refs_0_), channel_id=1, source_target_pairs={{0,2},{1,3},{2,0},{3,1},{4,6},{5,7},{6,4},{7,5},{8,10},{9,11},{10,... | collective-permute-start | bytes 245768 | tf_op jit(solution)/shard_map/ppermute | solution.py:28
  94.0 2.1 %copy-start.8 = (bf16[64,1280]{1,0:T(8,128)(2,1)}, bf16[64,1280]{1,0:T(8,128)(2,1)S(1)}, u32[]{:S(2)}) copy-start(bf16[64,1280]{1,0:T(8,128)(2,1)S(1)} %collective-permute-done.11) | copy-start | bytes 491524
  96.2 2.9 %collective-permute-start.24 = (f32[2,64,320]{2,1,0:T(8,128)S(1)}, f32[2,64,320]{2,1,0:T(8,128)S(1)}, u32[]{:S(2)}, u32[]{:S(2)}) collective-permute-start(f32[2,64,320]{2,1,0:T(8,128)S(1)} %get-tuple-element.47), channel_id=1, source_target_pairs={{0,1},{1,0},{2,3},{3,2},{4,5},{5,4},{6,7},{7,6},{8,9},{9,8},{10,11... | collective-permute-start | bytes 491528 | tf_op jit(solution)/shard_map/ppermute | solution.py:28
  97.2 3.4 %copy-start.3 = (bf16[320,1024]{1,0:T(8,128)(2,1)S(1)}, bf16[320,1024]{1,0:T(8,128)(2,1)}, u32[]{:S(2)}) copy-start(bf16[320,1024]{1,0:T(8,128)(2,1)} %copy-done.2) | copy-start | bytes 1966084
  97.2 3.4 %copy-start.5 = (bf16[1280,1024]{1,0:T(8,128)(2,1)S(1)}, bf16[1280,1024]{1,0:T(8,128)(2,1)}, u32[]{:S(2)}) copy-start(bf16[1280,1024]{1,0:T(8,128)(2,1)} %get-tuple-element.42.refs_8_) | copy-start | bytes 7864324
  97.2 3.4 %collective-permute-start.20 = (f32[2,64,320]{2,1,0:T(8,128)S(1)}, f32[2,64,320]{2,1,0:T(8,128)S(1)}, u32[]{:S(2)}, u32[]{:S(2)}) collective-permute-start(f32[2,64,320]{2,1,0:T(8,128)S(1)} %pad_maximum_fusion.2), channel_id=1, source_target_pairs={{0,1},{1,0},{2,3},{3,2},{4,5},{5,4},{6,7},{7,6},{8,9},{9,8},{10,11... | collective-permute-start | bytes 491528 | tf_op jit(solution)/shard_map/ppermute | solution.py:28
  97.5 17.7 %collective-permute-start.5 = (bf16[320,1024]{1,0:T(8,128)(2,1)S(1)}, bf16[320,1024]{1,0:T(8,128)(2,1)S(1)}, u32[]{:S(2)}, u32[]{:S(2)}) collective-permute-start(bf16[320,1024]{1,0:T(8,128)(2,1)S(1)} %add_convert_fusion), channel_id=1, source_target_pairs={{0,2},{1,3},{2,0},{3,1},{4,6},{5,7},{6,4},{7,5},{8,10},{9,11},{10,... | collective-permute-start | bytes 1966088 | tf_op jit(solution)/shard_map/ppermute | solution.py:28
  99.8 23.4 %collective-permute-start.25 = (f32[1,64,320]{2,1,0:T(8,128)}, f32[1,64,320]{2,1,0:T(8,128)}, u32[]{:S(2)}, u32[]{:S(2)}) collective-permute-start(f32[1,64,320]{2,1,0:T(8,128)} %slice_bitcast_fusion.2), channel_id=1, source_target_pairs={{0,2},{1,3},{2,0},{3,1},{4,6},{5,7},{6,4},{7,5},{8,10},{9,11},{10,... | collective-permute-start | bytes 245768 | tf_op jit(solution)/shard_map/ppermute | solution.py:28
  103.3 34.4 %collective-permute-start.21 = (bf16[64,1280]{1,0:T(8,128)(2,1)}, bf16[64,1280]{1,0:T(8,128)(2,1)}, u32[]{:S(2)}, u32[]{:S(2)}) collective-permute-start(bf16[64,1280]{1,0:T(8,128)(2,1)} %convert_element_type.111), channel_id=1, source_target_pairs={{0,4},{4,0},{8,12},{12,8},{16,20},{20,16},{24,28},{28,24},{1,5},{5... | collective-permute-start | bytes 491528 | tf_op jit(solution)/shard_map/ppermute | solution.py:28
  117.5 36.1 %copy-start.9 = (bf16[64,1280]{1,0:T(8,128)(2,1)S(1)}, bf16[64,1280]{1,0:T(8,128)(2,1)}, u32[]{:S(2)}) copy-start(bf16[64,1280]{1,0:T(8,128)(2,1)} %copy-done.8) | copy-start | bytes 491524
  117.5 60.6 %all-to-all-start = ((bf16[16,336,128]{2,1,0:T(8,128)(2,1)}), bf16[16,336,128]{2,1,0:T(8,128)(2,1)S(1)}, u32[]{:S(2)}, u32[]{:S(2)}) async-start(bf16[16,336,128]{2,1,0:T(8,128)(2,1)} %shard_map.121), calls=%async_computation | async-start | bytes 2752512 | tf_op jit(solution)/shard_map/all_to_all | solution.py:496
  124.1 12.6 %collective-permute-start.26 = (f32[64,320]{1,0:T(8,128)S(1)}, f32[64,320]{1,0:T(8,128)S(1)}, u32[]{:S(2)}, u32[]{:S(2)}) collective-permute-start(f32[64,320]{1,0:T(8,128)S(1)} %fusion.3), channel_id=1, source_target_pairs={{0,4},{4,0},{8,12},{12,8},{16,20},{20,16},{24,28},{28,24},{1,5},{5... | collective-permute-start | bytes 245768 | tf_op jit(solution)/shard_map/ppermute | solution.py:28
  136.7 12.0 %collective-permute-start.27 = (f32[64,320]{1,0:T(8,128)S(1)}, f32[64,320]{1,0:T(8,128)S(1)}, u32[]{:S(2)}, u32[]{:S(2)}) collective-permute-start(f32[64,320]{1,0:T(8,128)S(1)} %add.81), channel_id=1, source_target_pairs={{0,8},{4,12},{8,0},{12,4},{16,24},{20,28},{24,16},{28,20},{1,9},{5... | collective-permute-start | bytes 245768 | tf_op jit(solution)/shard_map/ppermute | solution.py:28
  138.6 22.6 %collective-permute-start.22 = (bf16[64,1280]{1,0:T(8,128)(2,1)S(1)}, bf16[64,1280]{1,0:T(8,128)(2,1)S(1)}, u32[]{:S(2)}, u32[]{:S(2)}) collective-permute-start(bf16[64,1280]{1,0:T(8,128)(2,1)S(1)} %add_convert_fusion.3), channel_id=1, source_target_pairs={{0,8},{4,12},{8,0},{12,4},{16,24},{20,28},{24,16},{28,20},{1,9},{5... | collective-permute-start | bytes 491528 | tf_op jit(solution)/shard_map/ppermute | solution.py:28
  148.7 10.9 %collective-permute-start.28 = (f32[64,320]{1,0:T(8,128)S(1)}, f32[64,320]{1,0:T(8,128)S(1)}, u32[]{:S(2)}, u32[]{:S(2)}) collective-permute-start(f32[64,320]{1,0:T(8,128)S(1)} %add.82), channel_id=1, source_target_pairs={{0,16},{4,20},{8,24},{12,28},{16,0},{20,4},{24,8},{28,12},{1,17},{... | collective-permute-start | bytes 245768 | tf_op jit(solution)/shard_map/ppermute | solution.py:28
  154.1 7.3 %collective-permute-start.12 = (f32[64,64]{1,0:T(8,128)S(1)}, f32[64,64]{1,0:T(8,128)S(1)}, u32[]{:S(2)}, u32[]{:S(2)}) collective-permute-start(f32[64,64]{1,0:T(8,128)S(1)} %fusion.8), channel_id=1, source_target_pairs={{0,1},{1,0},{2,3},{3,2},{4,5},{5,4},{6,7},{7,6},{8,9},{9,8},{10,11... | collective-permute-start | bytes 49160 | tf_op jit(solution)/shard_map/ppermute | solution.py:28
  159.6 10.5 %collective-permute-start.29 = (f32[64,320]{1,0:T(8,128)S(1)}, f32[64,320]{1,0:T(8,128)S(1)}, u32[]{:S(2)}, u32[]{:S(2)}) collective-permute-start(f32[64,320]{1,0:T(8,128)S(1)} %add.83.refs_0_), channel_id=1, source_target_pairs={{0,2},{1,3},{2,0},{3,1},{4,6},{5,7},{6,4},{7,5},{8,10},{9,11},{10,... | collective-permute-start | bytes 245768 | tf_op jit(solution)/shard_map/ppermute | solution.py:28
  161.3 8.9 %collective-permute-start.23 = (bf16[64,1280]{1,0:T(8,128)(2,1)S(1)}, bf16[64,1280]{1,0:T(8,128)(2,1)S(1)}, u32[]{:S(2)}, u32[]{:S(2)}) collective-permute-start(bf16[64,1280]{1,0:T(8,128)(2,1)S(1)} %add_convert_fusion.2), channel_id=1, source_target_pairs={{0,16},{4,20},{8,24},{12,28},{16,0},{20,4},{24,8},{28,12},{1,17},{... | collective-permute-start | bytes 491528 | tf_op jit(solution)/shard_map/ppermute | solution.py:28
  161.4 4.0 %collective-permute-start.13 = (f32[64,64]{1,0:T(8,128)S(1)}, f32[64,64]{1,0:T(8,128)S(1)}, u32[]{:S(2)}, u32[]{:S(2)}) collective-permute-start(f32[64,64]{1,0:T(8,128)S(1)} %add.69), channel_id=1, source_target_pairs={{0,2},{1,3},{2,0},{3,1},{4,6},{5,7},{6,4},{7,5},{8,10},{9,11},{10,... | collective-permute-start | bytes 49160 | tf_op jit(solution)/shard_map/ppermute | solution.py:28
  170.1 4.1 %collective-permute-start.30 = (f32[2,64,320]{2,1,0:T(8,128)S(1)}, f32[2,64,320]{2,1,0:T(8,128)S(1)}, u32[]{:S(2)}, u32[]{:S(2)}) collective-permute-start(f32[2,64,320]{2,1,0:T(8,128)S(1)} %pad_maximum_fusion.3), channel_id=1, source_target_pairs={{0,1},{1,0},{2,3},{3,2},{4,5},{5,4},{6,7},{7,6},{8,9},{9,8},{10,11... | collective-permute-start | bytes 491528 | tf_op jit(solution)/shard_map/ppermute | solution.py:28
